TPU v7x, 256 devices: a whole 4x4x8 slice. The times are simulated.
256 devices in a mesh: rows: 32 (over z, x_hi, core), lev: 8 (over y, x_lo).
Axes of the slice: x: 4 (x_hi: 2, x_lo: 2; x = x_hi * 2 + x_lo), y: 4, z: 8, core: 2. Of those that a mesh axis runs over, the one named last changes fastest.
Arguments:
- field: bfloat16 [2, 8, 512, 64, 1024], P(None, 'lev', 'rows'), may hold values from -6 to 6
- spectral_weight: bfloat16 [3, 64, 64, 64, 64], P(None, None, 'rows'), may hold values from -5 to 5
- local_weight: bfloat16 [64, 64], replicated, may hold values from -0.75 to 0.75
- local_bias: float32 [64], replicated, may hold values from -4 to 4
- gate_weight: bfloat16 [64, 256], replicated, may hold values from -0.75 to 0.75
- up_weight: bfloat16 [64, 256], replicated, may hold values from -0.75 to 0.75
- down_weight: bfloat16 [256, 64], replicated, may hold values from -0.375 to 0.375
Outputs:
- updated: bfloat16 [2, 8, 512, 64, 1024], P(None, 'lev', 'rows')
All inputs are finite; a program needn't handle non-finite values.
Results may differ from a plain program's by a relative error of at most 0.02.
Values may be sent and summed in bfloat16 or wider, within the bound.
A program may use at most 128 MiB of HBM per device.

v0:
```python
import math

import jax
import jax.numpy as jnp
from jax import lax
from jax.sharding import PartitionSpec as P


def extended(cells, sides, width):
    for axis, dim in sides:
        count = lax.axis_size(axis)
        ends = count - 1
        head = lax.slice_in_dim(cells, 0, width, axis=dim)
        tail = lax.slice_in_dim(cells, cells.shape[dim] - width, cells.shape[dim], axis=dim)
        cells = jnp.concatenate(
            [
                lax.ppermute(tail, axis, [(i, (i + 1) % count) for i in range(ends)]),
                cells,
                lax.ppermute(head, axis, [((i + 1) % count, i) for i in range(ends)]),
            ],
            axis=dim,
        )
    return cells


def cas_rows(positions, count, modes):
    freq = jnp.arange(modes, dtype=jnp.int32) - modes // 2
    turns = positions[:, None] * freq[None, :] % count
    angle = 2.0 * math.pi / count * turns.astype(jnp.float32)
    return (jnp.cos(angle) + jnp.sin(angle)) / math.sqrt(count)


def body(field, spectral_weight, local_weight, local_bias, gate_weight, up_weight, down_weight):
    high = lax.Precision.HIGHEST
    batch, levels, lat_rows, chans, lon_cells = field.shape
    ranks = lax.axis_size("rows")
    lat_total = lat_rows * ranks
    lat_modes = spectral_weight.shape[1]
    lon_modes = spectral_weight.shape[2] * ranks
    lon_table = cas_rows(jnp.arange(lon_cells, dtype=jnp.int32), lon_cells, lon_modes).astype(
        jnp.bfloat16
    )
    own_rows = lax.axis_index("rows") * lat_rows + jnp.arange(lat_rows, dtype=jnp.int32)
    along = jnp.dot(field.reshape(-1, lon_cells), lon_table, preferred_element_type=jnp.float32)
    along = along.reshape(batch, levels, lat_rows, chans, lon_modes)
    own_table = cas_rows(own_rows, lat_total, lat_modes)
    partial_modes = jnp.einsum("nk,blncm->blkcm", own_table, along, precision=high)
    modes = lax.psum_scatter(
        partial_modes.astype(jnp.bfloat16), "rows", scatter_dimension=4, tiled=True
    )
    padded = extended(modes, (("lev", 1),), 1)
    mixed = jnp.einsum(
        "kmco,blkcm->blkom",
        spectral_weight[0],
        padded[:, 0:levels],
        preferred_element_type=jnp.float32,
    )
    mixed = mixed + jnp.einsum(
        "kmco,blkcm->blkom",
        spectral_weight[1],
        padded[:, 1 : levels + 1],
        preferred_element_type=jnp.float32,
    )
    mixed = mixed + jnp.einsum(
        "kmco,blkcm->blkom",
        spectral_weight[2],
        padded[:, 2 : levels + 2],
        preferred_element_type=jnp.float32,
    )
    mixed_b = mixed.astype(jnp.bfloat16)
    own_inverse = cas_rows(own_rows, lat_total, lat_modes)
    values = jnp.einsum(
        "nk,blkom->blnom",
        own_inverse,
        lax.all_gather(mixed_b, "rows", axis=4, tiled=True).astype(jnp.float32),
        precision=high,
    )
    back_b = values.astype(jnp.bfloat16)

    def finish(pair):
        grid, coarse = pair
        spectral = jnp.dot(
            coarse.reshape(-1, lon_modes), lon_table.T, preferred_element_type=jnp.float32
        )
        spectral = spectral.reshape(lat_rows, chans, lon_cells)
        local = jnp.einsum("co,ncx->nox", local_weight, grid, preferred_element_type=jnp.float32)
        value = spectral + local + local_bias[None, :, None]
        act = jax.nn.gelu(value, approximate=False).astype(jnp.bfloat16)
        gate = jnp.einsum("ch,ncx->nhx", gate_weight, act, preferred_element_type=jnp.float32)
        upper = jnp.einsum("ch,ncx->nhx", up_weight, act, preferred_element_type=jnp.float32)
        hidden = (jax.nn.silu(gate) * upper).astype(jnp.bfloat16)
        down = jnp.einsum("hc,nhx->ncx", down_weight, hidden, preferred_element_type=jnp.float32)
        return (grid.astype(jnp.float32) + down).astype(jnp.bfloat16)

    result = lax.map(
        finish,
        (
            field.reshape(batch * levels, lat_rows, chans, lon_cells),
            back_b.reshape(batch * levels, lat_rows, chans, lon_modes),
        ),
    )
    return result.reshape(batch, levels, lat_rows, chans, lon_cells)


def solution(mesh):
    return jax.shard_map(
        body,
        mesh=mesh,
        in_specs=(
            P(None, "lev", "rows", None, None),
            P(None, None, "rows", None, None),
            P(),
            P(),
            P(),
            P(),
            P(),
        ),
        out_specs=P(None, "lev", "rows", None, None),
        check_vma=False,
    )
```

profile of v0, /device:TPU:25, one launch (start us, length us, event | category | flops | bytes accessed | tf_op | source)
XLA Modules:
  0.0 305.2 jit_solution(10441724947035010969)
XLA Ops:
  6.5 5.4 %convolution_bitcast_fusion = f32[2048,64]{0,1:T(8,128)S(1)} fusion(bf16[2048,1024]{1,0:T(8,128)(2,1)} %bitcast.154, s32[64]{0:T(128)S(1)} %iota_add_fusion.1), kind=kOutput, calls=%fused_computation.70 | convolution fusion | flops 269549568 | bytes 4718848 | tf_op jit(solution)/shard_map/dot_general | solution.py:44
  12.0 0.4 reshape.55
  12.4 0.9 copy.17
  13.3 7.0 %convert_bitcast_fusion = bf16[2,1,64,64,64]{2,4,3,0,1:T(8,128)(2,1)S(1)} fusion(f32[2,16,64,64]{3,1,2,0:T(8,128)S(1)} %copy.17, s32[64]{0:T(128)S(1)} %iota_add_fusion.1, s32[16]{0:T(128)S(1)} %iota_add_fusion), kind=kOutput, calls=%fused_computation.80 | convolution fusion | flops 101203968 | bytes 1573184 | tf_op jit(solution)/shard_map/nk,blncm->blkcm/dot_general | solution.py:47
  20.3 2.9 copy.18
  23.2 0.0 reduce-scatter.2.cloned.1.call-update
  23.3 0.0 all-gather.2.cloned.1.call-start
  23.3 117.0 %reduce-scatter.2.cloned.1.call-done = bf16[2,1,64,64,2]{3,2,1,0,4:T(8,128)(2,1)} async-done(((bf16[2,1,64,64,64]{3,2,1,0,4:T(8,128)(2,1)}), bf16[2,1,64,64,2]{3,2,1,0,4:T(8,128)(2,1)}) %reduce-scatter.2.cloned.1.call-update) | async-done | bytes 32784 | tf_op jit(solution)/shard_map/reduce_scatter | solution.py:48
  140.3 0.9 copy.19
  141.2 2.5 collective-permute-start.1
  143.7 2.8 collective-permute-start
  146.5 2.3 fusion.53
  148.8 2.2 fusion.51
  151.1 2.9 fusion.70
  154.0 0.0 all-gather.2.cloned.1.call-update
  154.0 0.1 copy.24
  154.1 69.6 %all-gather.2.cloned.1.call-done = bf16[2,1,64,64,64]{3,0,4,2,1:T(2,128)(2,1)} async-done(((bf16[2,1,64,64,2]{3,0,4,2,1:T(2,128)(2,1)}), bf16[2,1,64,64,64]{3,0,4,2,1:T(2,128)(2,1)}) %all-gather.2.cloned.1.call-update) | async-done | bytes 1048592 | tf_op jit(solution)/shard_map/all_gather | solution.py:75
  223.7 5.3 %copy.22 = bf16[2,64,64,64]{3,1,2,0:T(8,128)(2,1)S(1)} copy(bf16[2,64,64,64]{2,0,3,1:T(2,128)(2,1)} %bitcast.156) | data formatting | bytes 2097152 | tf_op jit(solution)/shard_map/reshape.16
  229.0 1.1 fusion.60
  230.1 68.3 %while.11 = (s32[]{:T(128)}, bf16[2,16,64,1024]{3,2,1,0:T(8,128)(2,1)}, bf16[2,16,64,1024]{3,2,1,0:T(8,128)(2,1)}, bf16[2,16,64,64]{3,1,2,0:T(8,128)(2,1)S(1)}, ...) while((s32[]{:T(128)}, ...), condition=%wide.region_2.3_spmd.clone, body=%wide.region_1.2_spmd.clone.sunk | while | flops 1989148672 | bytes 80463248 | solution.py:95
  230.3 1.8 fusion.130
  232.1 0.4 copy-done
  232.5 1.7 fusion.131
  234.1 9.2 %fusion.132 = bf16[16,64,1024]{2,1,0:T(8,128)(2,1)S(1)} fusion(f32[16,64,1024]{2,1,0:T(8,128)S(1)} %get-tuple-element.186, u16[64,1024]{1,0:T(8,128)(2,1)S(1)} %get-tuple-element.187), kind=kLoop, calls=%fused_computation.11.clone.1 | loop fusion | flops 71303168 | bytes 6422528 | tf_op jit(solution)/shard_map/while/body/eval_jaxpr/convert_element_type | solution.py:88
  243.4 8.1 %fusion.133 = f32[16,1024,256]{2,1,0:T(8,128)} fusion(bf16[16,64,1024]{2,1,0:T(8,128)(2,1)S(1)} %fusion.132, bf16[64,256]{1,0:T(8,128)(2,1)S(1)} %get-tuple-element.217), kind=kOutput, calls=%fused_computation.58.clone.1 | convolution fusion | flops 536870912 | bytes 18907136 | tf_op jit(solution)/shard_map/while/body/eval_jaxpr/ch,ncx->nhx/dot_general | solution.py:90
  251.5 12.8 %fusion.134 = bf16[2,16,64,1024]{3,2,1,0:T(8,128)(2,1)} fusion(bf16[2,16,64,1024]{3,2,1,0:T(8,128)(2,1)} %get-tuple-element.200, s32[]{:T(128)} %get-tuple-element.199, bf16[2,16,64,1024]{3,2,1,0:T(8,128)(2,1)} %get-tuple-element.212, f32[16,1024,256]{2,1,0:T(8,128)} %fusion.133, bf16[16,64,1024]{2,1,0:T(8,128)(2,1)S(1)} %fusion.132, ...), kind=kOutput, calls=%fused_computation.34.clone.1 | convolution fusion | flops 1102053376 | bytes 23134720 | tf_op jit(solution)/shard_map/while/body/eval_jaxpr/hc,nhx->ncx/dot_general | solution.py:92
  264.4 1.8 fusion.130
  266.1 0.4 copy-done
  266.5 1.7 fusion.131
  268.2 9.2 %fusion.132 = bf16[16,64,1024]{2,1,0:T(8,128)(2,1)S(1)} fusion(f32[16,64,1024]{2,1,0:T(8,128)S(1)} %get-tuple-element.186, u16[64,1024]{1,0:T(8,128)(2,1)S(1)} %get-tuple-element.187), kind=kLoop, calls=%fused_computation.11.clone.1 | loop fusion | flops 71303168 | bytes 6422528 | tf_op jit(solution)/shard_map/while/body/eval_jaxpr/convert_element_type | solution.py:88
  277.4 8.1 %fusion.133 = f32[16,1024,256]{2,1,0:T(8,128)} fusion(bf16[16,64,1024]{2,1,0:T(8,128)(2,1)S(1)} %fusion.132, bf16[64,256]{1,0:T(8,128)(2,1)S(1)} %get-tuple-element.217), kind=kOutput, calls=%fused_computation.58.clone.1 | convolution fusion | flops 536870912 | bytes 18907136 | tf_op jit(solution)/shard_map/while/body/eval_jaxpr/ch,ncx->nhx/dot_general | solution.py:90
  285.6 12.8 %fusion.134 = bf16[2,16,64,1024]{3,2,1,0:T(8,128)(2,1)} fusion(bf16[2,16,64,1024]{3,2,1,0:T(8,128)(2,1)} %get-tuple-element.200, s32[]{:T(128)} %get-tuple-element.199, bf16[2,16,64,1024]{3,2,1,0:T(8,128)(2,1)} %get-tuple-element.212, f32[16,1024,256]{2,1,0:T(8,128)} %fusion.133, bf16[16,64,1024]{2,1,0:T(8,128)(2,1)S(1)} %fusion.132, ...), kind=kOutput, calls=%fused_computation.34.clone.1 | convolution fusion | flops 1102053376 | bytes 23134720 | tf_op jit(solution)/shard_map/while/body/eval_jaxpr/hc,nhx->ncx/dot_general | solution.py:92
  (20 shorter events, 0.1 us)
Async XLA Ops:
  6.5 133.8 %reduce-scatter.2.cloned.1.call-start = ((), (), s32[]{:S(2)}) async-start(), calls=%async_computation.1 | async-start | bytes 2162688 | tf_op jit(solution)/shard_map/reduce_scatter | solution.py:48
  23.3 130.8 %copy-start.2 = (bf16[64,64]{1,0:T(8,128)(2,1)S(1)}, bf16[64,64]{1,0:T(8,128)(2,1)}, u32[]{:S(2)}) copy-start(bf16[64,64]{1,0:T(8,128)(2,1)} %param.11) | copy-start | bytes 24580
  23.3 200.5 %all-gather.2.cloned.1.call-start = ((), (), s32[]{:S(2)}) async-start(), calls=%async_computation.2 | async-start | bytes 2162688 | tf_op jit(solution)/shard_map/all_gather | solution.py:75
  141.2 7.6 %collective-permute-start.1 = (bf16[2,1,64,64,2]{3,0,4,2,1:T(2,128)(2,1)S(1)}, bf16[2,1,64,64,2]{3,0,4,2,1:T(2,128)(2,1)S(1)}, u32[]{:S(2)}, u32[]{:S(2)}) collective-permute-start(bf16[2,1,64,64,2]{3,0,4,2,1:T(2,128)(2,1)S(1)} %copy.19), channel_id=1, source_target_pairs={{1,0},{2,1},{3,2},{4,3},{5,4},{6,5},{7,6},{9,8},{10,9},{11,10},{12... | collective-permute-start | bytes 98312 | tf_op jit(solution)/shard_map/ppermute | solution.py:19
  143.7 7.4 %collective-permute-start = (bf16[2,1,64,64,2]{3,0,4,2,1:T(2,128)(2,1)S(1)}, bf16[2,1,64,64,2]{3,0,4,2,1:T(2,128)(2,1)S(1)}, u32[]{:S(2)}, u32[]{:S(2)}) collective-permute-start(bf16[2,1,64,64,2]{3,0,4,2,1:T(2,128)(2,1)S(1)} %copy.19), channel_id=1, source_target_pairs={{0,1},{1,2},{2,3},{3,4},{4,5},{5,6},{6,7},{8,9},{9,10},{10,11},{11... | collective-permute-start | bytes 98312 | tf_op jit(solution)/shard_map/ppermute | solution.py:17
  151.0 79.0 %copy-start.1 = (bf16[64,256]{1,0:T(8,128)(2,1)S(1)}, bf16[64,256]{1,0:T(8,128)(2,1)}, u32[]{:S(2)}) copy-start(bf16[64,256]{1,0:T(8,128)(2,1)} %param.14) | copy-start | bytes 98308
  151.0 79.0 %copy-start.3 = (f32[64]{0:T(128)S(1)}, f32[64]{0:T(128)}, u32[]{:S(2)}) copy-start(f32[64]{0:T(128)} %param.12) | copy-start | bytes 772
  151.0 79.0 %copy-start.4 = (bf16[64,256]{1,0:T(8,128)(2,1)S(1)}, bf16[64,256]{1,0:T(8,128)(2,1)}, u32[]{:S(2)}) copy-start(bf16[64,256]{1,0:T(8,128)(2,1)} %param.13) | copy-start | bytes 98308
  151.0 79.0 %copy-start.5 = (bf16[256,64]{0,1:T(8,128)(2,1)S(1)}, bf16[256,64]{0,1:T(8,128)(2,1)}, u32[]{:S(2)}) copy-start(bf16[256,64]{0,1:T(8,128)(2,1)} %param.15) | copy-start | bytes 98308
  230.3 2.2 copy-start
  264.3 2.2 copy-start
Sparse Core Ops, SparseCore 0:
  23.4 116.8 reduce-scatter.1
  154.1 69.5 all-gather.1
where the time goes:
time: 307 us; the launch traced here: 305 us
  waiting for transfers between devices  187 us (61%)
  matrix products  69.7 us (23%)
  other arithmetic  18.5 us (6%)
  between operations  13.6 us (4%)
  local copies, waits for them, and re-layouts  11.3 us (4%)
  starting transfers between devices  5.32 us (2%)
    reduce_scatter x1, waiting for transfers between devices, body(): lax.psum_scatter(partial_modes.astype(jnp.bfloat16), 'rows', scatter_dime...  117 us
    all_gather x1, waiting for transfers between devices, body(): lax.all_gather(mixed_b, 'rows', axis=4, tiled=True).astype(jnp.float32)  69.6 us
    dot_general x2, matrix products, finish(): jnp.einsum('hc,nhx->ncx', down_weight, hidden, preferred_element_type=jnp...  25.6 us
    convert_element_type x2, other arithmetic, finish(): act = jax.nn.gelu(value, approximate=False).astype(jnp.bfloat16)  18.5 us
    dot_general x2, matrix products, finish(): jnp.einsum('ch,ncx->nhx', up_weight, act, preferred_element_type=jnp.floa...  16.3 us
    dot_general x1, matrix products, body(): jnp.einsum('nk,blncm->blkcm', own_table, along, precision=high)  6.98 us
    another operation x3, local copies, waits for them, and re-layouts  6.57 us
  transfers between devices with their start and end apart: 4, of which 2 were waited for; matrix products, arithmetic and copies ran while one was open for 2% of the time, Pallas kernels for 0%

commit v1 on v0

--- a/solution.py
+++ b/solution.py
@@ -41,38 +41,37 @@
         jnp.bfloat16
     )
     own_rows = lax.axis_index("rows") * lat_rows + jnp.arange(lat_rows, dtype=jnp.int32)
-    along = jnp.dot(field.reshape(-1, lon_cells), lon_table, preferred_element_type=jnp.float32)
-    along = along.reshape(batch, levels, lat_rows, chans, lon_modes)
     own_table = cas_rows(own_rows, lat_total, lat_modes)
-    partial_modes = jnp.einsum("nk,blncm->blkcm", own_table, along, precision=high)
+    along = jnp.einsum("xm,blncx->mblnc", lon_table, field, preferred_element_type=jnp.float32)
+    partial_modes = jnp.einsum("nk,mblnc->mblkc", own_table, along, precision=high)
     modes = lax.psum_scatter(
-        partial_modes.astype(jnp.bfloat16), "rows", scatter_dimension=4, tiled=True
+        partial_modes.astype(jnp.bfloat16), "rows", scatter_dimension=0, tiled=True
     )
-    padded = extended(modes, (("lev", 1),), 1)
+    padded = extended(modes, (("lev", 2),), 1)
     mixed = jnp.einsum(
-        "kmco,blkcm->blkom",
+        "kjco,jblkc->jblko",
         spectral_weight[0],
-        padded[:, 0:levels],
+        padded[:, :, 0:levels],
         preferred_element_type=jnp.float32,
     )
     mixed = mixed + jnp.einsum(
-        "kmco,blkcm->blkom",
+        "kjco,jblkc->jblko",
         spectral_weight[1],
-        padded[:, 1 : levels + 1],
+        padded[:, :, 1 : levels + 1],
         preferred_element_type=jnp.float32,
     )
     mixed = mixed + jnp.einsum(
-        "kmco,blkcm->blkom",
+        "kjco,jblkc->jblko",
         spectral_weight[2],
-        padded[:, 2 : levels + 2],
+        padded[:, :, 2 : levels + 2],
         preferred_element_type=jnp.float32,
     )
     mixed_b = mixed.astype(jnp.bfloat16)
-    own_inverse = cas_rows(own_rows, lat_total, lat_modes)
+    gathered = lax.all_gather(mixed_b, "rows", axis=0, tiled=True)
     values = jnp.einsum(
-        "nk,blkom->blnom",
-        own_inverse,
-        lax.all_gather(mixed_b, "rows", axis=4, tiled=True).astype(jnp.float32),
+        "nk,mblko->blnom",
+        own_table,
+        gathered.astype(jnp.float32),
         precision=high,
     )
     back_b = values.astype(jnp.bfloat16)

time: 307 us -> 317 us (1.033)
  waiting for transfers between devices: 187 us -> 196 us
    all_gather x1, waiting for transfers between devices: 69.6 us -> 85.9 us  [body(): gathered = lax.all_gather(mixed_b, 'rows', axis=0, tiled=True)]
    reduce_scatter x1, waiting for transfers between devices: 117 us -> 110 us  [body(): lax.psum_scatter(partial_modes.astype(jnp.bfloat16), 'rows', scatter_dime...]
    slice x0 -> x1, local copies, waits for them, and re-layouts: none -> 7.28 us  [body(): spectral_weight[0]]
    another operation x3, local copies, waits for them, and re-layouts: 6.57 us -> 1.14 us
  transfers between devices with their start and end apart: 4 -> 4, of which waited for: 2 -> 3; matrix products, arithmetic and copies ran while one was open for 2% -> 3% of each run, Pallas kernels for 0% -> 0%
where the time goes in v1:
time: 317 us; the launch traced here: 315 us
  waiting for transfers between devices  196 us (62%)
  matrix products  70.7 us (22%)
  other arithmetic  18.5 us (6%)
  between operations  13.5 us (4%)
  local copies, waits for them, and re-layouts  10.7 us (3%)
  starting transfers between devices  5.32 us (2%)
    reduce_scatter x1, waiting for transfers between devices, body(): lax.psum_scatter(partial_modes.astype(jnp.bfloat16), 'rows', scatter_dime...  110 us
    all_gather x1, waiting for transfers between devices, body(): gathered = lax.all_gather(mixed_b, 'rows', axis=0, tiled=True)  85.9 us
    dot_general x2, matrix products, finish(): jnp.einsum('hc,nhx->ncx', down_weight, hidden, preferred_element_type=jnp...  25.6 us
    convert_element_type x2, other arithmetic, finish(): act = jax.nn.gelu(value, approximate=False).astype(jnp.bfloat16)  18.5 us
    dot_general x2, matrix products, finish(): jnp.einsum('ch,ncx->nhx', up_weight, act, preferred_element_type=jnp.floa...  16.2 us
    dot_general x1, matrix products, body(): jnp.einsum('nk,mblnc->mblkc', own_table, along, precision=high)  8.03 us
    slice x1, local copies, waits for them, and re-layouts, body(): spectral_weight[0]  7.28 us
  transfers between devices with their start and end apart: 4, of which 3 were waited for; matrix products, arithmetic and copies ran while one was open for 3% of the time, Pallas kernels for 0%

profile of v1, /device:TPU:25, one launch (start us, length us, event | category | flops | bytes accessed | tf_op | source)
XLA Modules:
  0.0 315.2 jit_solution(1026973673076233008)
XLA Ops:
  6.5 6.2 %fusion.75 = f32[64,2,16,64]{3,0,2,1:T(8,128)S(1)} fusion(s32[64]{0:T(128)S(1)} %iota_add_fusion.1, bf16[2,1,16,64,1024]{4,3,2,1,0:T(8,128)(2,1)} %param.9), kind=kOutput, calls=%fused_computation.97 | convolution fusion | flops 269549568 | bytes 4718848 | tf_op jit(solution)/shard_map/xm,blncx->mblnc/dot_general | solution.py:45
  12.8 8.0 %convert_bitcast_fusion = bf16[64,2,1,64,64]{3,4,1,0,2:T(8,128)(2,1)} fusion(f32[64,2,16,64]{3,0,2,1:T(8,128)S(1)} %fusion.75, s32[64]{0:T(128)S(1)} %iota_add_fusion.1, s32[16]{0:T(128)S(1)} %iota_add_fusion), kind=kOutput, calls=%fused_computation.78 | convolution fusion | flops 101203968 | bytes 1573184 | tf_op jit(solution)/shard_map/nk,mblnc->mblkc/dot_general | solution.py:46
  20.9 7.3 %fusion.104 = (bf16[1,64,2,64,64]{4,3,2,1,0:T(8,128)(2,1)}, bf16[1,64,2,64,64]{4,3,2,1,0:T(8,128)(2,1)}, bf16[1,64,2,64,64]{4,3,2,1,0:T(8,128)(2,1)S(1)}) fusion(bf16[3,64,2,64,64]{4,3,2,1,0:T(8,128)(2,1)} %param.10), kind=kLoop, calls=%fused_computation.133 | loop fusion | bytes 6291456 | tf_op jit(solution)/shard_map/slice | solution.py:53
  28.2 109.6 %reduce-scatter.2.cloned.1.call-done = bf16[2,2,1,64,64]{3,4,1,0,2:T(8,128)(2,1)} async-done(((bf16[64,2,1,64,64]{3,4,1,0,2:T(8,128)(2,1)}), bf16[2,2,1,64,64]{3,4,1,0,2:T(8,128)(2,1)}) %reduce-scatter.2.cloned.1.call-update) | async-done | bytes 32784 | tf_op jit(solution)/shard_map/reduce_scatter | solution.py:47
  137.8 0.9 copy.22
  138.8 2.2 collective-permute-start.1
  141.0 3.0 collective-permute-start
  144.1 2.2 fusion.53
  146.3 0.1 copy.24
  146.4 0.7 collective-permute-done
  147.1 0.1 copy.20
  147.2 0.7 fusion.52
  147.9 2.2 fusion.66
  150.1 0.6 copy.25
  150.8 0.1 copy.27
  150.9 85.9 %all-gather.2.cloned.1.call-done = bf16[64,2,1,64,64]{4,3,2,1,0:T(8,128)(2,1)} async-done(((bf16[2,2,1,64,64]{4,3,2,1,0:T(8,128)(2,1)}), bf16[64,2,1,64,64]{4,3,2,1,0:T(8,128)(2,1)}) %all-gather.2.cloned.1.call-update) | async-done | bytes 1048592 | tf_op jit(solution)/shard_map/all_gather | solution.py:70
  236.8 2.6 fusion.60
  239.5 68.9 %while.11 = (s32[]{:T(128)}, bf16[2,16,64,1024]{3,2,1,0:T(8,128)(2,1)}, bf16[2,16,64,1024]{3,2,1,0:T(8,128)(2,1)}, bf16[2,16,64,64]{2,1,0,3:T(8,128)(2,1)S(1)}, ...) while((s32[]{:T(128)}, ...), condition=%wide.region_2.3_spmd.clone, body=%wide.region_1.2_spmd.clone.sunk | while | flops 1989148672 | bytes 80725392 | solution.py:94
  239.7 0.3 copy.53
  240.0 1.7 fusion.129
  241.7 0.4 copy-done
  242.2 1.7 fusion.130
  243.8 9.2 %fusion.131 = bf16[16,64,1024]{2,1,0:T(8,128)(2,1)S(1)} fusion(f32[16,64,1024]{2,1,0:T(8,128)S(1)} %get-tuple-element.189, u16[64,1024]{1,0:T(8,128)(2,1)S(1)} %get-tuple-element.190), kind=kLoop, calls=%fused_computation.11.clone.1 | loop fusion | flops 71303168 | bytes 6422528 | tf_op jit(solution)/shard_map/while/body/eval_jaxpr/convert_element_type | solution.py:87
  253.1 8.1 %fusion.132 = f32[16,1024,256]{2,1,0:T(8,128)} fusion(bf16[16,64,1024]{2,1,0:T(8,128)(2,1)S(1)} %fusion.131, bf16[64,256]{1,0:T(8,128)(2,1)S(1)} %get-tuple-element.220), kind=kOutput, calls=%fused_computation.58.clone.1 | convolution fusion | flops 536870912 | bytes 18907136 | tf_op jit(solution)/shard_map/while/body/eval_jaxpr/ch,ncx->nhx/dot_general | solution.py:89
  261.2 12.8 %fusion.133 = bf16[2,16,64,1024]{3,2,1,0:T(8,128)(2,1)} fusion(bf16[2,16,64,1024]{3,2,1,0:T(8,128)(2,1)} %get-tuple-element.203, s32[]{:T(128)} %get-tuple-element.202, bf16[2,16,64,1024]{3,2,1,0:T(8,128)(2,1)} %get-tuple-element.215, f32[16,1024,256]{2,1,0:T(8,128)} %fusion.132, bf16[16,64,1024]{2,1,0:T(8,128)(2,1)S(1)} %fusion.131, ...), kind=kOutput, calls=%fused_computation.34.clone.1 | convolution fusion | flops 1102053376 | bytes 23134720 | tf_op jit(solution)/shard_map/while/body/eval_jaxpr/hc,nhx->ncx/dot_general | solution.py:91
  274.0 0.3 copy.53
  274.3 1.7 fusion.129
  276.1 0.4 copy-done
  276.5 1.7 fusion.130
  278.2 9.2 %fusion.131 = bf16[16,64,1024]{2,1,0:T(8,128)(2,1)S(1)} fusion(f32[16,64,1024]{2,1,0:T(8,128)S(1)} %get-tuple-element.189, u16[64,1024]{1,0:T(8,128)(2,1)S(1)} %get-tuple-element.190), kind=kLoop, calls=%fused_computation.11.clone.1 | loop fusion | flops 71303168 | bytes 6422528 | tf_op jit(solution)/shard_map/while/body/eval_jaxpr/convert_element_type | solution.py:87
  287.4 8.1 %fusion.132 = f32[16,1024,256]{2,1,0:T(8,128)} fusion(bf16[16,64,1024]{2,1,0:T(8,128)(2,1)S(1)} %fusion.131, bf16[64,256]{1,0:T(8,128)(2,1)S(1)} %get-tuple-element.220), kind=kOutput, calls=%fused_computation.58.clone.1 | convolution fusion | flops 536870912 | bytes 18907136 | tf_op jit(solution)/shard_map/while/body/eval_jaxpr/ch,ncx->nhx/dot_general | solution.py:89
  295.6 12.8 %fusion.133 = bf16[2,16,64,1024]{3,2,1,0:T(8,128)(2,1)} fusion(bf16[2,16,64,1024]{3,2,1,0:T(8,128)(2,1)} %get-tuple-element.203, s32[]{:T(128)} %get-tuple-element.202, bf16[2,16,64,1024]{3,2,1,0:T(8,128)(2,1)} %get-tuple-element.215, f32[16,1024,256]{2,1,0:T(8,128)} %fusion.132, bf16[16,64,1024]{2,1,0:T(8,128)(2,1)S(1)} %fusion.131, ...), kind=kOutput, calls=%fused_computation.34.clone.1 | convolution fusion | flops 1102053376 | bytes 23134720 | tf_op jit(solution)/shard_map/while/body/eval_jaxpr/hc,nhx->ncx/dot_general | solution.py:91
  (22 shorter events, 0.2 us)
Async XLA Ops:
  6.5 131.3 %reduce-scatter.2.cloned.1.call-start = ((), (), s32[]{:S(2)}) async-start(), calls=%async_computation.1 | async-start | bytes 2162688 | tf_op jit(solution)/shard_map/reduce_scatter | solution.py:47
  20.8 215.9 %all-gather.2.cloned.1.call-start = ((), (), s32[]{:S(2)}) async-start(), calls=%async_computation.2 | async-start | bytes 2162688 | tf_op jit(solution)/shard_map/all_gather | solution.py:70
  28.2 122.6 %copy-start.2 = (bf16[64,64]{1,0:T(8,128)(2,1)S(1)}, bf16[64,64]{1,0:T(8,128)(2,1)}, u32[]{:S(2)}) copy-start(bf16[64,64]{1,0:T(8,128)(2,1)} %param.11) | copy-start | bytes 24580
  138.8 7.6 %collective-permute-start.1 = (bf16[2,2,1,64,64]{3,4,1,0,2:T(8,128)(2,1)}, bf16[2,2,1,64,64]{3,4,1,0,2:T(8,128)(2,1)S(1)}, u32[]{:S(2)}, u32[]{:S(2)}) collective-permute-start(bf16[2,2,1,64,64]{3,4,1,0,2:T(8,128)(2,1)} %reduce-scatter.2.cloned.1.call-done), channel_id=1, source_target_pairs={{1,0},{2,1},{3,2},{4,3},{5,4},{6,5},{7,6},{9,8},{10,9},{11,10},{12... | collective-permute-start | bytes 98312 | tf_op jit(solution)/shard_map/ppermute | solution.py:19
  141.0 6.1 %collective-permute-start = (bf16[2,2,1,64,64]{3,4,1,0,2:T(8,128)(2,1)}, bf16[2,2,1,64,64]{3,4,1,0,2:T(8,128)(2,1)S(1)}, u32[]{:S(2)}, u32[]{:S(2)}) collective-permute-start(bf16[2,2,1,64,64]{3,4,1,0,2:T(8,128)(2,1)} %reduce-scatter.2.cloned.1.call-done), channel_id=1, source_target_pairs={{0,1},{1,2},{2,3},{3,4},{4,5},{5,6},{6,7},{8,9},{9,10},{10,11},{11... | collective-permute-start | bytes 98312 | tf_op jit(solution)/shard_map/ppermute | solution.py:17
  146.3 93.1 %copy-start.1 = (bf16[64,256]{1,0:T(8,128)(2,1)S(1)}, bf16[64,256]{1,0:T(8,128)(2,1)}, u32[]{:S(2)}) copy-start(bf16[64,256]{1,0:T(8,128)(2,1)} %param.14) | copy-start | bytes 98308
  146.3 93.1 %copy-start.3 = (f32[64]{0:T(128)S(1)}, f32[64]{0:T(128)}, u32[]{:S(2)}) copy-start(f32[64]{0:T(128)} %param.12) | copy-start | bytes 772
  146.3 93.1 %copy-start.4 = (bf16[64,256]{1,0:T(8,128)(2,1)S(1)}, bf16[64,256]{1,0:T(8,128)(2,1)}, u32[]{:S(2)}) copy-start(bf16[64,256]{1,0:T(8,128)(2,1)} %param.13) | copy-start | bytes 98308
  146.3 93.1 %copy-start.5 = (bf16[256,64]{0,1:T(8,128)(2,1)S(1)}, bf16[256,64]{0,1:T(8,128)(2,1)}, u32[]{:S(2)}) copy-start(bf16[256,64]{0,1:T(8,128)(2,1)} %param.15) | copy-start | bytes 98308
  240.0 2.2 copy-start
  274.3 2.2 copy-start
Sparse Core Ops, SparseCore 0:
  21.0 116.8 reduce-scatter.1
  150.9 85.8 all-gather.1

commit v2 on v1

--- a/solution.py
+++ b/solution.py
@@ -44,9 +44,10 @@
     own_table = cas_rows(own_rows, lat_total, lat_modes)
     along = jnp.einsum("xm,blncx->mblnc", lon_table, field, preferred_element_type=jnp.float32)
     partial_modes = jnp.einsum("nk,mblnc->mblkc", own_table, along, precision=high)
-    modes = lax.psum_scatter(
-        partial_modes.astype(jnp.bfloat16), "rows", scatter_dimension=0, tiled=True
-    )
+    per = lon_modes // ranks
+    pieces = partial_modes.astype(jnp.bfloat16).reshape((ranks, per) + partial_modes.shape[1:])
+    pieces = lax.all_to_all(pieces, "rows", 0, 0, tiled=True)
+    modes = pieces.astype(jnp.float32).sum(0).astype(jnp.bfloat16)
     padded = extended(modes, (("lev", 2),), 1)
     mixed = jnp.einsum(
         "kjco,jblkc->jblko",
@@ -67,7 +68,10 @@
         preferred_element_type=jnp.float32,
     )
     mixed_b = mixed.astype(jnp.bfloat16)
-    gathered = lax.all_gather(mixed_b, "rows", axis=0, tiled=True)
+    copies = jnp.broadcast_to(mixed_b[None], (ranks,) + mixed_b.shape)
+    gathered = lax.all_to_all(copies, "rows", 0, 0, tiled=True).reshape(
+        (lon_modes,) + mixed_b.shape[1:]
+    )
     values = jnp.einsum(
         "nk,mblko->blnom",
         own_table,

time: 317 us -> 179 us (0.56)
  waiting for transfers between devices: 196 us -> 49.2 us
  starting transfers between devices: 5.32 us -> 23.8 us
  between operations: 13.5 us -> 0.17 us
  local copies, waits for them, and re-layouts: 10.7 us -> 16.4 us
    reduce_scatter x1 -> x0, waiting for transfers between devices: 110 us -> none  [body(): lax.psum_scatter(partial_modes.astype(jnp.bfloat16), 'rows', scatter_dime...]
    all_gather x1 -> x0, waiting for transfers between devices: 85.9 us -> none  [body(): gathered = lax.all_gather(mixed_b, 'rows', axis=0, tiled=True)]
    all_to_all x0 -> x2, waiting for transfers between devices: none -> 49.2 us  [the longest x1 28 us: body(): lax.all_to_all(copies, 'rows', 0, 0, tiled=True)]
    all_to_all x0 -> x2, starting transfers between devices: none -> 18.2 us  [the longest x1 11.8 us: body(): pieces = lax.all_to_all(pieces, 'rows', 0, 0, tiled=True)]
    unnamed x11 -> x18, local copies, waits for them, and re-layouts: 0.11 us -> 7.78 us
  transfers between devices with their start and end apart: 4 -> 4, of which waited for: 3 -> 2; matrix products, arithmetic and copies ran while one was open for 3% -> 7% of each run, Pallas kernels for 0% -> 0%
where the time goes in v2:
time: 179 us; the launch traced here: 177 us
  matrix products  68.2 us (38%)
  waiting for transfers between devices  49.2 us (27%)
  starting transfers between devices  23.8 us (13%)
  other arithmetic  18.9 us (11%)
  local copies, waits for them, and re-layouts  16.4 us (9%)
    all_to_all x1, waiting for transfers between devices, body(): lax.all_to_all(copies, 'rows', 0, 0, tiled=True)  28 us
    dot_general x2, matrix products, finish(): jnp.einsum('hc,nhx->ncx', down_weight, hidden, preferred_element_type=jnp...  25.6 us
    all_to_all x1, waiting for transfers between devices, body(): pieces = lax.all_to_all(pieces, 'rows', 0, 0, tiled=True)  21.2 us
    convert_element_type x2, other arithmetic, finish(): act = jax.nn.gelu(value, approximate=False).astype(jnp.bfloat16)  18.5 us
    dot_general x2, matrix products, finish(): jnp.einsum('ch,ncx->nhx', up_weight, act, preferred_element_type=jnp.floa...  16.3 us
    all_to_all x1, starting transfers between devices, body(): pieces = lax.all_to_all(pieces, 'rows', 0, 0, tiled=True)  11.8 us
    unnamed x18, local copies, waits for them, and re-layouts  7.78 us
    dot_general x1, matrix products, body(): jnp.einsum('nk,mblnc->mblkc', own_table, along, precision=high)  7.06 us
  transfers between devices with their start and end apart: 4, of which 2 were waited for; matrix products, arithmetic and copies ran while one was open for 7% of the time, Pallas kernels for 0%

profile of v2, /device:TPU:25, one launch (start us, length us, event | category | flops | bytes accessed | tf_op | source)
XLA Modules:
  0.0 176.8 jit_solution(4950419153101527262)
XLA Ops:
  0.0 6.2 %fusion.68 = f32[64,2,16,64]{3,0,2,1:T(8,128)S(1)} fusion(s32[64]{0:T(128)S(1)} %iota_add_fusion.1, bf16[2,1,16,64,1024]{4,3,2,1,0:T(8,128)(2,1)} %param.9), kind=kOutput, calls=%fused_computation.96 | convolution fusion | flops 269549568 | bytes 4718848 | tf_op jit(solution)/shard_map/xm,blncx->mblnc/dot_general | solution.py:45
  6.3 7.1 %convolution_convert_fusion = bf16[64,2,64,64]{3,2,1,0:T(8,128)(2,1)S(1)} fusion(f32[64,2,16,64]{3,0,2,1:T(8,128)S(1)} %fusion.68, s32[64]{0:T(128)S(1)} %iota_add_fusion.1, s32[16]{0:T(128)S(1)} %iota_add_fusion), kind=kOutput, calls=%fused_computation.77 | convolution fusion | flops 101203968 | bytes 1573184 | tf_op jit(solution)/shard_map/nk,mblnc->mblkc/dot_general | solution.py:46
  13.3 2.3 %reshape.71 = bf16[32,2,8192]{2,1,0:T(2,128)(2,1)} reshape(bf16[32,1,2,2,64,64]{5,4,3,2,1,0:T(8,128)(2,1)S(1)} %bitcast.170) | data formatting | bytes 2097152
  15.6 11.8 %all-to-all-start = ((bf16[32,2,8192]{2,1,0:T(2,128)(2,1)}), bf16[32,2,8192]{2,1,0:T(2,128)(2,1)S(1)}, u32[]{:S(2)}, u32[]{:S(2)}) async-start(bf16[32,2,8192]{2,1,0:T(2,128)(2,1)} %reshape.71), calls=%async_computation | async-start | bytes 2097152 | tf_op jit(solution)/shard_map/all_to_all | solution.py:49
  27.3 7.0 %fusion.99 = (bf16[1,64,2,64,64]{4,3,2,1,0:T(8,128)(2,1)}, bf16[1,64,2,64,64]{4,3,2,1,0:T(8,128)(2,1)}, bf16[1,64,2,64,64]{4,3,2,1,0:T(8,128)(2,1)}) fusion(bf16[3,64,2,64,64]{4,3,2,1,0:T(8,128)(2,1)} %param.10), kind=kLoop, calls=%fused_computation.134 | loop fusion | bytes 6291456 | tf_op jit(solution)/shard_map/slice | solution.py:54
  34.3 21.2 %all-to-all-done = bf16[32,2,8192]{2,1,0:T(2,128)(2,1)S(1)} async-done(((bf16[32,2,8192]{2,1,0:T(2,128)(2,1)}), bf16[32,2,8192]{2,1,0:T(2,128)(2,1)S(1)}, u32[]{:S(2)}, u32[]{:S(2)}) %all-to-all-start) | async-done | bytes 1048608 | tf_op jit(solution)/shard_map/all_to_all | solution.py:49
  55.5 1.3 reshape.72
  56.8 0.4 bitcast_reduce_fusion
  57.4 2.5 %collective-permute-start.1 = (bf16[2,2,1,64,64]{4,1,3,0,2:T(2,128)(2,1)S(1)}, bf16[2,2,1,64,64]{4,1,3,0,2:T(2,128)(2,1)S(1)}, u32[]{:S(2)}, u32[]{:S(2)}) collective-permute-start(bf16[2,2,1,64,64]{4,1,3,0,2:T(2,128)(2,1)S(1)} %bitcast.171), channel_id=1, source_target_pairs={{1,0},{2,1},{3,2},{4,3},{5,4},{6,5},{7,6},{9,8},{10,9},{11,10},{12... | collective-permute-start | bytes 98312 | tf_op jit(solution)/shard_map/ppermute | solution.py:19
  59.9 3.1 %collective-permute-start = (bf16[2,2,1,64,64]{4,1,3,0,2:T(2,128)(2,1)S(1)}, bf16[2,2,1,64,64]{4,1,3,0,2:T(2,128)(2,1)S(1)}, u32[]{:S(2)}, u32[]{:S(2)}) collective-permute-start(bf16[2,2,1,64,64]{4,1,3,0,2:T(2,128)(2,1)S(1)} %bitcast.172), channel_id=1, source_target_pairs={{0,1},{1,2},{2,3},{3,4},{4,5},{5,6},{6,7},{8,9},{9,10},{10,11},{11... | collective-permute-start | bytes 98312 | tf_op jit(solution)/shard_map/ppermute | solution.py:17
  63.0 2.2 %fusion.53 = f32[2,64,2,64]{3,2,1,0:T(2,128)S(1)} fusion(bf16[2,2,64,64]{3,1,2,0:T(2,128)(2,1)S(1)} %copy.18, bf16[1,64,2,64,64]{4,3,2,1,0:T(8,128)(2,1)} %get-tuple-element.124), kind=kOutput, calls=%fused_computation.73 | convolution fusion | flops 2097152 | bytes 1146880 | tf_op jit(solution)/shard_map/kjco,jblkc->jblko/dot_general | solution.py:58
  65.2 2.2 %fusion.52 = f32[2,64,2,64]{3,2,1,0:T(2,128)S(1)} fusion(bf16[1,64,2,64,64]{4,3,2,1,0:T(8,128)(2,1)} %get-tuple-element.125, bf16[2,2,1,64,64]{4,1,3,0,2:T(2,128)(2,1)S(1)} %collective-permute-done.1), kind=kOutput, calls=%fused_computation.71 | convolution fusion | flops 2097152 | bytes 1146880 | tf_op jit(solution)/shard_map/kjco,jblkc->jblko/dot_general | solution.py:64
  67.5 0.7 fusion.59
  68.2 0.5 broadcast_bitcast_fusion
  68.7 2.2 %reshape.73 = bf16[32,2,8192]{2,1,0:T(2,128)(2,1)} reshape(bf16[32,1,2,2,64,64]{5,4,3,2,1,0:T(8,128)(2,1)S(1)} %broadcast_bitcast_fusion) | data formatting | bytes 2097152
  70.9 6.5 %all-to-all-start.1 = ((bf16[32,2,8192]{2,1,0:T(2,128)(2,1)}), bf16[32,2,8192]{2,1,0:T(2,128)(2,1)S(1)}, u32[]{:S(2)}, u32[]{:S(2)}) async-start(bf16[32,2,8192]{2,1,0:T(2,128)(2,1)} %reshape.73), calls=%async_computation.1 | async-start | bytes 2097152 | tf_op jit(solution)/shard_map/all_to_all | solution.py:72
  77.5 28.0 %all-to-all-done.1 = bf16[32,2,8192]{2,1,0:T(2,128)(2,1)S(1)} async-done(((bf16[32,2,8192]{2,1,0:T(2,128)(2,1)}), bf16[32,2,8192]{2,1,0:T(2,128)(2,1)S(1)}, u32[]{:S(2)}, u32[]{:S(2)}) %all-to-all-start.1) | async-done | bytes 1048608 | tf_op jit(solution)/shard_map/all_to_all | solution.py:72
  105.6 1.3 reshape.74
  106.9 1.1 fusion.55
  108.0 68.8 %while.11 = (s32[]{:T(128)}, bf16[2,16,64,1024]{3,2,1,0:T(8,128)(2,1)}, bf16[2,16,64,1024]{3,2,1,0:T(8,128)(2,1)}, bf16[2,16,64,64]{2,1,0,3:T(8,128)(2,1)S(1)}, ...) while((s32[]{:T(128)}, ...), condition=%wide.region_2.3_spmd.clone, body=%wide.region_1.2_spmd.clone.sunk | while | flops 1989148672 | bytes 80725392 | solution.py:98
  108.4 1.7 fusion.123
  110.1 0.5 copy-done
  110.5 1.7 fusion.124
  112.2 9.2 %fusion.125 = bf16[16,64,1024]{2,1,0:T(8,128)(2,1)S(1)} fusion(f32[16,64,1024]{2,1,0:T(8,128)S(1)} %get-tuple-element.189, u16[64,1024]{1,0:T(8,128)(2,1)S(1)} %get-tuple-element.190), kind=kLoop, calls=%fused_computation.11.clone.1 | loop fusion | flops 71303168 | bytes 6422528 | tf_op jit(solution)/shard_map/while/body/eval_jaxpr/convert_element_type | solution.py:91
  121.5 8.1 %fusion.126 = f32[16,1024,256]{2,1,0:T(8,128)} fusion(bf16[16,64,1024]{2,1,0:T(8,128)(2,1)S(1)} %fusion.125, bf16[64,256]{1,0:T(8,128)(2,1)S(1)} %get-tuple-element.220), kind=kOutput, calls=%fused_computation.58.clone.1 | convolution fusion | flops 536870912 | bytes 18907136 | tf_op jit(solution)/shard_map/while/body/eval_jaxpr/ch,ncx->nhx/dot_general | solution.py:93
  129.6 12.8 %fusion.127 = bf16[2,16,64,1024]{3,2,1,0:T(8,128)(2,1)} fusion(bf16[2,16,64,1024]{3,2,1,0:T(8,128)(2,1)} %get-tuple-element.203, s32[]{:T(128)} %get-tuple-element.202, bf16[2,16,64,1024]{3,2,1,0:T(8,128)(2,1)} %get-tuple-element.215, f32[16,1024,256]{2,1,0:T(8,128)} %fusion.126, bf16[16,64,1024]{2,1,0:T(8,128)(2,1)S(1)} %fusion.125, ...), kind=kOutput, calls=%fused_computation.34.clone.1 | convolution fusion | flops 1102053376 | bytes 23134720 | tf_op jit(solution)/shard_map/while/body/eval_jaxpr/hc,nhx->ncx/dot_general | solution.py:95
  142.7 1.7 fusion.123
  144.5 0.4 copy-done
  144.9 1.7 fusion.124
  146.6 9.2 %fusion.125 = bf16[16,64,1024]{2,1,0:T(8,128)(2,1)S(1)} fusion(f32[16,64,1024]{2,1,0:T(8,128)S(1)} %get-tuple-element.189, u16[64,1024]{1,0:T(8,128)(2,1)S(1)} %get-tuple-element.190), kind=kLoop, calls=%fused_computation.11.clone.1 | loop fusion | flops 71303168 | bytes 6422528 | tf_op jit(solution)/shard_map/while/body/eval_jaxpr/convert_element_type | solution.py:91
  155.8 8.1 %fusion.126 = f32[16,1024,256]{2,1,0:T(8,128)} fusion(bf16[16,64,1024]{2,1,0:T(8,128)(2,1)S(1)} %fusion.125, bf16[64,256]{1,0:T(8,128)(2,1)S(1)} %get-tuple-element.220), kind=kOutput, calls=%fused_computation.58.clone.1 | convolution fusion | flops 536870912 | bytes 18907136 | tf_op jit(solution)/shard_map/while/body/eval_jaxpr/ch,ncx->nhx/dot_general | solution.py:93
  164.0 12.8 %fusion.127 = bf16[2,16,64,1024]{3,2,1,0:T(8,128)(2,1)} fusion(bf16[2,16,64,1024]{3,2,1,0:T(8,128)(2,1)} %get-tuple-element.203, s32[]{:T(128)} %get-tuple-element.202, bf16[2,16,64,1024]{3,2,1,0:T(8,128)(2,1)} %get-tuple-element.215, f32[16,1024,256]{2,1,0:T(8,128)} %fusion.126, bf16[16,64,1024]{2,1,0:T(8,128)(2,1)S(1)} %fusion.125, ...), kind=kOutput, calls=%fused_computation.34.clone.1 | convolution fusion | flops 1102053376 | bytes 23134720 | tf_op jit(solution)/shard_map/while/body/eval_jaxpr/hc,nhx->ncx/dot_general | solution.py:95
  (26 shorter events, 0.9 us)
Async XLA Ops:
  15.6 39.9 %all-to-all-start = ((bf16[32,2,8192]{2,1,0:T(2,128)(2,1)}), bf16[32,2,8192]{2,1,0:T(2,128)(2,1)S(1)}, u32[]{:S(2)}, u32[]{:S(2)}) async-start(bf16[32,2,8192]{2,1,0:T(2,128)(2,1)} %reshape.71), calls=%async_computation | async-start | bytes 2097152 | tf_op jit(solution)/shard_map/all_to_all | solution.py:49
  57.2 10.2 %copy-start.1 = (bf16[1,64,2,64,64]{4,3,2,1,0:T(8,128)(2,1)S(1)}, bf16[1,64,2,64,64]{4,3,2,1,0:T(8,128)(2,1)}, u32[]{:S(2)}) copy-start(bf16[1,64,2,64,64]{4,3,2,1,0:T(8,128)(2,1)} %get-tuple-element.123) | copy-start | bytes 3145732
  57.4 7.8 %collective-permute-start.1 = (bf16[2,2,1,64,64]{4,1,3,0,2:T(2,128)(2,1)S(1)}, bf16[2,2,1,64,64]{4,1,3,0,2:T(2,128)(2,1)S(1)}, u32[]{:S(2)}, u32[]{:S(2)}) collective-permute-start(bf16[2,2,1,64,64]{4,1,3,0,2:T(2,128)(2,1)S(1)} %bitcast.171), channel_id=1, source_target_pairs={{1,0},{2,1},{3,2},{4,3},{5,4},{6,5},{7,6},{9,8},{10,9},{11,10},{12... | collective-permute-start | bytes 98312 | tf_op jit(solution)/shard_map/ppermute | solution.py:19
  59.9 7.6 %collective-permute-start = (bf16[2,2,1,64,64]{4,1,3,0,2:T(2,128)(2,1)S(1)}, bf16[2,2,1,64,64]{4,1,3,0,2:T(2,128)(2,1)S(1)}, u32[]{:S(2)}, u32[]{:S(2)}) collective-permute-start(bf16[2,2,1,64,64]{4,1,3,0,2:T(2,128)(2,1)S(1)} %bitcast.172), channel_id=1, source_target_pairs={{0,1},{1,2},{2,3},{3,4},{4,5},{5,6},{6,7},{8,9},{9,10},{10,11},{11... | collective-permute-start | bytes 98312 | tf_op jit(solution)/shard_map/ppermute | solution.py:17
  68.1 9.3 %copy-start.3 = (bf16[64,64]{1,0:T(8,128)(2,1)S(1)}, bf16[64,64]{1,0:T(8,128)(2,1)}, u32[]{:S(2)}) copy-start(bf16[64,64]{1,0:T(8,128)(2,1)} %param.11) | copy-start | bytes 24580
  70.9 37.0 %copy-start.2 = (bf16[64,256]{1,0:T(8,128)(2,1)S(1)}, bf16[64,256]{1,0:T(8,128)(2,1)}, u32[]{:S(2)}) copy-start(bf16[64,256]{1,0:T(8,128)(2,1)} %param.14) | copy-start | bytes 98308
  70.9 37.1 %copy-start.4 = (f32[64]{0:T(128)S(1)}, f32[64]{0:T(128)}, u32[]{:S(2)}) copy-start(f32[64]{0:T(128)} %param.12) | copy-start | bytes 772
  70.9 37.1 %copy-start.5 = (bf16[64,256]{1,0:T(8,128)(2,1)S(1)}, bf16[64,256]{1,0:T(8,128)(2,1)}, u32[]{:S(2)}) copy-start(bf16[64,256]{1,0:T(8,128)(2,1)} %param.13) | copy-start | bytes 98308
  70.9 37.1 %copy-start.6 = (bf16[256,64]{0,1:T(8,128)(2,1)S(1)}, bf16[256,64]{0,1:T(8,128)(2,1)}, u32[]{:S(2)}) copy-start(bf16[256,64]{0,1:T(8,128)(2,1)} %param.15) | copy-start | bytes 98308
  70.9 34.6 %all-to-all-start.1 = ((bf16[32,2,8192]{2,1,0:T(2,128)(2,1)}), bf16[32,2,8192]{2,1,0:T(2,128)(2,1)S(1)}, u32[]{:S(2)}, u32[]{:S(2)}) async-start(bf16[32,2,8192]{2,1,0:T(2,128)(2,1)} %reshape.73), calls=%async_computation.1 | async-start | bytes 2097152 | tf_op jit(solution)/shard_map/all_to_all | solution.py:72
  108.3 2.2 %copy-start = (bf16[2,16,64,1024]{3,2,1,0:T(8,128)(2,1)S(1)}, bf16[2,16,64,1024]{3,2,1,0:T(8,128)(2,1)}, u32[]{:S(2)}) copy-start(bf16[2,16,64,1024]{3,2,1,0:T(8,128)(2,1)} %get-tuple-element.215) | copy-start | bytes 12582916 | tf_op jit(solution)/shard_map/while
  142.7 2.2 %copy-start = (bf16[2,16,64,1024]{3,2,1,0:T(8,128)(2,1)S(1)}, bf16[2,16,64,1024]{3,2,1,0:T(8,128)(2,1)}, u32[]{:S(2)}) copy-start(bf16[2,16,64,1024]{3,2,1,0:T(8,128)(2,1)} %get-tuple-element.215) | copy-start | bytes 12582916 | tf_op jit(solution)/shard_map/while

commit v3 on v2

--- a/solution.py
+++ b/solution.py
@@ -3,6 +3,8 @@
 import jax
 import jax.numpy as jnp
 from jax import lax
+from jax.experimental import pallas as pl
+from jax.experimental.pallas import tpu as pltpu
 from jax.sharding import PartitionSpec as P
 
 
@@ -28,6 +30,58 @@
     turns = positions[:, None] * freq[None, :] % count
     angle = 2.0 * math.pi / count * turns.astype(jnp.float32)
     return (jnp.cos(angle) + jnp.sin(angle)) / math.sqrt(count)
+
+
+def finish_kernel(field_ref, back_ref, lon_ref, local_ref, bias_ref, gate_ref, up_ref, down_ref, out_ref):
+    sqrt_half = math.sqrt(0.5)
+    for r in range(field_ref.shape[0]):
+        grid = field_ref[r]
+        spectral = jnp.dot(back_ref[r], lon_ref[...], preferred_element_type=jnp.float32)
+        local = jnp.dot(local_ref[...], grid, preferred_element_type=jnp.float32)
+        value = spectral + local + bias_ref[...]
+        act = (0.5 * value * (1.0 + lax.erf(value * sqrt_half))).astype(jnp.bfloat16)
+        gate = jnp.dot(gate_ref[...], act, preferred_element_type=jnp.float32)
+        upper = jnp.dot(up_ref[...], act, preferred_element_type=jnp.float32)
+        hidden = (gate / (1.0 + jnp.exp(-gate)) * upper).astype(jnp.bfloat16)
+        down = jnp.dot(down_ref[...], hidden, preferred_element_type=jnp.float32)
+        out_ref[r] = (grid.astype(jnp.float32) + down).astype(out_ref.dtype)
+
+
+def finish(field, back, lon_table, local_weight, local_bias, gate_weight, up_weight, down_weight, block=2):
+    rows, chans, lon_cells = field.shape
+    modes = back.shape[2]
+    hid = gate_weight.shape[1]
+    whole = lambda i: (0, 0)
+    return pl.pallas_call(
+        finish_kernel,
+        out_shape=jax.ShapeDtypeStruct(field.shape, field.dtype),
+        grid=(rows // block,),
+        in_specs=[
+            pl.BlockSpec((block, chans, lon_cells), lambda i: (i, 0, 0)),
+            pl.BlockSpec((block, chans, modes), lambda i: (i, 0, 0)),
+            pl.BlockSpec((modes, lon_cells), whole),
+            pl.BlockSpec((chans, chans), whole),
+            pl.BlockSpec((chans, 1), whole),
+            pl.BlockSpec((hid, chans), whole),
+            pl.BlockSpec((hid, chans), whole),
+            pl.BlockSpec((chans, hid), whole),
+        ],
+        out_specs=pl.BlockSpec((block, chans, lon_cells), lambda i: (i, 0, 0)),
+        cost_estimate=pl.CostEstimate(
+            flops=2 * rows * lon_cells * chans * (modes + chans + 3 * hid),
+            transcendentals=rows * lon_cells * (chans + 2 * hid),
+            bytes_accessed=4 * field.size + 2 * back.size,
+        ),
+    )(
+        field,
+        back,
+        lon_table.T,
+        local_weight.T,
+        local_bias.reshape(chans, 1),
+        gate_weight.T,
+        up_weight.T,
+        down_weight.T,
+    )
 
 
 def body(field, spectral_weight, local_weight, local_bias, gate_weight, up_weight, down_weight):
@@ -80,27 +134,15 @@
     )
     back_b = values.astype(jnp.bfloat16)
 
-    def finish(pair):
-        grid, coarse = pair
-        spectral = jnp.dot(
-            coarse.reshape(-1, lon_modes), lon_table.T, preferred_element_type=jnp.float32
-        )
-        spectral = spectral.reshape(lat_rows, chans, lon_cells)
-        local = jnp.einsum("co,ncx->nox", local_weight, grid, preferred_element_type=jnp.float32)
-        value = spectral + local + local_bias[None, :, None]
-        act = jax.nn.gelu(value, approximate=False).astype(jnp.bfloat16)
-        gate = jnp.einsum("ch,ncx->nhx", gate_weight, act, preferred_element_type=jnp.float32)
-        upper = jnp.einsum("ch,ncx->nhx", up_weight, act, preferred_element_type=jnp.float32)
-        hidden = (jax.nn.silu(gate) * upper).astype(jnp.bfloat16)
-        down = jnp.einsum("hc,nhx->ncx", down_weight, hidden, preferred_element_type=jnp.float32)
-        return (grid.astype(jnp.float32) + down).astype(jnp.bfloat16)
-
-    result = lax.map(
-        finish,
-        (
-            field.reshape(batch * levels, lat_rows, chans, lon_cells),
-            back_b.reshape(batch * levels, lat_rows, chans, lon_modes),
-        ),
+    result = finish(
+        field.reshape(batch * levels * lat_rows, chans, lon_cells),
+        back_b.reshape(batch * levels * lat_rows, chans, lon_modes),
+        lon_table,
+        local_weight,
+        local_bias,
+        gate_weight,
+        up_weight,
+        down_weight,
     )
     return result.reshape(batch, levels, lat_rows, chans, lon_cells)
 

time: 179 us -> 138 us (0.77)
  matrix products: 68.2 us -> 18.1 us
  Pallas kernels: 0 us -> 27.6 us
  other arithmetic: 18.9 us -> 2.26 us
  waiting for transfers between devices: 49.2 us -> 44.6 us
  local copies, waits for them, and re-layouts: 16.4 us -> 19.1 us
    dot_general x8 -> x0, matrix products: 48.7 us -> none  [the longest x2 25.6 us: finish(): jnp.einsum('hc,nhx->ncx', down_weight, hidden, preferred_element_type=jnp...]
    pallas_call x0 -> x1, Pallas kernels: none -> 27.6 us  [finish(): pl.pallas_call(finish_kernel, out_shape=jax.ShapeDtypeStruct(field.shape,...]
    convert_element_type x2 -> x1, other arithmetic: 18.5 us -> 1.83 us  [body(): cas_rows(jnp.arange(lon_cells, dtype=jnp.int32), lon_cells, lon_modes)]
    all_to_all x1, waiting for transfers between devices: 28 us -> 23.4 us  [body(): lax.all_to_all(copies, 'rows', 0, 0, tiled=True)]
    unnamed x18 -> x20, local copies, waits for them, and re-layouts: 7.78 us -> 9.95 us
  transfers between devices with their start and end apart: 4 -> 4, of which waited for: 2 -> 2; matrix products, arithmetic and copies ran while one was open for 7% -> 11% of each run, Pallas kernels for 0% -> 0%
where the time goes in v3:
time: 138 us; the launch traced here: 137 us
  waiting for transfers between devices  44.6 us (32%)
  Pallas kernels  27.6 us (20%)
  starting transfers between devices  24.9 us (18%)
  local copies, waits for them, and re-layouts  19.1 us (14%)
  matrix products  18.1 us (13%)
  other arithmetic  2.26 us (2%)
    pallas_call x1, Pallas kernels, finish(): pl.pallas_call(finish_kernel, out_shape=jax.ShapeDtypeStruct(field.shape,...  27.6 us
    all_to_all x1, waiting for transfers between devices, body(): lax.all_to_all(copies, 'rows', 0, 0, tiled=True)  23.4 us
    all_to_all x1, waiting for transfers between devices, body(): pieces = lax.all_to_all(pieces, 'rows', 0, 0, tiled=True)  21.2 us
    all_to_all x1, starting transfers between devices, body(): pieces = lax.all_to_all(pieces, 'rows', 0, 0, tiled=True)  11.8 us
    unnamed x20, local copies, waits for them, and re-layouts  9.95 us
    all_to_all x1, starting transfers between devices, body(): lax.all_to_all(copies, 'rows', 0, 0, tiled=True)  7.57 us
    dot_general x1, matrix products, body(): jnp.einsum('nk,mblnc->mblkc', own_table, along, precision=high)  7.06 us
    slice x1, local copies, waits for them, and re-layouts, body(): spectral_weight[0]  6.97 us
  transfers between devices with their start and end apart: 4, of which 2 were waited for; matrix products, arithmetic and copies ran while one was open for 11% of the time, Pallas kernels for 0%

profile of v3, /device:TPU:25, one launch (start us, length us, event | category | flops | bytes accessed | tf_op | source)
XLA Modules:
  0.0 136.8 jit_solution(17681894946886331409)
XLA Ops:
  0.0 6.2 %fusion = f32[64,2,16,64]{3,0,2,1:T(8,128)S(1)} fusion(bf16[2,1,16,64,1024]{4,3,2,1,0:T(8,128)(2,1)} %param.7, s32[64]{0:T(128)S(1)} %iota_add_fusion.1), kind=kOutput, calls=%fused_computation | convolution fusion | flops 269549568 | bytes 4718848 | tf_op jit(solution)/shard_map/xm,blncx->mblnc/dot_general | solution.py:99
  6.3 7.1 %convolution_convert_fusion = bf16[64,2,64,64]{3,2,1,0:T(8,128)(2,1)S(1)} fusion(f32[64,2,16,64]{3,0,2,1:T(8,128)S(1)} %fusion, s32[64]{0:T(128)S(1)} %iota_add_fusion.1, s32[16]{0:T(128)S(1)} %iota_add_fusion), kind=kOutput, calls=%fused_computation.9 | convolution fusion | flops 101203968 | bytes 1573184 | tf_op jit(solution)/shard_map/nk,mblnc->mblkc/dot_general | solution.py:100
  13.3 2.3 %reshape.67 = bf16[32,2,8192]{2,1,0:T(2,128)(2,1)} reshape(bf16[32,1,2,2,64,64]{5,4,3,2,1,0:T(8,128)(2,1)S(1)} %bitcast.78) | data formatting | bytes 2097152
  15.7 11.8 %all-to-all-start = ((bf16[32,2,8192]{2,1,0:T(2,128)(2,1)}), bf16[32,2,8192]{2,1,0:T(2,128)(2,1)S(1)}, u32[]{:S(2)}, u32[]{:S(2)}) async-start(bf16[32,2,8192]{2,1,0:T(2,128)(2,1)} %reshape.67), calls=%async_computation | async-start | bytes 2097152 | tf_op jit(solution)/shard_map/all_to_all | solution.py:103
  27.4 7.0 %fusion.53 = (bf16[1,64,2,64,64]{4,3,2,1,0:T(8,128)(2,1)}, bf16[1,64,2,64,64]{4,3,2,1,0:T(8,128)(2,1)}, bf16[1,64,2,64,64]{4,3,2,1,0:T(8,128)(2,1)}) fusion(bf16[3,64,2,64,64]{4,3,2,1,0:T(8,128)(2,1)} %param.8), kind=kLoop, calls=%fused_computation.74 | loop fusion | bytes 6291456 | tf_op jit(solution)/shard_map/slice | solution.py:108
  34.4 21.2 %all-to-all-done = bf16[32,2,8192]{2,1,0:T(2,128)(2,1)S(1)} async-done(((bf16[32,2,8192]{2,1,0:T(2,128)(2,1)}), bf16[32,2,8192]{2,1,0:T(2,128)(2,1)S(1)}, u32[]{:S(2)}, u32[]{:S(2)}) %all-to-all-start) | async-done | bytes 1048608 | tf_op jit(solution)/shard_map/all_to_all | solution.py:103
  55.6 1.3 reshape.68
  56.9 0.4 bitcast_reduce_fusion
  57.3 0.1 copy.20
  57.4 2.5 %collective-permute-start.1 = (bf16[2,2,1,64,64]{4,1,3,0,2:T(2,128)(2,1)S(1)}, bf16[2,2,1,64,64]{4,1,3,0,2:T(2,128)(2,1)S(1)}, u32[]{:S(2)}, u32[]{:S(2)}) collective-permute-start(bf16[2,2,1,64,64]{4,1,3,0,2:T(2,128)(2,1)S(1)} %bitcast.80), channel_id=1, source_target_pairs={{1,0},{2,1},{3,2},{4,3},{5,4},{6,5},{7,6},{9,8},{10,9},{11,10},{12... | collective-permute-start | bytes 98312 | tf_op jit(solution)/shard_map/ppermute | solution.py:21
  60.0 3.1 %collective-permute-start = (bf16[2,2,1,64,64]{4,1,3,0,2:T(2,128)(2,1)S(1)}, bf16[2,2,1,64,64]{4,1,3,0,2:T(2,128)(2,1)S(1)}, u32[]{:S(2)}, u32[]{:S(2)}) collective-permute-start(bf16[2,2,1,64,64]{4,1,3,0,2:T(2,128)(2,1)S(1)} %bitcast.81), channel_id=1, source_target_pairs={{0,1},{1,2},{2,3},{3,4},{4,5},{5,6},{6,7},{8,9},{9,10},{10,11},{11... | collective-permute-start | bytes 98312 | tf_op jit(solution)/shard_map/ppermute | solution.py:19
  63.0 0.0 copy-start.1
  63.0 2.4 %fusion.3 = f32[2,64,2,64]{3,2,1,0:T(2,128)S(1)} fusion(bf16[2,2,64,64]{3,1,2,0:T(2,128)(2,1)S(1)} %copy.20, bf16[1,64,2,64,64]{4,3,2,1,0:T(8,128)(2,1)} %get-tuple-element.6), kind=kOutput, calls=%fused_computation.5 | convolution fusion | flops 2097152 | bytes 1146880 | tf_op jit(solution)/shard_map/kjco,jblkc->jblko/dot_general | solution.py:112
  65.4 0.7 fusion.2
  66.1 0.7 fusion.9
  66.8 0.5 broadcast_bitcast_fusion
  67.3 0.0 copy-start.2
  67.3 0.0 copy-start.3
  67.3 0.0 copy-start.5
  67.4 0.0 copy-start.4
  67.4 2.3 %reshape.69 = bf16[32,2,8192]{2,1,0:T(2,128)(2,1)} reshape(bf16[32,1,2,2,64,64]{5,4,3,2,1,0:T(8,128)(2,1)S(1)} %broadcast_bitcast_fusion) | data formatting | bytes 2097152
  69.7 7.6 %all-to-all-start.1 = ((bf16[32,2,8192]{2,1,0:T(2,128)(2,1)}), bf16[32,2,8192]{2,1,0:T(2,128)(2,1)S(1)}, u32[]{:S(2)}, u32[]{:S(2)}) async-start(bf16[32,2,8192]{2,1,0:T(2,128)(2,1)} %reshape.69), calls=%async_computation.1 | async-start | bytes 2097152 | tf_op jit(solution)/shard_map/all_to_all | solution.py:126
  77.2 0.7 copy.28
  78.0 0.7 copy.29
  78.7 0.7 copy.30.bias_ref
  79.4 0.7 copy.27
  80.1 1.8 %multiply_convert_fusion.1.lon_ref = bf16[64,1024]{1,0:T(8,128)(2,1)} fusion(s32[64]{0:T(128)S(1)} %iota_add_fusion.1), kind=kLoop, calls=%fused_computation.34 | loop fusion | flops 1114112 | bytes 131328 | tf_op jit(solution)/shard_map/convert_element_type | solution.py:94
  82.0 23.4 %all-to-all-done.1 = bf16[32,2,8192]{2,1,0:T(2,128)(2,1)S(1)} async-done(((bf16[32,2,8192]{2,1,0:T(2,128)(2,1)}), bf16[32,2,8192]{2,1,0:T(2,128)(2,1)S(1)}, u32[]{:S(2)}, u32[]{:S(2)}) %all-to-all-start.1) | async-done | bytes 1048608 | tf_op jit(solution)/shard_map/all_to_all | solution.py:126
  105.4 1.3 reshape.70
  106.7 1.1 fusion.5
  107.8 1.4 %copy.26 = bf16[2,1,16,64,64]{4,3,2,0,1:T(8,128)(2,1)} copy(bf16[2,1,16,64,64]{3,2,0,4,1:T(8,128)(2,1)S(1)} %fusion.5) | data formatting | bytes 524288 | tf_op jit(solution)/shard_map/convert_element_type | solution.py:135
  109.1 27.6 %shard_map.73 = bf16[32,64,1024]{2,1,0:T(8,128)(2,1)} custom-call(bf16[32,64,1024]{2,1,0:T(8,128)(2,1)} %bitcast.86, bf16[32,64,64]{2,1,0:T(8,128)(2,1)} %bitcast.79, bf16[64,1024]{1,0:T(8,128)(2,1)} %multiply_convert_fusion.1.lon_ref, bf16[64,64]{1,0:T(8,128)(2,1)} %bitcast.84, f32[64,1]{1,0:T(8,128)} %copy.30.bias_ref, bf16[256,64]{1,0:T(8,128)(2,1)} %bitcast.82, ...), custom_call_target="tpu_custom_call" | custom-call | flops 3758096384 | bytes 8650752 | tf_op jit(solution)/shard_map/pallas_call | solution.py:55
  (12 shorter events, 0.0 us)
Async XLA Ops:
  15.7 39.9 %all-to-all-start = ((bf16[32,2,8192]{2,1,0:T(2,128)(2,1)}), bf16[32,2,8192]{2,1,0:T(2,128)(2,1)S(1)}, u32[]{:S(2)}, u32[]{:S(2)}) async-start(bf16[32,2,8192]{2,1,0:T(2,128)(2,1)} %reshape.67), calls=%async_computation | async-start | bytes 2097152 | tf_op jit(solution)/shard_map/all_to_all | solution.py:103
  57.3 8.1 %copy-start = (bf16[1,64,2,64,64]{4,3,2,1,0:T(8,128)(2,1)S(1)}, bf16[1,64,2,64,64]{4,3,2,1,0:T(8,128)(2,1)}, u32[]{:S(2)}) copy-start(bf16[1,64,2,64,64]{4,3,2,1,0:T(8,128)(2,1)} %get-tuple-element.7) | copy-start | bytes 3145732
  57.4 8.0 %collective-permute-start.1 = (bf16[2,2,1,64,64]{4,1,3,0,2:T(2,128)(2,1)S(1)}, bf16[2,2,1,64,64]{4,1,3,0,2:T(2,128)(2,1)S(1)}, u32[]{:S(2)}, u32[]{:S(2)}) collective-permute-start(bf16[2,2,1,64,64]{4,1,3,0,2:T(2,128)(2,1)S(1)} %bitcast.80), channel_id=1, source_target_pairs={{1,0},{2,1},{3,2},{4,3},{5,4},{6,5},{7,6},{9,8},{10,9},{11,10},{12... | collective-permute-start | bytes 98312 | tf_op jit(solution)/shard_map/ppermute | solution.py:21
  60.0 6.2 %collective-permute-start = (bf16[2,2,1,64,64]{4,1,3,0,2:T(2,128)(2,1)S(1)}, bf16[2,2,1,64,64]{4,1,3,0,2:T(2,128)(2,1)S(1)}, u32[]{:S(2)}, u32[]{:S(2)}) collective-permute-start(bf16[2,2,1,64,64]{4,1,3,0,2:T(2,128)(2,1)S(1)} %bitcast.81), channel_id=1, source_target_pairs={{0,1},{1,2},{2,3},{3,4},{4,5},{5,6},{6,7},{8,9},{9,10},{10,11},{11... | collective-permute-start | bytes 98312 | tf_op jit(solution)/shard_map/ppermute | solution.py:19
  63.0 3.1 %copy-start.1 = (bf16[1,64,2,64,64]{4,3,2,1,0:T(8,128)(2,1)S(1)}, bf16[1,64,2,64,64]{4,3,2,1,0:T(8,128)(2,1)}, u32[]{:S(2)}) copy-start(bf16[1,64,2,64,64]{4,3,2,1,0:T(8,128)(2,1)} %get-tuple-element.5) | copy-start | bytes 3145732
  67.3 9.9 %copy-start.2 = (bf16[64,256]{1,0:T(8,128)(2,1)S(1)}, bf16[64,256]{1,0:T(8,128)(2,1)}, u32[]{:S(2)}) copy-start(bf16[64,256]{1,0:T(8,128)(2,1)} %param.11) | copy-start | bytes 98308
  67.3 10.6 %copy-start.3 = (bf16[64,256]{1,0:T(8,128)(2,1)S(1)}, bf16[64,256]{1,0:T(8,128)(2,1)}, u32[]{:S(2)}) copy-start(bf16[64,256]{1,0:T(8,128)(2,1)} %param.12) | copy-start | bytes 98308
  67.3 11.4 %copy-start.5 = (f32[64]{0:T(128)S(1)}, f32[64]{0:T(128)}, u32[]{:S(2)}) copy-start(f32[64]{0:T(128)} %param.10) | copy-start | bytes 772
  67.4 12.1 %copy-start.4 = (bf16[64,64]{1,0:T(8,128)(2,1)S(1)}, bf16[64,64]{1,0:T(8,128)(2,1)}, u32[]{:S(2)}) copy-start(bf16[64,64]{1,0:T(8,128)(2,1)} %param.9) | copy-start | bytes 24580
  69.7 35.7 %all-to-all-start.1 = ((bf16[32,2,8192]{2,1,0:T(2,128)(2,1)}), bf16[32,2,8192]{2,1,0:T(2,128)(2,1)S(1)}, u32[]{:S(2)}, u32[]{:S(2)}) async-start(bf16[32,2,8192]{2,1,0:T(2,128)(2,1)} %reshape.69), calls=%async_computation.1 | async-start | bytes 2097152 | tf_op jit(solution)/shard_map/all_to_all | solution.py:126

commit v4 on v3

--- a/solution.py
+++ b/solution.py
@@ -94,14 +94,14 @@
     lon_table = cas_rows(jnp.arange(lon_cells, dtype=jnp.int32), lon_cells, lon_modes).astype(
         jnp.bfloat16
     )
-    own_rows = lax.axis_index("rows") * lat_rows + jnp.arange(lat_rows, dtype=jnp.int32)
-    own_table = cas_rows(own_rows, lat_total, lat_modes)
+    lat_table = cas_rows(jnp.arange(lat_total, dtype=jnp.int32), lat_total, lat_modes).reshape(
+        ranks, lat_rows, lat_modes
+    )
+    per = lon_modes // ranks
     along = jnp.einsum("xm,blncx->mblnc", lon_table, field, preferred_element_type=jnp.float32)
-    partial_modes = jnp.einsum("nk,mblnc->mblkc", own_table, along, precision=high)
-    per = lon_modes // ranks
-    pieces = partial_modes.astype(jnp.bfloat16).reshape((ranks, per) + partial_modes.shape[1:])
-    pieces = lax.all_to_all(pieces, "rows", 0, 0, tiled=True)
-    modes = pieces.astype(jnp.float32).sum(0).astype(jnp.bfloat16)
+    along = lax.all_to_all(along.reshape((ranks, per) + along.shape[1:]), "rows", 0, 0, tiled=True)
+    modes = jnp.einsum("sjblnc,snk->jblkc", along, lat_table, precision=high)
+    modes = modes.astype(jnp.bfloat16)
     padded = extended(modes, (("lev", 2),), 1)
     mixed = jnp.einsum(
         "kjco,jblkc->jblko",
@@ -122,17 +122,13 @@
         preferred_element_type=jnp.float32,
     )
     mixed_b = mixed.astype(jnp.bfloat16)
-    copies = jnp.broadcast_to(mixed_b[None], (ranks,) + mixed_b.shape)
-    gathered = lax.all_to_all(copies, "rows", 0, 0, tiled=True).reshape(
-        (lon_modes,) + mixed_b.shape[1:]
+    values = jnp.einsum(
+        "rnk,jblko->rjblno", lat_table, mixed_b.astype(jnp.float32), precision=high
     )
-    values = jnp.einsum(
-        "nk,mblko->blnom",
-        own_table,
-        gathered.astype(jnp.float32),
-        precision=high,
+    values = lax.all_to_all(values.astype(jnp.bfloat16), "rows", 0, 0, tiled=True)
+    back_b = jnp.transpose(values, (2, 3, 4, 5, 0, 1)).reshape(
+        batch, levels, lat_rows, chans, lon_modes
     )
-    back_b = values.astype(jnp.bfloat16)
 
     result = finish(
         field.reshape(batch * levels * lat_rows, chans, lon_cells),

time: 138 us -> 107 us (0.78)
  waiting for transfers between devices: 44.6 us -> 19.7 us
  matrix products: 18.1 us -> 13.6 us
  local copies, waits for them, and re-layouts: 19.1 us -> 17.4 us
    all_to_all x2, waiting for transfers between devices: 44.6 us -> 19.7 us  [the longest x1 10.1 us: body(): lax.all_to_all(values.astype(jnp.bfloat16), 'rows', 0, 0, tiled=True)]
    unnamed x20 -> x19, local copies, waits for them, and re-layouts: 9.95 us -> 6.5 us
    dot_general x2, matrix products: 8.12 us -> 5.72 us  [the longest x1 3.83 us: body(): modes = jnp.einsum('sjblnc,snk->jblkc', along, lat_table, precision=high)]
    dot_general x1, matrix products: 6.24 us -> 4.3 us  [body(): jnp.einsum('xm,blncx->mblnc', lon_table, field, preferred_element_type=jn...]
    all_to_all x0 -> x1, other arithmetic: none -> 1.92 us  [body(): lax.all_to_all(along.reshape((ranks, per) + along.shape[1:]), 'rows', 0,...]
    another operation x0 -> x1, local copies, waits for them, and re-layouts: none -> 1.38 us  [body(): back_b.reshape(batch * levels * lat_rows, chans, lon_modes)]
  transfers between devices with their start and end apart: 4 -> 4, of which waited for: 2 -> 2; matrix products, arithmetic and copies ran while one was open for 11% -> 12% of each run, Pallas kernels for 0% -> 0%
where the time goes in v4:
time: 107 us; the launch traced here: 106 us
  Pallas kernels  27.6 us (26%)
  starting transfers between devices  24.9 us (23%)
  waiting for transfers between devices  19.7 us (18%)
  local copies, waits for them, and re-layouts  17.4 us (16%)
  matrix products  13.6 us (13%)
  other arithmetic  3.15 us (3%)
    pallas_call x1, Pallas kernels, finish(): pl.pallas_call(finish_kernel, out_shape=jax.ShapeDtypeStruct(field.shape,...  27.6 us
    all_to_all x1, starting transfers between devices, body(): lax.all_to_all(along.reshape((ranks, per) + along.shape[1:]), 'rows', 0,...  11.8 us
    all_to_all x1, waiting for transfers between devices, body(): lax.all_to_all(values.astype(jnp.bfloat16), 'rows', 0, 0, tiled=True)  10.1 us
    all_to_all x1, waiting for transfers between devices, body(): lax.all_to_all(along.reshape((ranks, per) + along.shape[1:]), 'rows', 0,...  9.65 us
    all_to_all x1, starting transfers between devices, body(): lax.all_to_all(values.astype(jnp.bfloat16), 'rows', 0, 0, tiled=True)  7.64 us
    slice x1, local copies, waits for them, and re-layouts, body(): spectral_weight[0]  7.35 us
    unnamed x19, local copies, waits for them, and re-layouts  6.5 us
    dot_general x1, matrix products, body(): jnp.einsum('xm,blncx->mblnc', lon_table, field, preferred_element_type=jn...  4.3 us
  transfers between devices with their start and end apart: 4, of which 2 were waited for; matrix products, arithmetic and copies ran while one was open for 12% of the time, Pallas kernels for 0%

profile of v4, /device:TPU:25, one launch (start us, length us, event | category | flops | bytes accessed | tf_op | source)
XLA Modules:
  0.0 106.5 jit_solution(6742131345735492636)
XLA Ops:
  0.0 1.2 %multiply_convert_fusion.lon_ref = bf16[64,1024]{1,0:T(8,128)(2,1)S(1)} fusion(s32[64]{0:T(128)S(1)} %iota_add_fusion), kind=kLoop, calls=%fused_computation.35 | loop fusion | flops 1114112 | bytes 131328 | tf_op jit(solution)/shard_map/convert_element_type | solution.py:94
  1.2 0.1 convert_element_type.69
  1.3 4.3 %fusion.5 = f32[32,2,2,1,16,64]{5,0,4,2,1,3:T(8,128)S(1)} fusion(bf16[2,1,16,64,1024]{4,3,2,1,0:T(8,128)(2,1)} %param.7, bf16[32,2,1024,1,1]{2,1,0,4,3:T(2,128)(2,1)S(1)} %bitcast.87), kind=kOutput, calls=%fused_computation.8 | convolution fusion | flops 268435456 | bytes 4849664 | tf_op jit(solution)/shard_map/xm,blncx->mblnc/dot_general | solution.py:101
  5.6 0.6 copy.96
  6.2 1.5 %reshape.122 = f32[32,1,4096]{2,1,0:T(1,128)} reshape(f32[32,1,2,2,16,64]{5,4,3,2,1,0:T(8,128)S(1)} %bitcast.83) | data formatting | bytes 1048576
  7.7 11.8 %all-to-all-start = ((f32[32,1,4096]{2,1,0:T(1,128)}), f32[32,1,4096]{2,1,0:T(1,128)S(1)}, u32[]{:S(2)}, u32[]{:S(2)}) async-start(f32[32,1,4096]{2,1,0:T(1,128)} %reshape.122), calls=%async_computation | async-start | bytes 1048576 | tf_op jit(solution)/shard_map/all_to_all | solution.py:102
  19.5 7.3 %fusion.42 = (bf16[1,64,2,64,64]{4,3,2,1,0:T(8,128)(2,1)S(1)}, bf16[1,64,2,64,64]{4,3,2,1,0:T(8,128)(2,1)}, bf16[1,64,2,64,64]{4,3,2,1,0:T(8,128)(2,1)}) fusion(bf16[3,64,2,64,64]{4,3,2,1,0:T(8,128)(2,1)} %param.8), kind=kLoop, calls=%fused_computation.57 | loop fusion | bytes 6291456 | tf_op jit(solution)/shard_map/slice | solution.py:108
  26.8 9.6 %all-to-all-done = f32[32,1,4096]{2,1,0:T(1,128)S(1)} async-done(((f32[32,1,4096]{2,1,0:T(1,128)}), f32[32,1,4096]{2,1,0:T(1,128)S(1)}, u32[]{:S(2)}, u32[]{:S(2)}) %all-to-all-start) | async-done | bytes 524320 | tf_op jit(solution)/shard_map/all_to_all | solution.py:102
  36.5 0.6 broadcast.157
  37.0 1.9 %reduce = f32[32,4096]{1,0:T(8,128)S(1)} reduce(f32[32,1,4096]{2,1,0:T(1,128)S(1)} %all-to-all-done, f32[]{:T(128)} %broadcast.157), dimensions={1}, to_apply=%all_to_all.6.reduce_sub_computation | reduce | bytes 1048580 | tf_op jit(solution)/shard_map/all_to_all | solution.py:102
  39.0 1.4 %reshape.123 = f32[32,1,2,2,16,64]{5,4,3,2,1,0:T(8,128)} reshape(f32[32,4096]{1,0:T(8,128)S(1)} %reduce) | data formatting | bytes 1048576
  40.4 3.8 %fusion.12 = bf16[64,2,2,64]{3,0,2,1:T(8,128)(2,1)S(1)} fusion(f32[32,2,2,1,16,64]{5,4,2,1,3,0:T(8,128)} %bitcast.86, s32[64]{0:T(128)S(1)} %iota_add_fusion, s32[32,16]{0,1:T(8,128)S(1)} %multiply_add_fusion), kind=kOutput, calls=%fused_computation.15 | convolution fusion | flops 101203968 | bytes 559360 | tf_op jit(solution)/shard_map/sjblnc,snk->jblkc/dot_general | solution.py:103
  44.2 2.4 %collective-permute-start.1 = (bf16[2,2,1,64,64]{4,3,1,0,2:T(8,128)(2,1)S(1)}, bf16[2,2,1,64,64]{4,3,1,0,2:T(8,128)(2,1)S(1)}, u32[]{:S(2)}, u32[]{:S(2)}) collective-permute-start(bf16[2,2,1,64,64]{4,3,1,0,2:T(8,128)(2,1)S(1)} %bitcast.92), channel_id=1, source_target_pairs={{1,0},{2,1},{3,2},{4,3},{5,4},{6,5},{7,6},{9,8},{10,9},{11,10},{12... | collective-permute-start | bytes 98312 | tf_op jit(solution)/shard_map/ppermute | solution.py:21
  46.6 3.1 %collective-permute-start = (bf16[2,2,1,64,64]{4,3,1,0,2:T(8,128)(2,1)S(1)}, bf16[2,2,1,64,64]{4,3,1,0,2:T(8,128)(2,1)S(1)}, u32[]{:S(2)}, u32[]{:S(2)}) collective-permute-start(bf16[2,2,1,64,64]{4,3,1,0,2:T(8,128)(2,1)S(1)} %bitcast.93), channel_id=1, source_target_pairs={{0,1},{1,2},{2,3},{3,4},{4,5},{5,6},{6,7},{8,9},{9,10},{10,11},{11... | collective-permute-start | bytes 98312 | tf_op jit(solution)/shard_map/ppermute | solution.py:19
  49.7 2.2 %fusion.3 = f32[2,64,2,64]{3,2,1,0:T(2,128)S(1)} fusion(bf16[1,64,2,64,64]{4,3,2,1,0:T(8,128)(2,1)} %get-tuple-element.6, bf16[2,2,64,64]{3,2,1,0:T(8,128)(2,1)S(1)} %bitcast.94), kind=kOutput, calls=%fused_computation.5 | convolution fusion | flops 2097152 | bytes 1146880 | tf_op jit(solution)/shard_map/kjco,jblkc->jblko/dot_general | solution.py:112
  51.9 0.7 fusion.2
  52.6 0.7 fusion.13
  53.3 0.0 copy-start.2
  53.3 0.0 copy-start.3
  53.3 0.0 copy-start.5
  53.3 1.9 %fusion.8 = bf16[32,2,2,1,16,64]{5,0,4,2,1,3:T(8,128)(2,1)S(1)} fusion(s32[64]{0:T(128)S(1)} %iota_add_fusion, s32[32,16]{0,1:T(8,128)S(1)} %multiply_add_fusion, bf16[2,2,64,64,1]{3,1,2,0,4:T(2,128)(2,1)S(1)} %fusion.13), kind=kOutput, calls=%fused_computation.10 | convolution fusion | flops 101318656 | bytes 297216 | tf_op jit(solution)/shard_map/rnk,jblko->rjblno/dot_general | solution.py:125
  55.2 0.2 copy.97
  55.4 1.1 %reshape.124 = bf16[32,2,2048]{2,1,0:T(2,128)(2,1)} reshape(bf16[32,1,2,2,16,64]{5,4,3,2,1,0:T(8,128)(2,1)S(1)} %bitcast.84) | data formatting | bytes 524288
  56.5 7.6 %all-to-all-start.1 = ((bf16[32,2,2048]{2,1,0:T(2,128)(2,1)}), bf16[32,2,2048]{2,1,0:T(2,128)(2,1)S(1)}, u32[]{:S(2)}, u32[]{:S(2)}) async-start(bf16[32,2,2048]{2,1,0:T(2,128)(2,1)} %reshape.124), calls=%async_computation.1 | async-start | bytes 524288 | tf_op jit(solution)/shard_map/all_to_all | solution.py:128
  64.2 0.7 copy.50
  64.9 0.7 copy.51
  65.6 0.7 copy.53.bias_ref
  66.3 0.7 copy.49
  67.0 10.1 %all-to-all-done.1 = bf16[32,2,2048]{2,1,0:T(2,128)(2,1)S(1)} async-done(((bf16[32,2,2048]{2,1,0:T(2,128)(2,1)}), bf16[32,2,2048]{2,1,0:T(2,128)(2,1)S(1)}, u32[]{:S(2)}, u32[]{:S(2)}) %all-to-all-start.1) | async-done | bytes 262176 | tf_op jit(solution)/shard_map/all_to_all | solution.py:128
  77.1 0.4 reshape.125
  77.5 1.4 %copy.52.back_ref = bf16[32,64,64]{2,1,0:T(8,128)(2,1)} copy(bf16[32,64,64]{1,0,2:T(8,128)(2,1)S(1)} %bitcast.85) | data formatting | bytes 524288 | tf_op jit(solution)/shard_map/reshape;reshape | solution.py:135
  78.8 27.6 %shard_map.73 = bf16[32,64,1024]{2,1,0:T(8,128)(2,1)} custom-call(bf16[32,64,1024]{2,1,0:T(8,128)(2,1)} %bitcast.82, bf16[32,64,64]{2,1,0:T(8,128)(2,1)} %copy.52.back_ref, bf16[64,1024]{1,0:T(8,128)(2,1)} %copy-done.1, bf16[64,64]{1,0:T(8,128)(2,1)} %bitcast.90, f32[64,1]{1,0:T(8,128)} %copy.53.bias_ref, bf16[256,64]{1,0:T(8,128)(2,1)} %bitcast.88, ...), custom_call_target="tpu_custom_call" | custom-call | flops 3758096384 | bytes 8650752 | tf_op jit(solution)/shard_map/pallas_call | solution.py:55
  (13 shorter events, 0.0 us)
Async XLA Ops:
  1.2 4.4 %copy-start.1 = (bf16[64,1024]{1,0:T(8,128)(2,1)}, bf16[64,1024]{1,0:T(8,128)(2,1)S(1)}, u32[]{:S(2)}) copy-start(bf16[64,1024]{1,0:T(8,128)(2,1)S(1)} %multiply_convert_fusion.lon_ref) | copy-start | bytes 393220
  7.7 28.8 %all-to-all-start = ((f32[32,1,4096]{2,1,0:T(1,128)}), f32[32,1,4096]{2,1,0:T(1,128)S(1)}, u32[]{:S(2)}, u32[]{:S(2)}) async-start(f32[32,1,4096]{2,1,0:T(1,128)} %reshape.122), calls=%async_computation | async-start | bytes 1048576 | tf_op jit(solution)/shard_map/all_to_all | solution.py:102
  40.4 11.6 %copy-start = (bf16[1,64,2,64,64]{4,3,2,1,0:T(8,128)(2,1)S(1)}, bf16[1,64,2,64,64]{4,3,2,1,0:T(8,128)(2,1)}, u32[]{:S(2)}) copy-start(bf16[1,64,2,64,64]{4,3,2,1,0:T(8,128)(2,1)} %get-tuple-element.7) | copy-start | bytes 3145732
  44.2 7.7 %collective-permute-start.1 = (bf16[2,2,1,64,64]{4,3,1,0,2:T(8,128)(2,1)S(1)}, bf16[2,2,1,64,64]{4,3,1,0,2:T(8,128)(2,1)S(1)}, u32[]{:S(2)}, u32[]{:S(2)}) collective-permute-start(bf16[2,2,1,64,64]{4,3,1,0,2:T(8,128)(2,1)S(1)} %bitcast.92), channel_id=1, source_target_pairs={{1,0},{2,1},{3,2},{4,3},{5,4},{6,5},{7,6},{9,8},{10,9},{11,10},{12... | collective-permute-start | bytes 98312 | tf_op jit(solution)/shard_map/ppermute | solution.py:21
  46.6 6.0 %collective-permute-start = (bf16[2,2,1,64,64]{4,3,1,0,2:T(8,128)(2,1)S(1)}, bf16[2,2,1,64,64]{4,3,1,0,2:T(8,128)(2,1)S(1)}, u32[]{:S(2)}, u32[]{:S(2)}) collective-permute-start(bf16[2,2,1,64,64]{4,3,1,0,2:T(8,128)(2,1)S(1)} %bitcast.93), channel_id=1, source_target_pairs={{0,1},{1,2},{2,3},{3,4},{4,5},{5,6},{6,7},{8,9},{9,10},{10,11},{11... | collective-permute-start | bytes 98312 | tf_op jit(solution)/shard_map/ppermute | solution.py:19
  53.3 10.9 %copy-start.2 = (bf16[64,256]{1,0:T(8,128)(2,1)S(1)}, bf16[64,256]{1,0:T(8,128)(2,1)}, u32[]{:S(2)}) copy-start(bf16[64,256]{1,0:T(8,128)(2,1)} %param.11) | copy-start | bytes 98308
  53.3 11.6 %copy-start.3 = (bf16[64,256]{1,0:T(8,128)(2,1)S(1)}, bf16[64,256]{1,0:T(8,128)(2,1)}, u32[]{:S(2)}) copy-start(bf16[64,256]{1,0:T(8,128)(2,1)} %param.12) | copy-start | bytes 98308
  53.3 12.3 %copy-start.5 = (f32[64]{0:T(128)S(1)}, f32[64]{0:T(128)}, u32[]{:S(2)}) copy-start(f32[64]{0:T(128)} %param.10) | copy-start | bytes 772
  53.3 13.0 %copy-start.4 = (bf16[64,64]{1,0:T(8,128)(2,1)S(1)}, bf16[64,64]{1,0:T(8,128)(2,1)}, u32[]{:S(2)}) copy-start(bf16[64,64]{1,0:T(8,128)(2,1)} %param.9) | copy-start | bytes 24580
  56.5 20.6 %all-to-all-start.1 = ((bf16[32,2,2048]{2,1,0:T(2,128)(2,1)}), bf16[32,2,2048]{2,1,0:T(2,128)(2,1)S(1)}, u32[]{:S(2)}, u32[]{:S(2)}) async-start(bf16[32,2,2048]{2,1,0:T(2,128)(2,1)} %reshape.124), calls=%async_computation.1 | async-start | bytes 524288 | tf_op jit(solution)/shard_map/all_to_all | solution.py:128

commit v5 on v4

--- a/solution.py
+++ b/solution.py
@@ -1,3 +1,4 @@
+import functools
 import math
 
 import jax
@@ -30,6 +31,73 @@
     turns = positions[:, None] * freq[None, :] % count
     angle = 2.0 * math.pi / count * turns.astype(jnp.float32)
     return (jnp.cos(angle) + jnp.sin(angle)) / math.sqrt(count)
+
+
+def exchange_kernel(axis, x_ref, y_ref, send_sems, recv_sems, own_sem):
+    ranks = x_ref.shape[0]
+    me = lax.axis_index(axis)
+    barrier = pltpu.get_barrier_semaphore()
+
+    def greet(i, carry):
+        peer = lax.rem(me + i, ranks)
+        pl.semaphore_signal(
+            barrier, inc=1, device_id={axis: peer}, device_id_type=pl.DeviceIdType.MESH
+        )
+        return carry
+
+    lax.fori_loop(1, ranks, greet, 0)
+    pl.semaphore_wait(barrier, ranks - 1)
+
+    own = pltpu.make_async_copy(x_ref.at[me], y_ref.at[me], own_sem)
+    own.start()
+
+    def copy_to(peer):
+        return pltpu.make_async_remote_copy(
+            src_ref=x_ref.at[peer],
+            dst_ref=y_ref.at[me],
+            send_sem=send_sems.at[peer],
+            recv_sem=recv_sems.at[me],
+            device_id={axis: peer},
+            device_id_type=pl.DeviceIdType.MESH,
+        )
+
+    def send(i, carry):
+        copy_to(lax.rem(me + i, ranks)).start()
+        return carry
+
+    lax.fori_loop(1, ranks, send, 0)
+
+    def wait(i, carry):
+        copy_to(lax.rem(me + i, ranks)).wait_send()
+        source = lax.rem(me + ranks - i, ranks)
+        pltpu.make_async_remote_copy(
+            src_ref=x_ref.at[source],
+            dst_ref=y_ref.at[source],
+            send_sem=send_sems.at[source],
+            recv_sem=recv_sems.at[source],
+            device_id={axis: source},
+            device_id_type=pl.DeviceIdType.MESH,
+        ).wait_recv()
+        return carry
+
+    lax.fori_loop(1, ranks, wait, 0)
+    own.wait()
+
+
+def exchange(x, axis, collective_id):
+    ranks = x.shape[0]
+    return pl.pallas_call(
+        functools.partial(exchange_kernel, axis),
+        out_shape=jax.ShapeDtypeStruct(x.shape, x.dtype),
+        in_specs=[pl.BlockSpec(memory_space=pl.ANY)],
+        out_specs=pl.BlockSpec(memory_space=pl.ANY),
+        scratch_shapes=[
+            pltpu.SemaphoreType.DMA((ranks,)),
+            pltpu.SemaphoreType.DMA((ranks,)),
+            pltpu.SemaphoreType.DMA,
+        ],
+        compiler_params=pltpu.CompilerParams(collective_id=collective_id, has_side_effects=True),
+    )(x)
 
 
 def finish_kernel(field_ref, back_ref, lon_ref, local_ref, bias_ref, gate_ref, up_ref, down_ref, out_ref):
@@ -99,7 +167,7 @@
     )
     per = lon_modes // ranks
     along = jnp.einsum("xm,blncx->mblnc", lon_table, field, preferred_element_type=jnp.float32)
-    along = lax.all_to_all(along.reshape((ranks, per) + along.shape[1:]), "rows", 0, 0, tiled=True)
+    along = exchange(along.reshape((ranks, per) + along.shape[1:]), "rows", 0)
     modes = jnp.einsum("sjblnc,snk->jblkc", along, lat_table, precision=high)
     modes = modes.astype(jnp.bfloat16)
     padded = extended(modes, (("lev", 2),), 1)
@@ -125,7 +193,7 @@
     values = jnp.einsum(
         "rnk,jblko->rjblno", lat_table, mixed_b.astype(jnp.float32), precision=high
     )
-    values = lax.all_to_all(values.astype(jnp.bfloat16), "rows", 0, 0, tiled=True)
+    values = exchange(values.astype(jnp.bfloat16), "rows", 1)
     back_b = jnp.transpose(values, (2, 3, 4, 5, 0, 1)).reshape(
         batch, levels, lat_rows, chans, lon_modes
     )

time: 107 us -> 120 us (1.12); the launches traced: 106 us -> 118 us
  Pallas kernels: 27.6 us -> 83.2 us
  waiting for transfers between devices: 19.7 us -> 0.01 us
  starting transfers between devices: 24.9 us -> 5.46 us
  local copies, waits for them, and re-layouts: 17.4 us -> 13.5 us
    pallas_call x0 -> x2, Pallas kernels: none -> 55.6 us  [exchange(): pl.pallas_call(functools.partial(exchange_kernel, axis), out_shape=jax.Sh...]
    all_to_all x2 -> x0, waiting for transfers between devices: 19.7 us -> none  [the longest x1 10.1 us: body(): lax.all_to_all(values.astype(jnp.bfloat16), 'rows', 0, 0, tiled=True)]
    all_to_all x2 -> x0, starting transfers between devices: 19.4 us -> none  [the longest x1 11.8 us: body(): lax.all_to_all(along.reshape((ranks, per) + along.shape[1:]), 'rows', 0,...]
    unnamed x19 -> x13, local copies, waits for them, and re-layouts: 6.5 us -> 2.14 us
    all_to_all x1 -> x0, other arithmetic: 1.92 us -> none  [body(): lax.all_to_all(along.reshape((ranks, per) + along.shape[1:]), 'rows', 0,...]
    dot_general x1, matrix products: 2.23 us -> 0.66 us  [body(): jnp.einsum('kjco,jblkc->jblko', spectral_weight[1], padded[:, :, 1:levels...]
    dot_general x1, matrix products: 0.67 us -> 2.24 us  [body(): jnp.einsum('kjco,jblkc->jblko', spectral_weight[2], padded[:, :, 2:levels...]
  transfers between devices with their start and end apart: 4 -> 2, of which waited for: 2 -> 0; matrix products, arithmetic and copies ran while one was open for 12% -> 11% of each run, Pallas kernels for 0% -> 0%
where the time goes in v5:
time: 120 us; the launch traced here: 118 us
  Pallas kernels  83.2 us (69%)
  local copies, waits for them, and re-layouts  13.5 us (11%)
  matrix products  13 us (11%)
  starting transfers between devices  5.46 us (5%)
  other arithmetic  2.36 us (2%)
    pallas_call x2, Pallas kernels, exchange(): pl.pallas_call(functools.partial(exchange_kernel, axis), out_shape=jax.Sh...  55.6 us
    pallas_call x1, Pallas kernels, finish(): pl.pallas_call(finish_kernel, out_shape=jax.ShapeDtypeStruct(field.shape,...  27.6 us
    slice x1, local copies, waits for them, and re-layouts, body(): spectral_weight[0]  6.64 us
    dot_general x1, matrix products, body(): jnp.einsum('xm,blncx->mblnc', lon_table, field, preferred_element_type=jn...  4.29 us
    dot_general x1, matrix products, body(): modes = jnp.einsum('sjblnc,snk->jblkc', along, lat_table, precision=high)  3.69 us
    ppermute x1, starting transfers between devices, extended(): lax.ppermute(head, axis, [((i + 1) % count, i) for i in range(ends)])  3.27 us
  transfers between devices with their start and end apart: 2, of which 0 were waited for; matrix products, arithmetic and copies ran while one was open for 11% of the time, Pallas kernels for 0%

profile of v5, /device:TPU:25, one launch (start us, length us, event | category | flops | bytes accessed | tf_op | source)
XLA Modules:
  0.0 117.6 jit_solution(18139625791525803862)
XLA Ops:
  0.0 1.2 %multiply_convert_fusion.lon_ref = bf16[64,1024]{1,0:T(8,128)(2,1)S(1)} fusion(s32[64]{0:T(128)S(1)} %iota_add_fusion), kind=kLoop, calls=%fused_computation.34 | loop fusion | flops 1114112 | bytes 131328 | tf_op jit(solution)/shard_map/convert_element_type | solution.py:162
  1.3 0.0 copy-start
  1.3 0.1 convert_element_type.67
  1.3 4.3 %fusion = f32[32,2,2,16,64]{4,0,3,2,1:T(8,128)S(1)} fusion(bf16[2,1,16,64,1024]{4,3,2,1,0:T(8,128)(2,1)} %param.7, bf16[32,2,1024,1,1]{2,1,0,4,3:T(2,128)(2,1)S(1)} %bitcast.73), kind=kOutput, calls=%fused_computation | convolution fusion | flops 268435456 | bytes 4849664 | tf_op jit(solution)/shard_map/xm,blncx->mblnc/dot_general | solution.py:169
  5.6 0.0 copy-done
  5.6 1.6 %copy.83 = f32[32,2,2,16,64]{4,3,2,1,0:T(8,128)} copy(f32[32,2,2,16,64]{4,0,3,2,1:T(8,128)S(1)} %fusion) | data formatting | bytes 1048576 | tf_op jit(solution)/shard_map/xm,blncx->mblnc/dot_general | solution.py:169
  7.2 34.2 %shard_map.73 = f32[32,2,2,1,16,64]{5,4,3,2,1,0:T(8,128)} custom-call(f32[32,2,2,1,16,64]{5,4,3,2,1,0:T(8,128)} %bitcast.70), custom_call_target="tpu_custom_call" | custom-call | tf_op jit(solution)/shard_map/pallas_call | solution.py:89
  41.4 3.7 %fusion.9 = bf16[64,2,2,64]{3,0,2,1:T(8,128)(2,1)S(1)} fusion(f32[32,2,2,16,64]{4,3,2,1,0:T(8,128)} %bitcast.72, s32[64]{0:T(128)S(1)} %iota_add_fusion, s32[32,16]{0,1:T(8,128)S(1)} %multiply_add_fusion), kind=kOutput, calls=%fused_computation.14 | convolution fusion | flops 101203968 | bytes 559360 | tf_op jit(solution)/shard_map/sjblnc,snk->jblkc/dot_general | solution.py:171
  45.1 3.3 %collective-permute-start.1 = (bf16[2,2,1,64,64]{4,3,1,0,2:T(8,128)(2,1)S(1)}, bf16[2,2,1,64,64]{4,3,1,0,2:T(8,128)(2,1)S(1)}, u32[]{:S(2)}, u32[]{:S(2)}) collective-permute-start(bf16[2,2,1,64,64]{4,3,1,0,2:T(8,128)(2,1)S(1)} %bitcast.78), channel_id=1, source_target_pairs={{1,0},{2,1},{3,2},{4,3},{5,4},{6,5},{7,6},{9,8},{10,9},{11,10},{12... | collective-permute-start | bytes 98312 | tf_op jit(solution)/shard_map/ppermute | solution.py:22
  48.4 2.2 %collective-permute-start = (bf16[2,2,1,64,64]{4,3,1,0,2:T(8,128)(2,1)S(1)}, bf16[2,2,1,64,64]{4,3,1,0,2:T(8,128)(2,1)S(1)}, u32[]{:S(2)}, u32[]{:S(2)}) collective-permute-start(bf16[2,2,1,64,64]{4,3,1,0,2:T(8,128)(2,1)S(1)} %bitcast.79), channel_id=1, source_target_pairs={{0,1},{1,2},{2,3},{3,4},{4,5},{5,6},{6,7},{8,9},{9,10},{10,11},{11... | collective-permute-start | bytes 98312 | tf_op jit(solution)/shard_map/ppermute | solution.py:20
  50.6 6.6 %fusion.35 = (bf16[1,64,2,64,64]{4,3,2,1,0:T(8,128)(2,1)S(1)}, bf16[1,64,2,64,64]{4,3,2,1,0:T(8,128)(2,1)S(1)}, bf16[1,64,2,64,64]{4,3,2,1,0:T(8,128)(2,1)}) fusion(bf16[3,64,2,64,64]{4,3,2,1,0:T(8,128)(2,1)} %param.8), kind=kLoop, calls=%fused_computation.53 | loop fusion | bytes 6291456 | tf_op jit(solution)/shard_map/slice | solution.py:176
  57.2 0.0 copy-start.1
  57.2 0.0 copy-start.4
  57.2 0.0 copy-start.3
  57.2 0.7 fusion.3
  57.9 1.1 fusion.24
  59.0 0.0 copy-done.1
  59.0 0.7 copy.37
  59.7 0.0 copy-done.2
  59.7 0.7 copy.38
  60.4 0.0 copy-done.4
  60.4 0.7 copy.40.bias_ref
  61.1 0.0 copy-done.3
  61.1 0.7 copy.36
  61.8 0.0 collective-permute-done.1
  61.8 2.2 %fusion.2 = f32[2,64,2,64]{3,2,1,0:T(2,128)S(1)} fusion(bf16[1,64,2,64,64]{4,3,2,1,0:T(8,128)(2,1)} %get-tuple-element.7, bf16[2,2,64,64]{3,2,1,0:T(8,128)(2,1)S(1)} %bitcast.82), kind=kOutput, calls=%fused_computation.3 | convolution fusion | flops 2097152 | bytes 1146880 | tf_op jit(solution)/shard_map/kjco,jblkc->jblko/dot_general | solution.py:186
  64.1 0.0 collective-permute-done
  64.1 0.7 fusion.10
  64.8 1.4 %fusion.5.x_ref = bf16[32,2,2,1,16,64]{5,4,3,2,1,0:T(8,128)(2,1)} fusion(f32[32,16,64,1,1]{2,0,1,3,4:T(8,128)S(1)} %fusion.24, bf16[2,2,64,64]{3,1,2,0:T(2,128)(2,1)S(1)} %fusion.10), kind=kOutput, calls=%fused_computation.9 | convolution fusion | flops 100794368 | bytes 425984 | tf_op jit(solution)/shard_map/rnk,jblko->rjblno/dot_general | solution.py:193
  66.2 21.4 %shard_map.74 = bf16[32,2,2,1,16,64]{5,4,3,2,1,0:T(8,128)(2,1)} custom-call(bf16[32,2,2,1,16,64]{5,4,3,2,1,0:T(8,128)(2,1)} %fusion.5.x_ref), custom_call_target="tpu_custom_call" | custom-call | tf_op jit(solution)/shard_map/pallas_call | solution.py:89
  87.6 2.4 %copy.39.back_ref = bf16[32,64,64]{2,1,0:T(8,128)(2,1)} copy(bf16[32,64,64]{1,0,2:T(8,128)(2,1)} %bitcast.71) | data formatting | bytes 524288 | tf_op jit(solution)/shard_map/reshape;reshape | solution.py:203
  90.0 27.6 %shard_map.75 = bf16[32,64,1024]{2,1,0:T(8,128)(2,1)} custom-call(bf16[32,64,1024]{2,1,0:T(8,128)(2,1)} %bitcast.69, bf16[32,64,64]{2,1,0:T(8,128)(2,1)} %copy.39.back_ref, bf16[64,1024]{1,0:T(8,128)(2,1)} %copy-done, bf16[64,64]{1,0:T(8,128)(2,1)} %bitcast.76, f32[64,1]{1,0:T(8,128)} %copy.40.bias_ref, bf16[256,64]{1,0:T(8,128)(2,1)} %bitcast.74, ...), custom_call_target="tpu_custom_call" | custom-call | flops 3758096384 | bytes 8650752 | tf_op jit(solution)/shard_map/pallas_call | solution.py:123
  (3 shorter events, 0.0 us)
Async XLA Ops:
  1.3 4.4 %copy-start = (bf16[64,1024]{1,0:T(8,128)(2,1)}, bf16[64,1024]{1,0:T(8,128)(2,1)S(1)}, u32[]{:S(2)}) copy-start(bf16[64,1024]{1,0:T(8,128)(2,1)S(1)} %multiply_convert_fusion.lon_ref) | copy-start | bytes 393220
  45.1 16.8 %collective-permute-start.1 = (bf16[2,2,1,64,64]{4,3,1,0,2:T(8,128)(2,1)S(1)}, bf16[2,2,1,64,64]{4,3,1,0,2:T(8,128)(2,1)S(1)}, u32[]{:S(2)}, u32[]{:S(2)}) collective-permute-start(bf16[2,2,1,64,64]{4,3,1,0,2:T(8,128)(2,1)S(1)} %bitcast.78), channel_id=1, source_target_pairs={{1,0},{2,1},{3,2},{4,3},{5,4},{6,5},{7,6},{9,8},{10,9},{11,10},{12... | collective-permute-start | bytes 98312 | tf_op jit(solution)/shard_map/ppermute | solution.py:22
  48.4 15.7 %collective-permute-start = (bf16[2,2,1,64,64]{4,3,1,0,2:T(8,128)(2,1)S(1)}, bf16[2,2,1,64,64]{4,3,1,0,2:T(8,128)(2,1)S(1)}, u32[]{:S(2)}, u32[]{:S(2)}) collective-permute-start(bf16[2,2,1,64,64]{4,3,1,0,2:T(8,128)(2,1)S(1)} %bitcast.79), channel_id=1, source_target_pairs={{0,1},{1,2},{2,3},{3,4},{4,5},{5,6},{6,7},{8,9},{9,10},{10,11},{11... | collective-permute-start | bytes 98312 | tf_op jit(solution)/shard_map/ppermute | solution.py:20
  57.2 1.8 %copy-start.1 = (bf16[64,256]{1,0:T(8,128)(2,1)S(1)}, bf16[64,256]{1,0:T(8,128)(2,1)}, u32[]{:S(2)}) copy-start(bf16[64,256]{1,0:T(8,128)(2,1)} %param.11) | copy-start | bytes 98308
  57.2 2.5 %copy-start.2 = (bf16[64,256]{1,0:T(8,128)(2,1)S(1)}, bf16[64,256]{1,0:T(8,128)(2,1)}, u32[]{:S(2)}) copy-start(bf16[64,256]{1,0:T(8,128)(2,1)} %param.12) | copy-start | bytes 98308
  57.2 3.2 %copy-start.4 = (f32[64]{0:T(128)S(1)}, f32[64]{0:T(128)}, u32[]{:S(2)}) copy-start(f32[64]{0:T(128)} %param.10) | copy-start | bytes 772
  57.2 3.9 %copy-start.3 = (bf16[64,64]{1,0:T(8,128)(2,1)S(1)}, bf16[64,64]{1,0:T(8,128)(2,1)}, u32[]{:S(2)}) copy-start(bf16[64,64]{1,0:T(8,128)(2,1)} %param.9) | copy-start | bytes 24580

commit v6 on v4

v6 whole, which is shorter than its diff:
```python
import math

import jax
import jax.numpy as jnp
from jax import lax
from jax.experimental import pallas as pl
from jax.experimental.pallas import tpu as pltpu
from jax.sharding import PartitionSpec as P


def extended(cells, sides, width):
    for axis, dim in sides:
        count = lax.axis_size(axis)
        ends = count - 1
        head = lax.slice_in_dim(cells, 0, width, axis=dim)
        tail = lax.slice_in_dim(cells, cells.shape[dim] - width, cells.shape[dim], axis=dim)
        cells = jnp.concatenate(
            [
                lax.ppermute(tail, axis, [(i, (i + 1) % count) for i in range(ends)]),
                cells,
                lax.ppermute(head, axis, [((i + 1) % count, i) for i in range(ends)]),
            ],
            axis=dim,
        )
    return cells


def cas_rows(positions, count, modes):
    freq = jnp.arange(modes, dtype=jnp.int32) - modes // 2
    turns = positions[:, None] * freq[None, :] % count
    angle = 2.0 * math.pi / count * turns.astype(jnp.float32)
    return (jnp.cos(angle) + jnp.sin(angle)) / math.sqrt(count)


def finish_kernel(field_ref, back_ref, lon_ref, local_ref, bias_ref, gate_ref, up_ref, down_ref, *rest):
    out_ref = rest[-1]
    sqrt_half = math.sqrt(0.5)
    for r in range(field_ref.shape[0]):
        grid = field_ref[r]
        spectral = jnp.dot(back_ref[r], lon_ref[...], preferred_element_type=jnp.float32)
        local = jnp.dot(local_ref[...], grid, preferred_element_type=jnp.float32)
        value = spectral + local + bias_ref[...]
        act = (0.5 * value * (1.0 + lax.erf(value * sqrt_half))).astype(jnp.bfloat16)
        gate = jnp.dot(gate_ref[...], act, preferred_element_type=jnp.float32)
        upper = jnp.dot(up_ref[...], act, preferred_element_type=jnp.float32)
        hidden = (gate / (1.0 + jnp.exp(-gate)) * upper).astype(jnp.bfloat16)
        down = jnp.dot(down_ref[...], hidden, preferred_element_type=jnp.float32)
        out_ref[r] = (grid.astype(jnp.float32) + down).astype(out_ref.dtype)


def finish(field, back, lon_table, local_weight, local_bias, gate_weight, up_weight, down_weight, start, prev=None, block=2):
    rows, chans, lon_cells = field.shape
    part, _, modes = back.shape
    hid = gate_weight.shape[1]
    whole = lambda i: (0, 0)
    shift = start // block
    in_specs = [
        pl.BlockSpec((block, chans, lon_cells), lambda i: (i + shift, 0, 0)),
        pl.BlockSpec((block, chans, modes), lambda i: (i, 0, 0)),
        pl.BlockSpec((modes, lon_cells), whole),
        pl.BlockSpec((chans, chans), whole),
        pl.BlockSpec((chans, 1), whole),
        pl.BlockSpec((hid, chans), whole),
        pl.BlockSpec((hid, chans), whole),
        pl.BlockSpec((chans, hid), whole),
    ]
    args = [
        field,
        back,
        lon_table.T,
        local_weight.T,
        local_bias.reshape(chans, 1),
        gate_weight.T,
        up_weight.T,
        down_weight.T,
    ]
    aliases = {}
    if prev is not None:
        in_specs.append(pl.BlockSpec(memory_space=pl.ANY))
        args.append(prev)
        aliases = {len(args) - 1: 0}
    return pl.pallas_call(
        finish_kernel,
        out_shape=jax.ShapeDtypeStruct(field.shape, field.dtype),
        grid=(part // block,),
        in_specs=in_specs,
        out_specs=pl.BlockSpec((block, chans, lon_cells), lambda i: (i + shift, 0, 0)),
        input_output_aliases=aliases,
        cost_estimate=pl.CostEstimate(
            flops=2 * part * lon_cells * chans * (modes + chans + 3 * hid),
            transcendentals=part * lon_cells * (chans + 2 * hid),
            bytes_accessed=4 * part * chans * lon_cells + 2 * back.size,
        ),
    )(*args)


def body(field, spectral_weight, local_weight, local_bias, gate_weight, up_weight, down_weight):
    high = lax.Precision.HIGHEST
    batch, levels, lat_rows, chans, lon_cells = field.shape
    ranks = lax.axis_size("rows")
    lat_total = lat_rows * ranks
    lat_modes = spectral_weight.shape[1]
    lon_modes = spectral_weight.shape[2] * ranks
    lon_table = cas_rows(jnp.arange(lon_cells, dtype=jnp.int32), lon_cells, lon_modes).astype(
        jnp.bfloat16
    )
    lat_table = cas_rows(jnp.arange(lat_total, dtype=jnp.int32), lat_total, lat_modes).reshape(
        ranks, lat_rows, lat_modes
    )
    per = lon_modes // ranks

    def synthesis(grid):
        along = jnp.einsum("xm,blncx->mblnc", lon_table, grid, preferred_element_type=jnp.float32)
        along = lax.all_to_all(
            along.reshape((ranks, per) + along.shape[1:]), "rows", 0, 0, tiled=True
        )
        modes = jnp.einsum("sjblnc,snk->jblkc", along, lat_table, precision=high)
        modes = modes.astype(jnp.bfloat16)
        padded = extended(modes, (("lev", 2),), 1)
        mixed = jnp.einsum(
            "kjco,jblkc->jblko",
            spectral_weight[0],
            padded[:, :, 0:levels],
            preferred_element_type=jnp.float32,
        )
        mixed = mixed + jnp.einsum(
            "kjco,jblkc->jblko",
            spectral_weight[1],
            padded[:, :, 1 : levels + 1],
            preferred_element_type=jnp.float32,
        )
        mixed = mixed + jnp.einsum(
            "kjco,jblkc->jblko",
            spectral_weight[2],
            padded[:, :, 2 : levels + 2],
            preferred_element_type=jnp.float32,
        )
        mixed_b = mixed.astype(jnp.bfloat16)
        values = jnp.einsum(
            "rnk,jblko->rjblno", lat_table, mixed_b.astype(jnp.float32), precision=high
        )
        return values.astype(jnp.bfloat16)

    def arrive(values):
        values = lax.all_to_all(values, "rows", 0, 0, tiled=True)
        back_b = jnp.transpose(values, (2, 3, 4, 5, 0, 1))
        return back_b.reshape(-1, chans, lon_modes)

    rows = field.reshape(batch * levels * lat_rows, chans, lon_cells)
    result = None
    sent = [synthesis(field[0:1])]
    for sample in range(batch):
        back_b = arrive(sent[sample])
        if sample + 1 < batch:
            following = synthesis(field[sample + 1 : sample + 2])
            back_b, following = lax.optimization_barrier((back_b, following))
            sent.append(following)
        result = finish(
            rows,
            back_b,
            lon_table,
            local_weight,
            local_bias,
            gate_weight,
            up_weight,
            down_weight,
            sample * levels * lat_rows,
            result,
        )
    return result.reshape(batch, levels, lat_rows, chans, lon_cells)


def solution(mesh):
    return jax.shard_map(
        body,
        mesh=mesh,
        in_specs=(
            P(None, "lev", "rows", None, None),
            P(None, None, "rows", None, None),
            P(),
            P(),
            P(),
            P(),
            P(),
        ),
        out_specs=P(None, "lev", "rows", None, None),
        check_vma=False,
    )
```

time: 107 us -> 131 us (1.22)
  starting transfers between devices: 24.9 us -> 42.4 us
  matrix products: 13.6 us -> 18.3 us
  waiting for transfers between devices: 19.7 us -> 17.3 us
  Pallas kernels: 27.6 us -> 29.4 us
    all_to_all x2 -> x4, starting transfers between devices: 19.4 us -> 31.6 us  [the longest x2 15.9 us: synthesis(): lax.all_to_all(along.reshape((ranks, per) + along.shape[1:]), 'rows', 0,...]
    slice x1 -> x0, local copies, waits for them, and re-layouts: 7.35 us -> none  [body(): spectral_weight[0]]
    squeeze x0 -> x1, local copies, waits for them, and re-layouts: none -> 7.31 us  [synthesis(): spectral_weight[1]]
    dot_general x6 -> x12, matrix products: 13.6 us -> 18.3 us  [the longest x2 5.42 us: synthesis(): jnp.einsum('xm,blncx->mblnc', lon_table, grid, preferred_element_type=jnp...]
    ppermute x1 -> x2, starting transfers between devices: 2.4 us -> 5.69 us  [extended(): lax.ppermute(head, axis, [((i + 1) % count, i) for i in range(ends)])]
    all_to_all x2 -> x4, waiting for transfers between devices: 19.7 us -> 17.2 us  [the longest x2 8.88 us: synthesis(): lax.all_to_all(along.reshape((ranks, per) + along.shape[1:]), 'rows', 0,...]
    ppermute x1 -> x2, starting transfers between devices: 3.06 us -> 5.04 us  [extended(): lax.ppermute(tail, axis, [(i, (i + 1) % count) for i in range(ends)])]
    pallas_call x1 -> x2, Pallas kernels: 27.6 us -> 29.4 us  [finish(): pl.pallas_call(finish_kernel, out_shape=jax.ShapeDtypeStruct(field.shape,...]
  transfers between devices with their start and end apart: 4 -> 8, of which waited for: 2 -> 2; matrix products, arithmetic and copies ran while one was open for 12% -> 25% of each run, Pallas kernels for 0% -> 11%
where the time goes in v6:
time: 131 us; the launch traced here: 130 us
  starting transfers between devices  42.4 us (32%)
  Pallas kernels  29.4 us (22%)
  matrix products  18.3 us (14%)
  local copies, waits for them, and re-layouts  18.2 us (14%)
  waiting for transfers between devices  17.3 us (13%)
  other arithmetic  3.86 us (3%)
    pallas_call x2, Pallas kernels, finish(): pl.pallas_call(finish_kernel, out_shape=jax.ShapeDtypeStruct(field.shape,...  29.4 us
    all_to_all x2, starting transfers between devices, synthesis(): lax.all_to_all(along.reshape((ranks, per) + along.shape[1:]), 'rows', 0,...  15.9 us
    all_to_all x2, starting transfers between devices, arrive(): values = lax.all_to_all(values, 'rows', 0, 0, tiled=True)  15.7 us
    all_to_all x2, waiting for transfers between devices, synthesis(): lax.all_to_all(along.reshape((ranks, per) + along.shape[1:]), 'rows', 0,...  8.88 us
    all_to_all x2, waiting for transfers between devices, arrive(): values = lax.all_to_all(values, 'rows', 0, 0, tiled=True)  8.37 us
    squeeze x1, local copies, waits for them, and re-layouts, synthesis(): spectral_weight[1]  7.31 us
    unnamed x25, local copies, waits for them, and re-layouts  6.81 us
    ppermute x2, starting transfers between devices, extended(): lax.ppermute(head, axis, [((i + 1) % count, i) for i in range(ends)])  5.69 us
  transfers between devices with their start and end apart: 8, of which 2 were waited for; matrix products, arithmetic and copies ran while one was open for 25% of the time, Pallas kernels for 11%

profile of v6, /device:TPU:25, one launch (start us, length us, event | category | flops | bytes accessed | tf_op | source)
XLA Modules:
  0.0 129.7 jit_solution(2775775855529600783)
XLA Ops:
  0.0 1.2 multiply_convert_fusion.lon_ref
  1.3 2.7 %fusion.21 = f32[32,2,1,1,16,64]{5,0,4,1,3,2:T(8,128)S(1)} fusion(bf16[2,1,16,64,1024]{4,3,2,1,0:T(8,128)(2,1)} %param.7, bf16[32,2,1024,1]{2,1,0,3:T(2,128)(2,1)S(1)} %bitcast.150), kind=kOutput, calls=%fused_computation.22 | convolution fusion | flops 134217728 | bytes 2490368 | tf_op jit(solution)/shard_map/xm,blncx->mblnc/dot_general | solution.py:113
  4.3 1.0 reshape.208
  5.4 11.8 %all-to-all-start.2 = ((f32[32,1,2048]{2,1,0:T(1,128)}), f32[32,1,2048]{2,1,0:T(1,128)S(1)}, u32[]{:S(2)}, u32[]{:S(2)}) async-start(f32[32,1,2048]{2,1,0:T(1,128)} %reshape.208), calls=%async_computation.2 | async-start | bytes 524288 | tf_op jit(solution)/shard_map/all_to_all | solution.py:114
  17.1 2.7 %fusion.18 = f32[32,2,1,1,16,64]{5,0,4,1,3,2:T(8,128)S(1)} fusion(bf16[2,1,16,64,1024]{4,3,2,1,0:T(8,128)(2,1)} %param.7, bf16[32,2,1024,1]{2,1,0,3:T(2,128)(2,1)S(1)} %bitcast.151), kind=kOutput, calls=%fused_computation.21 | convolution fusion | flops 134217728 | bytes 2490368 | tf_op jit(solution)/shard_map/xm,blncx->mblnc/dot_general | solution.py:113
  20.2 1.0 reshape.204
  21.2 8.9 %all-to-all-done.2 = f32[32,1,2048]{2,1,0:T(1,128)S(1)} async-done(((f32[32,1,2048]{2,1,0:T(1,128)}), f32[32,1,2048]{2,1,0:T(1,128)S(1)}, u32[]{:S(2)}, u32[]{:S(2)}) %all-to-all-start.2) | async-done | bytes 262176 | tf_op jit(solution)/shard_map/all_to_all | solution.py:114
  30.1 4.1 %all-to-all-start = ((f32[32,1,2048]{2,1,0:T(1,128)}), f32[32,1,2048]{2,1,0:T(1,128)S(1)}, u32[]{:S(2)}, u32[]{:S(2)}) async-start(f32[32,1,2048]{2,1,0:T(1,128)} %reshape.204), calls=%async_computation | async-start | bytes 524288 | tf_op jit(solution)/shard_map/all_to_all | solution.py:114
  34.2 7.3 %slice_bitcast_fusion.1 = (bf16[64,2,64,64]{3,2,1,0:T(8,128)(2,1)}, bf16[64,2,64,64]{3,2,1,0:T(8,128)(2,1)}, bf16[64,2,64,64]{3,2,1,0:T(8,128)(2,1)S(1)}) fusion(bf16[3,64,2,64,64]{4,3,2,1,0:T(8,128)(2,1)} %param.8), kind=kLoop, calls=%fused_computation.6 | loop fusion | bytes 6291456 | tf_op jit(solution)/shard_map/squeeze | solution.py:128
  42.1 1.3 %reduce.1 = f32[32,2048]{1,0:T(8,128)S(1)} reduce(f32[32,1,2048]{2,1,0:T(1,128)S(1)} %all-to-all-done.2, f32[]{:T(128)} %broadcast.198), dimensions={1}, to_apply=%all_to_all.14.reduce_sub_computation | reduce | bytes 524292 | tf_op jit(solution)/shard_map/all_to_all | solution.py:114
  43.7 1.9 %fusion.27 = bf16[64,2,64]{2,0,1:T(8,128)(2,1)S(1)} fusion(f32[32,2,1,1,16,64]{5,4,1,3,2,0:T(8,128)S(1)} %bitcast.148, s32[64]{0:T(128)S(1)} %iota_add_fusion, s32[32,16]{0,1:T(8,128)S(1)} %multiply_add_fusion), kind=kOutput, calls=%fused_computation.30 | convolution fusion | flops 50864128 | bytes 280832 | tf_op jit(solution)/shard_map/sjblnc,snk->jblkc/dot_general | solution.py:117
  45.6 2.4 %collective-permute-start.3 = (bf16[2,1,1,64,64]{4,3,0,2,1:T(8,128)(2,1)S(1)}, bf16[2,1,1,64,64]{4,3,0,2,1:T(8,128)(2,1)S(1)}, u32[]{:S(2)}, u32[]{:S(2)}) collective-permute-start(bf16[2,1,1,64,64]{4,3,0,2,1:T(8,128)(2,1)S(1)} %bitcast.164), channel_id=1, source_target_pairs={{1,0},{2,1},{3,2},{4,3},{5,4},{6,5},{7,6},{9,8},{10,9},{11,10},{12... | collective-permute-start | bytes 49160 | tf_op jit(solution)/shard_map/ppermute | solution.py:21
  48.0 2.9 %collective-permute-start.2 = (bf16[2,1,1,64,64]{4,3,0,2,1:T(8,128)(2,1)S(1)}, bf16[2,1,1,64,64]{4,3,0,2,1:T(8,128)(2,1)S(1)}, u32[]{:S(2)}, u32[]{:S(2)}) collective-permute-start(bf16[2,1,1,64,64]{4,3,0,2,1:T(8,128)(2,1)S(1)} %bitcast.165), channel_id=1, source_target_pairs={{0,1},{1,2},{2,3},{3,4},{4,5},{5,6},{6,7},{8,9},{9,10},{10,11},{11... | collective-permute-start | bytes 49160 | tf_op jit(solution)/shard_map/ppermute | solution.py:19
  50.9 1.3 %reduce = f32[32,2048]{1,0:T(8,128)S(1)} reduce(f32[32,1,2048]{2,1,0:T(1,128)S(1)} %all-to-all-done, f32[]{:T(128)} %broadcast.198), dimensions={1}, to_apply=%all_to_all.12.reduce_sub_computation | reduce | bytes 524292 | tf_op jit(solution)/shard_map/all_to_all | solution.py:114
  52.4 1.9 %fusion.26 = bf16[64,2,64]{2,0,1:T(8,128)(2,1)S(1)} fusion(f32[32,2,1,1,16,64]{5,4,1,3,2,0:T(8,128)S(1)} %bitcast.149, s32[64]{0:T(128)S(1)} %iota_add_fusion, s32[32,16]{0,1:T(8,128)S(1)} %multiply_add_fusion), kind=kOutput, calls=%fused_computation.29 | convolution fusion | flops 50864128 | bytes 280832 | tf_op jit(solution)/shard_map/sjblnc,snk->jblkc/dot_general | solution.py:117
  54.4 3.3 %collective-permute-start.1 = (bf16[2,1,1,64,64]{4,3,0,2,1:T(8,128)(2,1)S(1)}, bf16[2,1,1,64,64]{4,3,0,2,1:T(8,128)(2,1)S(1)}, u32[]{:S(2)}, u32[]{:S(2)}) collective-permute-start(bf16[2,1,1,64,64]{4,3,0,2,1:T(8,128)(2,1)S(1)} %bitcast.169), channel_id=1, source_target_pairs={{1,0},{2,1},{3,2},{4,3},{5,4},{6,5},{7,6},{9,8},{10,9},{11,10},{12... | collective-permute-start | bytes 49160 | tf_op jit(solution)/shard_map/ppermute | solution.py:21
  57.7 2.2 %collective-permute-start = (bf16[2,1,1,64,64]{4,3,0,2,1:T(8,128)(2,1)S(1)}, bf16[2,1,1,64,64]{4,3,0,2,1:T(8,128)(2,1)S(1)}, u32[]{:S(2)}, u32[]{:S(2)}) collective-permute-start(bf16[2,1,1,64,64]{4,3,0,2,1:T(8,128)(2,1)S(1)} %bitcast.170), channel_id=1, source_target_pairs={{0,1},{1,2},{2,3},{3,4},{4,5},{5,6},{6,7},{8,9},{9,10},{10,11},{11... | collective-permute-start | bytes 49160 | tf_op jit(solution)/shard_map/ppermute | solution.py:19
  59.9 2.4 %fusion.10 = f32[2,64,1,64]{3,2,1,0:T(1,128)S(1)} fusion(bf16[64,2,64,64]{3,2,1,0:T(8,128)(2,1)} %get-tuple-element.9, bf16[2,64,64,1]{2,1,0,3:T(8,128)(2,1)S(1)} %bitcast.166), kind=kOutput, calls=%fused_computation.13 | convolution fusion | flops 1048576 | bytes 1097728 | tf_op jit(solution)/shard_map/kjco,jblkc->jblko/dot_general | solution.py:126
  64.9 1.7 %fusion.24 = bf16[32,2,1,1,16,64]{5,0,4,1,3,2:T(8,128)(2,1)S(1)} fusion(s32[64]{0:T(128)S(1)} %iota_add_fusion, s32[32,16]{0,1:T(8,128)S(1)} %multiply_add_fusion, f32[2,64,64]{2,1,0:T(8,128)S(1)} %bitcast.178, f32[2,64,64]{2,1,0:T(8,128)S(1)} %bitcast.176, f32[2,64,64]{2,1,0:T(8,128)S(1)} %bitcast.175), kind=kOutput, calls=%fused_computation.25 | convolution fusion | flops 50946048 | bytes 231680 | tf_op jit(solution)/shard_map/rnk,jblko->rjblno/dot_general | solution.py:139
  66.7 0.8 reshape.206
  67.6 12.0 %all-to-all-start.1 = ((bf16[32,2,1024]{2,1,0:T(2,128)(2,1)}), bf16[32,2,1024]{2,1,0:T(2,128)(2,1)S(1)}, u32[]{:S(2)}, u32[]{:S(2)}) async-start(bf16[32,2,1024]{2,1,0:T(2,128)(2,1)} %reshape.206), calls=%async_computation.1 | async-start | bytes 262144 | tf_op jit(solution)/shard_map/all_to_all | solution.py:145
  80.3 1.7 %fusion.25 = bf16[32,2,1,1,16,64]{5,0,4,1,3,2:T(8,128)(2,1)S(1)} fusion(s32[64]{0:T(128)S(1)} %iota_add_fusion, s32[32,16]{0,1:T(8,128)S(1)} %multiply_add_fusion, f32[2,64,64]{2,1,0:T(8,128)S(1)} %bitcast.177, f32[2,64,64]{2,1,0:T(8,128)S(1)} %bitcast.174, f32[2,64,64]{2,1,0:T(8,128)S(1)} %bitcast.173), kind=kOutput, calls=%fused_computation.26 | convolution fusion | flops 50946048 | bytes 231680 | tf_op jit(solution)/shard_map/rnk,jblko->rjblno/dot_general | solution.py:139
  82.0 8.4 %all-to-all-done.1 = bf16[32,2,1024]{2,1,0:T(2,128)(2,1)S(1)} async-done(((bf16[32,2,1024]{2,1,0:T(2,128)(2,1)}), bf16[32,2,1024]{2,1,0:T(2,128)(2,1)S(1)}, u32[]{:S(2)}, u32[]{:S(2)}) %all-to-all-start.1) | async-done | bytes 131104 | tf_op jit(solution)/shard_map/all_to_all | solution.py:145
  90.7 0.8 reshape.210
  91.5 3.7 %all-to-all-start.3 = ((bf16[32,2,1024]{2,1,0:T(2,128)(2,1)}), bf16[32,2,1024]{2,1,0:T(2,128)(2,1)S(1)}, u32[]{:S(2)}, u32[]{:S(2)}) async-start(bf16[32,2,1024]{2,1,0:T(2,128)(2,1)} %reshape.210), calls=%async_computation.3 | async-start | bytes 262144 | tf_op jit(solution)/shard_map/all_to_all | solution.py:145
  96.0 0.7 copy.47.bias_ref
  96.7 0.7 copy.42
  97.4 0.7 copy.43
  98.1 1.0 copy.44.back_ref
  99.1 14.7 %shard_map.73.rest_0_ = bf16[32,64,1024]{2,1,0:T(8,128)(2,1)} custom-call(bf16[32,64,1024]{2,1,0:T(8,128)(2,1)} %bitcast.159, bf16[16,64,64]{2,1,0:T(8,128)(2,1)} %copy.44.back_ref, bf16[64,1024]{1,0:T(8,128)(2,1)} %copy-done.2, bf16[64,64]{1,0:T(8,128)(2,1)} %bitcast.156, f32[64,1]{1,0:T(8,128)} %copy.47.bias_ref, bf16[256,64]{1,0:T(8,128)(2,1)} %bitcast.152, ...), custom_call_target="tpu_custom_call" | custom-call | flops 1879048192 | bytes 4325376 | tf_op jit(solution)/shard_map/pallas_call | solution.py:82
  114.0 1.0 copy.46.back_ref
  115.0 14.7 %shard_map.74 = bf16[32,64,1024]{2,1,0:T(8,128)(2,1)} custom-call(bf16[32,64,1024]{2,1,0:T(8,128)(2,1)} %bitcast.160, bf16[16,64,64]{2,1,0:T(8,128)(2,1)} %copy.46.back_ref, bf16[64,1024]{1,0:T(8,128)(2,1)} %copy-done.2, bf16[64,64]{1,0:T(8,128)(2,1)} %bitcast.157, f32[64,1]{1,0:T(8,128)} %copy.47.bias_ref, ...), custom_call_target="tpu_custom_call", output_to_operand_aliasing={{}: (8, {})} | custom-call | flops 1879048192 | bytes 4325376 | tf_op jit(solution)/shard_map/pallas_call | solution.py:82
  (38 shorter events, 6.4 us)
Async XLA Ops:
  1.2 3.1 %copy-start.2 = (bf16[64,1024]{1,0:T(8,128)(2,1)}, bf16[64,1024]{1,0:T(8,128)(2,1)S(1)}, u32[]{:S(2)}) copy-start(bf16[64,1024]{1,0:T(8,128)(2,1)S(1)} %multiply_convert_fusion.lon_ref) | copy-start | bytes 393220
  5.4 24.7 %all-to-all-start.2 = ((f32[32,1,2048]{2,1,0:T(1,128)}), f32[32,1,2048]{2,1,0:T(1,128)S(1)}, u32[]{:S(2)}, u32[]{:S(2)}) async-start(f32[32,1,2048]{2,1,0:T(1,128)} %reshape.208), calls=%async_computation.2 | async-start | bytes 524288 | tf_op jit(solution)/shard_map/all_to_all | solution.py:114
  30.1 20.8 %all-to-all-start = ((f32[32,1,2048]{2,1,0:T(1,128)}), f32[32,1,2048]{2,1,0:T(1,128)S(1)}, u32[]{:S(2)}, u32[]{:S(2)}) async-start(f32[32,1,2048]{2,1,0:T(1,128)} %reshape.204), calls=%async_computation | async-start | bytes 524288 | tf_op jit(solution)/shard_map/all_to_all | solution.py:114
  45.6 34.0 %collective-permute-start.3 = (bf16[2,1,1,64,64]{4,3,0,2,1:T(8,128)(2,1)S(1)}, bf16[2,1,1,64,64]{4,3,0,2,1:T(8,128)(2,1)S(1)}, u32[]{:S(2)}, u32[]{:S(2)}) collective-permute-start(bf16[2,1,1,64,64]{4,3,0,2,1:T(8,128)(2,1)S(1)} %bitcast.164), channel_id=1, source_target_pairs={{1,0},{2,1},{3,2},{4,3},{5,4},{6,5},{7,6},{9,8},{10,9},{11,10},{12... | collective-permute-start | bytes 49160 | tf_op jit(solution)/shard_map/ppermute | solution.py:21
  48.0 14.9 %collective-permute-start.2 = (bf16[2,1,1,64,64]{4,3,0,2,1:T(8,128)(2,1)S(1)}, bf16[2,1,1,64,64]{4,3,0,2,1:T(8,128)(2,1)S(1)}, u32[]{:S(2)}, u32[]{:S(2)}) collective-permute-start(bf16[2,1,1,64,64]{4,3,0,2,1:T(8,128)(2,1)S(1)} %bitcast.165), channel_id=1, source_target_pairs={{0,1},{1,2},{2,3},{3,4},{4,5},{5,6},{6,7},{8,9},{9,10},{10,11},{11... | collective-permute-start | bytes 49160 | tf_op jit(solution)/shard_map/ppermute | solution.py:19
  52.4 9.8 %copy-start.1 = (bf16[64,2,64,64]{3,2,1,0:T(8,128)(2,1)S(1)}, bf16[64,2,64,64]{3,2,1,0:T(8,128)(2,1)}, u32[]{:S(2)}) copy-start(bf16[64,2,64,64]{3,2,1,0:T(8,128)(2,1)} %get-tuple-element.9) | copy-start | bytes 3145732
  54.4 9.9 %collective-permute-start.1 = (bf16[2,1,1,64,64]{4,3,0,2,1:T(8,128)(2,1)S(1)}, bf16[2,1,1,64,64]{4,3,0,2,1:T(8,128)(2,1)S(1)}, u32[]{:S(2)}, u32[]{:S(2)}) collective-permute-start(bf16[2,1,1,64,64]{4,3,0,2,1:T(8,128)(2,1)S(1)} %bitcast.169), channel_id=1, source_target_pairs={{1,0},{2,1},{3,2},{4,3},{5,4},{6,5},{7,6},{9,8},{10,9},{11,10},{12... | collective-permute-start | bytes 49160 | tf_op jit(solution)/shard_map/ppermute | solution.py:21
  57.7 5.9 %collective-permute-start = (bf16[2,1,1,64,64]{4,3,0,2,1:T(8,128)(2,1)S(1)}, bf16[2,1,1,64,64]{4,3,0,2,1:T(8,128)(2,1)S(1)}, u32[]{:S(2)}, u32[]{:S(2)}) collective-permute-start(bf16[2,1,1,64,64]{4,3,0,2,1:T(8,128)(2,1)S(1)} %bitcast.170), channel_id=1, source_target_pairs={{0,1},{1,2},{2,3},{3,4},{4,5},{5,6},{6,7},{8,9},{9,10},{10,11},{11... | collective-permute-start | bytes 49160 | tf_op jit(solution)/shard_map/ppermute | solution.py:19
  59.8 3.1 %copy-start = (bf16[64,2,64,64]{3,2,1,0:T(8,128)(2,1)S(1)}, bf16[64,2,64,64]{3,2,1,0:T(8,128)(2,1)}, u32[]{:S(2)}) copy-start(bf16[64,2,64,64]{3,2,1,0:T(8,128)(2,1)} %get-tuple-element.10) | copy-start | bytes 3145732
  67.6 22.8 %all-to-all-start.1 = ((bf16[32,2,1024]{2,1,0:T(2,128)(2,1)}), bf16[32,2,1024]{2,1,0:T(2,128)(2,1)S(1)}, u32[]{:S(2)}, u32[]{:S(2)}) async-start(bf16[32,2,1024]{2,1,0:T(2,128)(2,1)} %reshape.206), calls=%async_computation.1 | async-start | bytes 262144 | tf_op jit(solution)/shard_map/all_to_all | solution.py:145
  79.6 15.7 %copy-start.5 = (bf16[64,64]{1,0:T(8,128)(2,1)S(1)}, bf16[64,64]{1,0:T(8,128)(2,1)}, u32[]{:S(2)}) copy-start(bf16[64,64]{1,0:T(8,128)(2,1)} %param.9) | copy-start | bytes 24580
  79.6 16.4 %copy-start.6 = (f32[64]{0:T(128)S(1)}, f32[64]{0:T(128)}, u32[]{:S(2)}) copy-start(f32[64]{0:T(128)} %param.10) | copy-start | bytes 772
  79.6 17.1 %copy-start.3 = (bf16[64,256]{1,0:T(8,128)(2,1)S(1)}, bf16[64,256]{1,0:T(8,128)(2,1)}, u32[]{:S(2)}) copy-start(bf16[64,256]{1,0:T(8,128)(2,1)} %param.11) | copy-start | bytes 98308
  80.3 17.1 %copy-start.4 = (bf16[64,256]{1,0:T(8,128)(2,1)S(1)}, bf16[64,256]{1,0:T(8,128)(2,1)}, u32[]{:S(2)}) copy-start(bf16[64,256]{1,0:T(8,128)(2,1)} %param.12) | copy-start | bytes 98308
  91.5 22.3 %all-to-all-start.3 = ((bf16[32,2,1024]{2,1,0:T(2,128)(2,1)}), bf16[32,2,1024]{2,1,0:T(2,128)(2,1)S(1)}, u32[]{:S(2)}, u32[]{:S(2)}) async-start(bf16[32,2,1024]{2,1,0:T(2,128)(2,1)} %reshape.210), calls=%async_computation.3 | async-start | bytes 262144 | tf_op jit(solution)/shard_map/all_to_all | solution.py:145

commit v7 on v4

--- a/solution.py
+++ b/solution.py
@@ -34,20 +34,24 @@
 
 def finish_kernel(field_ref, back_ref, lon_ref, local_ref, bias_ref, gate_ref, up_ref, down_ref, out_ref):
     sqrt_half = math.sqrt(0.5)
-    for r in range(field_ref.shape[0]):
-        grid = field_ref[r]
-        spectral = jnp.dot(back_ref[r], lon_ref[...], preferred_element_type=jnp.float32)
-        local = jnp.dot(local_ref[...], grid, preferred_element_type=jnp.float32)
-        value = spectral + local + bias_ref[...]
-        act = (0.5 * value * (1.0 + lax.erf(value * sqrt_half))).astype(jnp.bfloat16)
-        gate = jnp.dot(gate_ref[...], act, preferred_element_type=jnp.float32)
-        upper = jnp.dot(up_ref[...], act, preferred_element_type=jnp.float32)
-        hidden = (gate / (1.0 + jnp.exp(-gate)) * upper).astype(jnp.bfloat16)
-        down = jnp.dot(down_ref[...], hidden, preferred_element_type=jnp.float32)
-        out_ref[r] = (grid.astype(jnp.float32) + down).astype(out_ref.dtype)
+    rows, _, lon_cells = field_ref.shape
+    acts = []
+    for r in range(rows):
+        lhs = jnp.concatenate([back_ref[r], local_ref[...]], axis=1)
+        rhs = jnp.concatenate([lon_ref[...], field_ref[r]], axis=0)
+        value = jnp.dot(lhs, rhs, preferred_element_type=jnp.float32) + bias_ref[...]
+        acts.append((0.5 * value * (1.0 + lax.erf(value * sqrt_half))).astype(jnp.bfloat16))
+    act = jnp.concatenate(acts, axis=1)
+    gate = jnp.dot(gate_ref[...], act, preferred_element_type=jnp.float32)
+    upper = jnp.dot(up_ref[...], act, preferred_element_type=jnp.float32)
+    hidden = (0.5 * gate * (1.0 + jnp.tanh(0.5 * gate)) * upper).astype(jnp.bfloat16)
+    down = jnp.dot(down_ref[...], hidden, preferred_element_type=jnp.float32)
+    for r in range(rows):
+        grid = field_ref[r].astype(jnp.float32)
+        out_ref[r] = (grid + down[:, r * lon_cells : (r + 1) * lon_cells]).astype(out_ref.dtype)
 
 
-def finish(field, back, lon_table, local_weight, local_bias, gate_weight, up_weight, down_weight, block=2):
+def finish(field, back, lon_table, local_weight, local_bias, gate_weight, up_weight, down_weight, block=4):
     rows, chans, lon_cells = field.shape
     modes = back.shape[2]
     hid = gate_weight.shape[1]

time: 107 us -> 99.8 us (0.933)
  Pallas kernels: 27.6 us -> 20.6 us
    pallas_call x1, Pallas kernels: 27.6 us -> 20.6 us  [finish(): pl.pallas_call(finish_kernel, out_shape=jax.ShapeDtypeStruct(field.shape,...]
  transfers between devices with their start and end apart: 4 -> 4, of which waited for: 2 -> 2; matrix products, arithmetic and copies ran while one was open for 12% -> 13% of each run, Pallas kernels for 0% -> 0%
where the time goes in v7:
time: 99.8 us; the launch traced here: 99.4 us
  starting transfers between devices  24.9 us (25%)
  Pallas kernels  20.6 us (21%)
  waiting for transfers between devices  19.7 us (20%)
  local copies, waits for them, and re-layouts  17.4 us (17%)
  matrix products  13.6 us (14%)
  other arithmetic  3.15 us (3%)
    pallas_call x1, Pallas kernels, finish(): pl.pallas_call(finish_kernel, out_shape=jax.ShapeDtypeStruct(field.shape,...  20.6 us
    all_to_all x1, starting transfers between devices, body(): lax.all_to_all(along.reshape((ranks, per) + along.shape[1:]), 'rows', 0,...  11.8 us
    all_to_all x1, waiting for transfers between devices, body(): lax.all_to_all(values.astype(jnp.bfloat16), 'rows', 0, 0, tiled=True)  10.1 us
    all_to_all x1, waiting for transfers between devices, body(): lax.all_to_all(along.reshape((ranks, per) + along.shape[1:]), 'rows', 0,...  9.65 us
    all_to_all x1, starting transfers between devices, body(): lax.all_to_all(values.astype(jnp.bfloat16), 'rows', 0, 0, tiled=True)  7.64 us
    slice x1, local copies, waits for them, and re-layouts, body(): spectral_weight[0]  7.35 us
    unnamed x19, local copies, waits for them, and re-layouts  6.5 us
    dot_general x1, matrix products, body(): jnp.einsum('xm,blncx->mblnc', lon_table, field, preferred_element_type=jn...  4.3 us
  transfers between devices with their start and end apart: 4, of which 2 were waited for; matrix products, arithmetic and copies ran while one was open for 13% of the time, Pallas kernels for 0%

profile of v7, /device:TPU:25, one launch (start us, length us, event | category | flops | bytes accessed | tf_op | source)
XLA Modules:
  0.0 99.4 jit_solution(18185663119684480)
XLA Ops:
  0.0 1.2 %multiply_convert_fusion.lon_ref = bf16[64,1024]{1,0:T(8,128)(2,1)S(1)} fusion(s32[64]{0:T(128)S(1)} %iota_add_fusion), kind=kLoop, calls=%fused_computation.35 | loop fusion | flops 1114112 | bytes 131328 | tf_op jit(solution)/shard_map/convert_element_type | solution.py:98
  1.2 0.1 convert_element_type.69
  1.3 4.3 %fusion.5 = f32[32,2,2,1,16,64]{5,0,4,2,1,3:T(8,128)S(1)} fusion(bf16[2,1,16,64,1024]{4,3,2,1,0:T(8,128)(2,1)} %param.7, bf16[32,2,1024,1,1]{2,1,0,4,3:T(2,128)(2,1)S(1)} %bitcast.87), kind=kOutput, calls=%fused_computation.8 | convolution fusion | flops 268435456 | bytes 4849664 | tf_op jit(solution)/shard_map/xm,blncx->mblnc/dot_general | solution.py:105
  5.6 0.6 copy.96
  6.2 1.5 %reshape.122 = f32[32,1,4096]{2,1,0:T(1,128)} reshape(f32[32,1,2,2,16,64]{5,4,3,2,1,0:T(8,128)S(1)} %bitcast.83) | data formatting | bytes 1048576
  7.7 11.8 %all-to-all-start = ((f32[32,1,4096]{2,1,0:T(1,128)}), f32[32,1,4096]{2,1,0:T(1,128)S(1)}, u32[]{:S(2)}, u32[]{:S(2)}) async-start(f32[32,1,4096]{2,1,0:T(1,128)} %reshape.122), calls=%async_computation | async-start | bytes 1048576 | tf_op jit(solution)/shard_map/all_to_all | solution.py:106
  19.5 7.3 %fusion.42 = (bf16[1,64,2,64,64]{4,3,2,1,0:T(8,128)(2,1)S(1)}, bf16[1,64,2,64,64]{4,3,2,1,0:T(8,128)(2,1)}, bf16[1,64,2,64,64]{4,3,2,1,0:T(8,128)(2,1)}) fusion(bf16[3,64,2,64,64]{4,3,2,1,0:T(8,128)(2,1)} %param.8), kind=kLoop, calls=%fused_computation.57 | loop fusion | bytes 6291456 | tf_op jit(solution)/shard_map/slice | solution.py:112
  26.8 9.6 %all-to-all-done = f32[32,1,4096]{2,1,0:T(1,128)S(1)} async-done(((f32[32,1,4096]{2,1,0:T(1,128)}), f32[32,1,4096]{2,1,0:T(1,128)S(1)}, u32[]{:S(2)}, u32[]{:S(2)}) %all-to-all-start) | async-done | bytes 524320 | tf_op jit(solution)/shard_map/all_to_all | solution.py:106
  36.5 0.6 broadcast.157
  37.0 1.9 %reduce = f32[32,4096]{1,0:T(8,128)S(1)} reduce(f32[32,1,4096]{2,1,0:T(1,128)S(1)} %all-to-all-done, f32[]{:T(128)} %broadcast.157), dimensions={1}, to_apply=%all_to_all.6.reduce_sub_computation | reduce | bytes 1048580 | tf_op jit(solution)/shard_map/all_to_all | solution.py:106
  39.0 1.4 %reshape.123 = f32[32,1,2,2,16,64]{5,4,3,2,1,0:T(8,128)} reshape(f32[32,4096]{1,0:T(8,128)S(1)} %reduce) | data formatting | bytes 1048576
  40.4 3.8 %fusion.12 = bf16[64,2,2,64]{3,0,2,1:T(8,128)(2,1)S(1)} fusion(f32[32,2,2,1,16,64]{5,4,2,1,3,0:T(8,128)} %bitcast.86, s32[64]{0:T(128)S(1)} %iota_add_fusion, s32[32,16]{0,1:T(8,128)S(1)} %multiply_add_fusion), kind=kOutput, calls=%fused_computation.15 | convolution fusion | flops 101203968 | bytes 559360 | tf_op jit(solution)/shard_map/sjblnc,snk->jblkc/dot_general | solution.py:107
  44.2 2.4 %collective-permute-start.1 = (bf16[2,2,1,64,64]{4,3,1,0,2:T(8,128)(2,1)S(1)}, bf16[2,2,1,64,64]{4,3,1,0,2:T(8,128)(2,1)S(1)}, u32[]{:S(2)}, u32[]{:S(2)}) collective-permute-start(bf16[2,2,1,64,64]{4,3,1,0,2:T(8,128)(2,1)S(1)} %bitcast.92), channel_id=1, source_target_pairs={{1,0},{2,1},{3,2},{4,3},{5,4},{6,5},{7,6},{9,8},{10,9},{11,10},{12... | collective-permute-start | bytes 98312 | tf_op jit(solution)/shard_map/ppermute | solution.py:21
  46.6 3.1 %collective-permute-start = (bf16[2,2,1,64,64]{4,3,1,0,2:T(8,128)(2,1)S(1)}, bf16[2,2,1,64,64]{4,3,1,0,2:T(8,128)(2,1)S(1)}, u32[]{:S(2)}, u32[]{:S(2)}) collective-permute-start(bf16[2,2,1,64,64]{4,3,1,0,2:T(8,128)(2,1)S(1)} %bitcast.93), channel_id=1, source_target_pairs={{0,1},{1,2},{2,3},{3,4},{4,5},{5,6},{6,7},{8,9},{9,10},{10,11},{11... | collective-permute-start | bytes 98312 | tf_op jit(solution)/shard_map/ppermute | solution.py:19
  49.7 2.2 %fusion.3 = f32[2,64,2,64]{3,2,1,0:T(2,128)S(1)} fusion(bf16[1,64,2,64,64]{4,3,2,1,0:T(8,128)(2,1)} %get-tuple-element.6, bf16[2,2,64,64]{3,2,1,0:T(8,128)(2,1)S(1)} %bitcast.94), kind=kOutput, calls=%fused_computation.5 | convolution fusion | flops 2097152 | bytes 1146880 | tf_op jit(solution)/shard_map/kjco,jblkc->jblko/dot_general | solution.py:116
  51.9 0.7 fusion.2
  52.6 0.7 fusion.13
  53.3 0.0 copy-start.2
  53.3 0.0 copy-start.3
  53.3 0.0 copy-start.5
  53.3 1.9 %fusion.8 = bf16[32,2,2,1,16,64]{5,0,4,2,1,3:T(8,128)(2,1)S(1)} fusion(s32[64]{0:T(128)S(1)} %iota_add_fusion, s32[32,16]{0,1:T(8,128)S(1)} %multiply_add_fusion, bf16[2,2,64,64,1]{3,1,2,0,4:T(2,128)(2,1)S(1)} %fusion.13), kind=kOutput, calls=%fused_computation.10 | convolution fusion | flops 101318656 | bytes 297216 | tf_op jit(solution)/shard_map/rnk,jblko->rjblno/dot_general | solution.py:129
  55.2 0.2 copy.97
  55.4 1.1 %reshape.124 = bf16[32,2,2048]{2,1,0:T(2,128)(2,1)} reshape(bf16[32,1,2,2,16,64]{5,4,3,2,1,0:T(8,128)(2,1)S(1)} %bitcast.84) | data formatting | bytes 524288
  56.5 7.6 %all-to-all-start.1 = ((bf16[32,2,2048]{2,1,0:T(2,128)(2,1)}), bf16[32,2,2048]{2,1,0:T(2,128)(2,1)S(1)}, u32[]{:S(2)}, u32[]{:S(2)}) async-start(bf16[32,2,2048]{2,1,0:T(2,128)(2,1)} %reshape.124), calls=%async_computation.1 | async-start | bytes 524288 | tf_op jit(solution)/shard_map/all_to_all | solution.py:132
  64.2 0.7 copy.50
  64.9 0.7 copy.51
  65.6 0.7 copy.53.bias_ref
  66.3 0.7 copy.49
  67.0 10.1 %all-to-all-done.1 = bf16[32,2,2048]{2,1,0:T(2,128)(2,1)S(1)} async-done(((bf16[32,2,2048]{2,1,0:T(2,128)(2,1)}), bf16[32,2,2048]{2,1,0:T(2,128)(2,1)S(1)}, u32[]{:S(2)}, u32[]{:S(2)}) %all-to-all-start.1) | async-done | bytes 262176 | tf_op jit(solution)/shard_map/all_to_all | solution.py:132
  77.1 0.4 reshape.125
  77.5 1.4 %copy.52.back_ref = bf16[32,64,64]{2,1,0:T(8,128)(2,1)} copy(bf16[32,64,64]{1,0,2:T(8,128)(2,1)S(1)} %bitcast.85) | data formatting | bytes 524288 | tf_op jit(solution)/shard_map/reshape;reshape | solution.py:139
  78.8 20.6 %shard_map.73 = bf16[32,64,1024]{2,1,0:T(8,128)(2,1)} custom-call(bf16[32,64,1024]{2,1,0:T(8,128)(2,1)} %bitcast.82, bf16[32,64,64]{2,1,0:T(8,128)(2,1)} %copy.52.back_ref, bf16[64,1024]{1,0:T(8,128)(2,1)} %copy-done.1, bf16[64,64]{1,0:T(8,128)(2,1)} %bitcast.90, f32[64,1]{1,0:T(8,128)} %copy.53.bias_ref, bf16[256,64]{1,0:T(8,128)(2,1)} %bitcast.88, ...), custom_call_target="tpu_custom_call" | custom-call | flops 3758096384 | bytes 8650752 | tf_op jit(solution)/shard_map/pallas_call | solution.py:59
  (13 shorter events, 0.0 us)
Async XLA Ops:
  1.2 4.4 %copy-start.1 = (bf16[64,1024]{1,0:T(8,128)(2,1)}, bf16[64,1024]{1,0:T(8,128)(2,1)S(1)}, u32[]{:S(2)}) copy-start(bf16[64,1024]{1,0:T(8,128)(2,1)S(1)} %multiply_convert_fusion.lon_ref) | copy-start | bytes 393220
  7.7 28.8 %all-to-all-start = ((f32[32,1,4096]{2,1,0:T(1,128)}), f32[32,1,4096]{2,1,0:T(1,128)S(1)}, u32[]{:S(2)}, u32[]{:S(2)}) async-start(f32[32,1,4096]{2,1,0:T(1,128)} %reshape.122), calls=%async_computation | async-start | bytes 1048576 | tf_op jit(solution)/shard_map/all_to_all | solution.py:106
  40.4 11.6 %copy-start = (bf16[1,64,2,64,64]{4,3,2,1,0:T(8,128)(2,1)S(1)}, bf16[1,64,2,64,64]{4,3,2,1,0:T(8,128)(2,1)}, u32[]{:S(2)}) copy-start(bf16[1,64,2,64,64]{4,3,2,1,0:T(8,128)(2,1)} %get-tuple-element.7) | copy-start | bytes 3145732
  44.2 7.7 %collective-permute-start.1 = (bf16[2,2,1,64,64]{4,3,1,0,2:T(8,128)(2,1)S(1)}, bf16[2,2,1,64,64]{4,3,1,0,2:T(8,128)(2,1)S(1)}, u32[]{:S(2)}, u32[]{:S(2)}) collective-permute-start(bf16[2,2,1,64,64]{4,3,1,0,2:T(8,128)(2,1)S(1)} %bitcast.92), channel_id=1, source_target_pairs={{1,0},{2,1},{3,2},{4,3},{5,4},{6,5},{7,6},{9,8},{10,9},{11,10},{12... | collective-permute-start | bytes 98312 | tf_op jit(solution)/shard_map/ppermute | solution.py:21
  46.6 6.0 %collective-permute-start = (bf16[2,2,1,64,64]{4,3,1,0,2:T(8,128)(2,1)S(1)}, bf16[2,2,1,64,64]{4,3,1,0,2:T(8,128)(2,1)S(1)}, u32[]{:S(2)}, u32[]{:S(2)}) collective-permute-start(bf16[2,2,1,64,64]{4,3,1,0,2:T(8,128)(2,1)S(1)} %bitcast.93), channel_id=1, source_target_pairs={{0,1},{1,2},{2,3},{3,4},{4,5},{5,6},{6,7},{8,9},{9,10},{10,11},{11... | collective-permute-start | bytes 98312 | tf_op jit(solution)/shard_map/ppermute | solution.py:19
  53.3 10.9 %copy-start.2 = (bf16[64,256]{1,0:T(8,128)(2,1)S(1)}, bf16[64,256]{1,0:T(8,128)(2,1)}, u32[]{:S(2)}) copy-start(bf16[64,256]{1,0:T(8,128)(2,1)} %param.11) | copy-start | bytes 98308
  53.3 11.6 %copy-start.3 = (bf16[64,256]{1,0:T(8,128)(2,1)S(1)}, bf16[64,256]{1,0:T(8,128)(2,1)}, u32[]{:S(2)}) copy-start(bf16[64,256]{1,0:T(8,128)(2,1)} %param.12) | copy-start | bytes 98308
  53.3 12.3 %copy-start.5 = (f32[64]{0:T(128)S(1)}, f32[64]{0:T(128)}, u32[]{:S(2)}) copy-start(f32[64]{0:T(128)} %param.10) | copy-start | bytes 772
  53.3 13.0 %copy-start.4 = (bf16[64,64]{1,0:T(8,128)(2,1)S(1)}, bf16[64,64]{1,0:T(8,128)(2,1)}, u32[]{:S(2)}) copy-start(bf16[64,64]{1,0:T(8,128)(2,1)} %param.9) | copy-start | bytes 24580
  56.5 20.6 %all-to-all-start.1 = ((bf16[32,2,2048]{2,1,0:T(2,128)(2,1)}), bf16[32,2,2048]{2,1,0:T(2,128)(2,1)S(1)}, u32[]{:S(2)}, u32[]{:S(2)}) async-start(bf16[32,2,2048]{2,1,0:T(2,128)(2,1)} %reshape.124), calls=%async_computation.1 | async-start | bytes 524288 | tf_op jit(solution)/shard_map/all_to_all | solution.py:132

commit v8 on v7

--- a/solution.py
+++ b/solution.py
@@ -103,7 +103,8 @@
     )
     per = lon_modes // ranks
     along = jnp.einsum("xm,blncx->mblnc", lon_table, field, preferred_element_type=jnp.float32)
-    along = lax.all_to_all(along.reshape((ranks, per) + along.shape[1:]), "rows", 0, 0, tiled=True)
+    along = along.astype(jnp.bfloat16).reshape((ranks, per) + along.shape[1:])
+    along = lax.all_to_all(along, "rows", 0, 0, tiled=True).astype(jnp.float32)
     modes = jnp.einsum("sjblnc,snk->jblkc", along, lat_table, precision=high)
     modes = modes.astype(jnp.bfloat16)
     padded = extended(modes, (("lev", 2),), 1)

time: 99.8 us -> 87.8 us (0.88)
  waiting for transfers between devices: 19.7 us -> 13.9 us
  local copies, waits for them, and re-layouts: 17.4 us -> 15.3 us
  starting transfers between devices: 24.9 us -> 23.3 us
  other arithmetic: 3.15 us -> 1.84 us
  matrix products: 13.6 us -> 12.4 us
    all_to_all x1, waiting for transfers between devices: 9.65 us -> 5.58 us  [body(): along = lax.all_to_all(along, 'rows', 0, 0, tiled=True).astype(jnp.float32)]
    dot_general x1, matrix products: 3.83 us -> 1.72 us  [body(): modes = jnp.einsum('sjblnc,snk->jblkc', along, lat_table, precision=high)]
    all_to_all x1 -> x0, other arithmetic: 1.92 us -> none  [body(): lax.all_to_all(along.reshape((ranks, per) + along.shape[1:]), 'rows', 0,...]
    all_to_all x1, waiting for transfers between devices: 10.1 us -> 8.23 us  [body(): lax.all_to_all(values.astype(jnp.bfloat16), 'rows', 0, 0, tiled=True)]
    unnamed x19 -> x17, local copies, waits for them, and re-layouts: 6.5 us -> 5.08 us
    all_to_all x1, starting transfers between devices: 7.64 us -> 6.24 us  [body(): lax.all_to_all(values.astype(jnp.bfloat16), 'rows', 0, 0, tiled=True)]
  transfers between devices with their start and end apart: 4 -> 4, of which waited for: 2 -> 3; matrix products, arithmetic and copies ran while one was open for 13% -> 17% of each run, Pallas kernels for 0% -> 0%
where the time goes in v8:
time: 87.8 us; the launch traced here: 87.5 us
  starting transfers between devices  23.3 us (27%)
  Pallas kernels  20.6 us (23%)
  local copies, waits for them, and re-layouts  15.3 us (17%)
  waiting for transfers between devices  13.9 us (16%)
  matrix products  12.4 us (14%)
  other arithmetic  1.84 us (2%)
    pallas_call x1, Pallas kernels, finish(): pl.pallas_call(finish_kernel, out_shape=jax.ShapeDtypeStruct(field.shape,...  20.6 us
    all_to_all x1, starting transfers between devices, body(): along = lax.all_to_all(along, 'rows', 0, 0, tiled=True).astype(jnp.float32)  11.8 us
    all_to_all x1, waiting for transfers between devices, body(): lax.all_to_all(values.astype(jnp.bfloat16), 'rows', 0, 0, tiled=True)  8.23 us
    slice x1, local copies, waits for them, and re-layouts, body(): spectral_weight[0]  7.34 us
    all_to_all x1, starting transfers between devices, body(): lax.all_to_all(values.astype(jnp.bfloat16), 'rows', 0, 0, tiled=True)  6.24 us
    all_to_all x1, waiting for transfers between devices, body(): along = lax.all_to_all(along, 'rows', 0, 0, tiled=True).astype(jnp.float32)  5.58 us
    dot_general x1, matrix products, body(): jnp.einsum('xm,blncx->mblnc', lon_table, field, preferred_element_type=jn...  5.24 us
    unnamed x17, local copies, waits for them, and re-layouts  5.08 us
  transfers between devices with their start and end apart: 4, of which 3 were waited for; matrix products, arithmetic and copies ran while one was open for 17% of the time, Pallas kernels for 0%

profile of v8, /device:TPU:25, one launch (start us, length us, event | category | flops | bytes accessed | tf_op | source)
XLA Modules:
  0.0 87.5 jit_solution(7397722101285904463)
XLA Ops:
  0.0 5.2 %fusion.5 = bf16[64,2,16,64]{3,0,2,1:T(8,128)(2,1)S(1)} fusion(bf16[2,1,16,64,1024]{4,3,2,1,0:T(8,128)(2,1)} %param.7, s32[64]{0:T(128)S(1)} %iota_add_fusion), kind=kOutput, calls=%fused_computation.8 | convolution fusion | flops 269680640 | bytes 4456704 | tf_op jit(solution)/shard_map/xm,blncx->mblnc/dot_general | solution.py:105
  5.2 0.6 copy.92
  5.9 1.1 %reshape.96 = bf16[32,2,2048]{2,1,0:T(2,128)(2,1)} reshape(bf16[32,1,2,2,16,64]{5,4,3,2,1,0:T(8,128)(2,1)S(1)} %bitcast.84) | data formatting | bytes 524288
  7.0 11.8 %all-to-all-start = ((bf16[32,2,2048]{2,1,0:T(2,128)(2,1)}), bf16[32,2,2048]{2,1,0:T(2,128)(2,1)S(1)}, u32[]{:S(2)}, u32[]{:S(2)}) async-start(bf16[32,2,2048]{2,1,0:T(2,128)(2,1)} %reshape.96), calls=%async_computation | async-start | bytes 524288 | tf_op jit(solution)/shard_map/all_to_all | solution.py:107
  18.7 7.3 %fusion.60 = (bf16[1,64,2,64,64]{4,3,2,1,0:T(8,128)(2,1)S(1)}, bf16[1,64,2,64,64]{4,3,2,1,0:T(8,128)(2,1)}, bf16[1,64,2,64,64]{4,3,2,1,0:T(8,128)(2,1)}) fusion(bf16[3,64,2,64,64]{4,3,2,1,0:T(8,128)(2,1)} %param.8), kind=kLoop, calls=%fused_computation.78 | loop fusion | bytes 6291456 | tf_op jit(solution)/shard_map/slice | solution.py:113
  26.1 5.6 %all-to-all-done = bf16[32,2,2048]{2,1,0:T(2,128)(2,1)S(1)} async-done(((bf16[32,2,2048]{2,1,0:T(2,128)(2,1)}), bf16[32,2,2048]{2,1,0:T(2,128)(2,1)S(1)}, u32[]{:S(2)}, u32[]{:S(2)}) %all-to-all-start) | async-done | bytes 262176 | tf_op jit(solution)/shard_map/all_to_all | solution.py:107
  31.7 0.4 reshape.97
  32.0 1.7 %fusion.12 = bf16[64,2,2,64]{3,0,2,1:T(8,128)(2,1)S(1)} fusion(bf16[32,2,2,1,16,64]{5,4,2,1,3,0:T(8,128)(2,1)S(1)} %bitcast.87, s32[64]{0:T(128)S(1)} %iota_add_fusion, s32[32,16]{0,1:T(8,128)S(1)} %multiply_add_fusion), kind=kOutput, calls=%fused_computation.15 | convolution fusion | flops 101203968 | bytes 297216 | tf_op jit(solution)/shard_map/sjblnc,snk->jblkc/dot_general | solution.py:108
  33.7 2.4 %collective-permute-start.1 = (bf16[2,2,1,64,64]{4,3,1,0,2:T(8,128)(2,1)S(1)}, bf16[2,2,1,64,64]{4,3,1,0,2:T(8,128)(2,1)S(1)}, u32[]{:S(2)}, u32[]{:S(2)}) collective-permute-start(bf16[2,2,1,64,64]{4,3,1,0,2:T(8,128)(2,1)S(1)} %bitcast.94), channel_id=1, source_target_pairs={{1,0},{2,1},{3,2},{4,3},{5,4},{6,5},{7,6},{9,8},{10,9},{11,10},{12... | collective-permute-start | bytes 98312 | tf_op jit(solution)/shard_map/ppermute | solution.py:21
  36.1 2.9 %collective-permute-start = (bf16[2,2,1,64,64]{4,3,1,0,2:T(8,128)(2,1)S(1)}, bf16[2,2,1,64,64]{4,3,1,0,2:T(8,128)(2,1)S(1)}, u32[]{:S(2)}, u32[]{:S(2)}) collective-permute-start(bf16[2,2,1,64,64]{4,3,1,0,2:T(8,128)(2,1)S(1)} %bitcast.95), channel_id=1, source_target_pairs={{0,1},{1,2},{2,3},{3,4},{4,5},{5,6},{6,7},{8,9},{9,10},{10,11},{11... | collective-permute-start | bytes 98312 | tf_op jit(solution)/shard_map/ppermute | solution.py:19
  39.0 2.2 %fusion.3 = f32[2,64,2,64]{3,2,1,0:T(2,128)S(1)} fusion(bf16[1,64,2,64,64]{4,3,2,1,0:T(8,128)(2,1)} %get-tuple-element.6, bf16[2,2,64,64]{3,2,1,0:T(8,128)(2,1)S(1)} %bitcast.96), kind=kOutput, calls=%fused_computation.5 | convolution fusion | flops 2097152 | bytes 1146880 | tf_op jit(solution)/shard_map/kjco,jblkc->jblko/dot_general | solution.py:117
  41.3 0.0 collective-permute-done.1
  41.3 0.7 fusion.2
  41.9 0.1 collective-permute-done
  42.1 0.7 fusion.13
  42.7 0.0 copy-start.1
  42.7 0.0 copy-start.2
  42.7 0.0 copy-start.4
  42.7 0.0 copy-start.3
  42.8 1.9 %fusion.8 = bf16[32,2,2,1,16,64]{5,0,4,2,1,3:T(8,128)(2,1)S(1)} fusion(s32[64]{0:T(128)S(1)} %iota_add_fusion, s32[32,16]{0,1:T(8,128)S(1)} %multiply_add_fusion, bf16[2,2,64,64,1]{3,1,2,0,4:T(2,128)(2,1)S(1)} %fusion.13), kind=kOutput, calls=%fused_computation.10 | convolution fusion | flops 101318656 | bytes 297216 | tf_op jit(solution)/shard_map/rnk,jblko->rjblno/dot_general | solution.py:130
  44.6 0.2 copy.91
  44.9 1.1 %reshape.98 = bf16[32,2,2048]{2,1,0:T(2,128)(2,1)} reshape(bf16[32,1,2,2,16,64]{5,4,3,2,1,0:T(8,128)(2,1)S(1)} %bitcast.85) | data formatting | bytes 524288
  46.0 6.2 %all-to-all-start.1 = ((bf16[32,2,2048]{2,1,0:T(2,128)(2,1)}), bf16[32,2,2048]{2,1,0:T(2,128)(2,1)S(1)}, u32[]{:S(2)}, u32[]{:S(2)}) async-start(bf16[32,2,2048]{2,1,0:T(2,128)(2,1)} %reshape.98), calls=%async_computation.1 | async-start | bytes 524288 | tf_op jit(solution)/shard_map/all_to_all | solution.py:133
  52.2 0.7 copy.49
  52.9 0.7 copy.50
  53.7 0.7 copy.52.bias_ref
  54.4 0.7 copy.48
  55.1 1.8 %multiply_convert_fusion.lon_ref = bf16[64,1024]{1,0:T(8,128)(2,1)} fusion(s32[64]{0:T(128)S(1)} %iota_add_fusion), kind=kLoop, calls=%fused_computation.41 | loop fusion | flops 1114112 | bytes 131328 | tf_op jit(solution)/shard_map/convert_element_type | solution.py:98
  56.9 8.2 %all-to-all-done.1 = bf16[32,2,2048]{2,1,0:T(2,128)(2,1)S(1)} async-done(((bf16[32,2,2048]{2,1,0:T(2,128)(2,1)}), bf16[32,2,2048]{2,1,0:T(2,128)(2,1)S(1)}, u32[]{:S(2)}, u32[]{:S(2)}) %all-to-all-start.1) | async-done | bytes 262176 | tf_op jit(solution)/shard_map/all_to_all | solution.py:133
  65.1 0.4 reshape.99
  65.5 1.4 %copy.51.back_ref = bf16[32,64,64]{2,1,0:T(8,128)(2,1)} copy(bf16[32,64,64]{1,0,2:T(8,128)(2,1)S(1)} %bitcast.86) | data formatting | bytes 524288 | tf_op jit(solution)/shard_map/reshape;reshape | solution.py:140
  66.9 20.6 %shard_map.73 = bf16[32,64,1024]{2,1,0:T(8,128)(2,1)} custom-call(bf16[32,64,1024]{2,1,0:T(8,128)(2,1)} %bitcast.93, bf16[32,64,64]{2,1,0:T(8,128)(2,1)} %copy.51.back_ref, bf16[64,1024]{1,0:T(8,128)(2,1)} %multiply_convert_fusion.lon_ref, bf16[64,64]{1,0:T(8,128)(2,1)} %bitcast.91, f32[64,1]{1,0:T(8,128)} %copy.52.bias_ref, bf16[256,64]{1,0:T(8,128)(2,1)} %bitcast.89, ...), custom_call_target="tpu_custom_call" | custom-call | flops 3758096384 | bytes 8650752 | tf_op jit(solution)/shard_map/pallas_call | solution.py:59
  (8 shorter events, 0.0 us)
Async XLA Ops:
  7.0 24.7 %all-to-all-start = ((bf16[32,2,2048]{2,1,0:T(2,128)(2,1)}), bf16[32,2,2048]{2,1,0:T(2,128)(2,1)S(1)}, u32[]{:S(2)}, u32[]{:S(2)}) async-start(bf16[32,2,2048]{2,1,0:T(2,128)(2,1)} %reshape.96), calls=%async_computation | async-start | bytes 524288 | tf_op jit(solution)/shard_map/all_to_all | solution.py:107
  32.0 9.3 %copy-start = (bf16[1,64,2,64,64]{4,3,2,1,0:T(8,128)(2,1)S(1)}, bf16[1,64,2,64,64]{4,3,2,1,0:T(8,128)(2,1)}, u32[]{:S(2)}) copy-start(bf16[1,64,2,64,64]{4,3,2,1,0:T(8,128)(2,1)} %get-tuple-element.7) | copy-start | bytes 3145732
  33.7 7.5 %collective-permute-start.1 = (bf16[2,2,1,64,64]{4,3,1,0,2:T(8,128)(2,1)S(1)}, bf16[2,2,1,64,64]{4,3,1,0,2:T(8,128)(2,1)S(1)}, u32[]{:S(2)}, u32[]{:S(2)}) collective-permute-start(bf16[2,2,1,64,64]{4,3,1,0,2:T(8,128)(2,1)S(1)} %bitcast.94), channel_id=1, source_target_pairs={{1,0},{2,1},{3,2},{4,3},{5,4},{6,5},{7,6},{9,8},{10,9},{11,10},{12... | collective-permute-start | bytes 98312 | tf_op jit(solution)/shard_map/ppermute | solution.py:21
  36.1 5.9 %collective-permute-start = (bf16[2,2,1,64,64]{4,3,1,0,2:T(8,128)(2,1)S(1)}, bf16[2,2,1,64,64]{4,3,1,0,2:T(8,128)(2,1)S(1)}, u32[]{:S(2)}, u32[]{:S(2)}) collective-permute-start(bf16[2,2,1,64,64]{4,3,1,0,2:T(8,128)(2,1)S(1)} %bitcast.95), channel_id=1, source_target_pairs={{0,1},{1,2},{2,3},{3,4},{4,5},{5,6},{6,7},{8,9},{9,10},{10,11},{11... | collective-permute-start | bytes 98312 | tf_op jit(solution)/shard_map/ppermute | solution.py:19
  42.7 9.5 %copy-start.1 = (bf16[64,256]{1,0:T(8,128)(2,1)S(1)}, bf16[64,256]{1,0:T(8,128)(2,1)}, u32[]{:S(2)}) copy-start(bf16[64,256]{1,0:T(8,128)(2,1)} %param.11) | copy-start | bytes 98308
  42.7 10.2 %copy-start.2 = (bf16[64,256]{1,0:T(8,128)(2,1)S(1)}, bf16[64,256]{1,0:T(8,128)(2,1)}, u32[]{:S(2)}) copy-start(bf16[64,256]{1,0:T(8,128)(2,1)} %param.12) | copy-start | bytes 98308
  42.7 10.9 %copy-start.4 = (f32[64]{0:T(128)S(1)}, f32[64]{0:T(128)}, u32[]{:S(2)}) copy-start(f32[64]{0:T(128)} %param.10) | copy-start | bytes 772
  42.7 11.6 %copy-start.3 = (bf16[64,64]{1,0:T(8,128)(2,1)S(1)}, bf16[64,64]{1,0:T(8,128)(2,1)}, u32[]{:S(2)}) copy-start(bf16[64,64]{1,0:T(8,128)(2,1)} %param.9) | copy-start | bytes 24580
  46.0 19.2 %all-to-all-start.1 = ((bf16[32,2,2048]{2,1,0:T(2,128)(2,1)}), bf16[32,2,2048]{2,1,0:T(2,128)(2,1)S(1)}, u32[]{:S(2)}, u32[]{:S(2)}) async-start(bf16[32,2,2048]{2,1,0:T(2,128)(2,1)} %reshape.98), calls=%async_computation.1 | async-start | bytes 524288 | tf_op jit(solution)/shard_map/all_to_all | solution.py:133

commit v9 on v8

--- a/solution.py
+++ b/solution.py
@@ -1,3 +1,4 @@
+import functools
 import math
 
 import jax
@@ -30,6 +31,45 @@
     turns = positions[:, None] * freq[None, :] % count
     angle = 2.0 * math.pi / count * turns.astype(jnp.float32)
     return (jnp.cos(angle) + jnp.sin(angle)) / math.sqrt(count)
+
+
+def halo_kernel(axis, x_ref, below_ref, above_ref, send_sems, recv_sems):
+    count = lax.axis_size(axis)
+    me = lax.axis_index(axis)
+    up = lax.rem(me + 1, count)
+    down = lax.rem(me + count - 1, count)
+    barrier = pltpu.get_barrier_semaphore()
+    for neighbour in (down, up):
+        pl.semaphore_signal(
+            barrier, inc=1, device_id={axis: neighbour}, device_id_type=pl.DeviceIdType.MESH
+        )
+    pl.semaphore_wait(barrier, 2)
+    copies = [
+        pltpu.make_async_remote_copy(
+            src_ref=x_ref,
+            dst_ref=dst,
+            send_sem=send_sems.at[slot],
+            recv_sem=recv_sems.at[slot],
+            device_id={axis: peer},
+            device_id_type=pl.DeviceIdType.MESH,
+        )
+        for slot, (dst, peer) in enumerate(((below_ref, up), (above_ref, down)))
+    ]
+    for copy in copies:
+        copy.start()
+    for copy in copies:
+        copy.wait()
+
+
+def halo(x, axis):
+    return pl.pallas_call(
+        functools.partial(halo_kernel, axis),
+        out_shape=(jax.ShapeDtypeStruct(x.shape, x.dtype),) * 2,
+        in_specs=[pl.BlockSpec(memory_space=pl.ANY)],
+        out_specs=(pl.BlockSpec(memory_space=pl.ANY),) * 2,
+        scratch_shapes=[pltpu.SemaphoreType.DMA((2,)), pltpu.SemaphoreType.DMA((2,))],
+        compiler_params=pltpu.CompilerParams(collective_id=0, has_side_effects=True),
+    )(x)
 
 
 def finish_kernel(field_ref, back_ref, lon_ref, local_ref, bias_ref, gate_ref, up_ref, down_ref, out_ref):
@@ -107,24 +147,13 @@
     along = lax.all_to_all(along, "rows", 0, 0, tiled=True).astype(jnp.float32)
     modes = jnp.einsum("sjblnc,snk->jblkc", along, lat_table, precision=high)
     modes = modes.astype(jnp.bfloat16)
-    padded = extended(modes, (("lev", 2),), 1)
+    below, above = halo(modes, "lev")
+    level = lax.axis_index("lev")
+    below = jnp.where(level > 0, below, jnp.zeros_like(below))
+    above = jnp.where(level < lax.axis_size("lev") - 1, above, jnp.zeros_like(above))
+    stacked = jnp.stack([below, modes, above])
     mixed = jnp.einsum(
-        "kjco,jblkc->jblko",
-        spectral_weight[0],
-        padded[:, :, 0:levels],
-        preferred_element_type=jnp.float32,
-    )
-    mixed = mixed + jnp.einsum(
-        "kjco,jblkc->jblko",
-        spectral_weight[1],
-        padded[:, :, 1 : levels + 1],
-        preferred_element_type=jnp.float32,
-    )
-    mixed = mixed + jnp.einsum(
-        "kjco,jblkc->jblko",
-        spectral_weight[2],
-        padded[:, :, 2 : levels + 2],
-        preferred_element_type=jnp.float32,
+        "dkjco,djblkc->jblko", spectral_weight, stacked, preferred_element_type=jnp.float32
     )
     mixed_b = mixed.astype(jnp.bfloat16)
     values = jnp.einsum(

time: 87.8 us -> 92.3 us (1.051)
  the two profiles are of different devices: /device:TPU:25 before, /device:TPU:1 now
where the time goes in v9:
time: 92.3 us; the launch traced here: 91.9 us
  Pallas kernels  26.6 us (29%)
  waiting for transfers between devices  21.2 us (23%)
  starting transfers between devices  18.2 us (20%)
  matrix products  14.1 us (15%)
  local copies, waits for them, and re-layouts  7.96 us (9%)
  other arithmetic  3.61 us (4%)
    pallas_call x1, Pallas kernels, finish(): pl.pallas_call(finish_kernel, out_shape=jax.ShapeDtypeStruct(field.shape,...  20.6 us
    all_to_all x1, waiting for transfers between devices, body(): along = lax.all_to_all(along, 'rows', 0, 0, tiled=True).astype(jnp.float32)  12.9 us
    all_to_all x1, starting transfers between devices, body(): along = lax.all_to_all(along, 'rows', 0, 0, tiled=True).astype(jnp.float32)  12.6 us
    all_to_all x1, waiting for transfers between devices, body(): lax.all_to_all(values.astype(jnp.bfloat16), 'rows', 0, 0, tiled=True)  8.27 us
    pallas_call x1, Pallas kernels, halo(): pl.pallas_call(functools.partial(halo_kernel, axis), out_shape=(jax.Shape...  6.08 us
    all_to_all x1, starting transfers between devices, body(): lax.all_to_all(values.astype(jnp.bfloat16), 'rows', 0, 0, tiled=True)  5.65 us
    dot_general x1, matrix products, body(): jnp.einsum('xm,blncx->mblnc', lon_table, field, preferred_element_type=jn...  5.23 us
    unnamed x15, local copies, waits for them, and re-layouts  5.06 us
  transfers between devices with their start and end apart: 2, of which 2 were waited for; matrix products, arithmetic and copies ran while one was open for 5% of the time, Pallas kernels for 0%

profile of v9, /device:TPU:1, one launch (start us, length us, event | category | flops | bytes accessed | tf_op | source)
XLA Modules:
  0.0 91.9 jit_solution(5692859296931969061)
XLA Ops:
  0.0 5.2 %fusion.4 = bf16[64,2,16,64]{3,0,2,1:T(8,128)(2,1)S(1)} fusion(bf16[2,1,16,64,1024]{4,3,2,1,0:T(8,128)(2,1)} %param.7, s32[64]{0:T(128)S(1)} %iota_add_fusion), kind=kOutput, calls=%fused_computation.4 | convolution fusion | flops 269680640 | bytes 4456704 | tf_op jit(solution)/shard_map/xm,blncx->mblnc/dot_general | solution.py:145
  5.2 0.6 copy.74
  5.9 1.1 %reshape.85 = bf16[32,2,2048]{2,1,0:T(2,128)(2,1)} reshape(bf16[32,1,2,2,16,64]{5,4,3,2,1,0:T(8,128)(2,1)S(1)} %bitcast.86) | data formatting | bytes 524288
  7.0 12.6 %all-to-all-start = ((bf16[32,2,2048]{2,1,0:T(2,128)(2,1)}), bf16[32,2,2048]{2,1,0:T(2,128)(2,1)S(1)}, u32[]{:S(2)}, u32[]{:S(2)}) async-start(bf16[32,2,2048]{2,1,0:T(2,128)(2,1)} %reshape.85), calls=%async_computation | async-start | bytes 524288 | tf_op jit(solution)/shard_map/all_to_all | solution.py:147
  19.6 12.9 %all-to-all-done = bf16[32,2,2048]{2,1,0:T(2,128)(2,1)S(1)} async-done(((bf16[32,2,2048]{2,1,0:T(2,128)(2,1)}), bf16[32,2,2048]{2,1,0:T(2,128)(2,1)S(1)}, u32[]{:S(2)}, u32[]{:S(2)}) %all-to-all-start) | async-done | bytes 262176 | tf_op jit(solution)/shard_map/all_to_all | solution.py:147
  32.5 0.3 reshape.86
  32.8 2.4 %fusion.14 = bf16[64,2,2,64]{3,0,2,1:T(8,128)(2,1)} fusion(bf16[32,2,2,1,16,64]{5,4,2,1,3,0:T(8,128)(2,1)S(1)} %bitcast.89, s32[64]{0:T(128)S(1)} %iota_add_fusion, s32[32,16]{0,1:T(8,128)S(1)} %multiply_add_fusion), kind=kOutput, calls=%fused_computation.10 | convolution fusion | flops 101203968 | bytes 297216 | tf_op jit(solution)/shard_map/sjblnc,snk->jblkc/dot_general | solution.py:148
  35.2 0.0 copy-start.2
  35.2 0.0 copy-start.3
  35.2 0.0 copy-start
  35.2 0.0 copy-start.1
  35.2 6.1 %shard_map.73 = (bf16[2,2,1,64,64]{4,3,2,1,0:T(8,128)(2,1)}, bf16[2,2,1,64,64]{4,3,2,1,0:T(8,128)(2,1)}) custom-call(bf16[2,2,1,64,64]{4,3,2,1,0:T(8,128)(2,1)} %bitcast.91), custom_call_target="tpu_custom_call" | custom-call | tf_op jit(solution)/shard_map/pallas_call | solution.py:65
  41.3 0.9 fusion.47
  42.2 0.9 maximum_bitcast_fusion
  43.1 4.6 %fusion.15 = bf16[2,2,64,64,1]{3,1,2,0,4:T(2,128)(2,1)S(1)} fusion(bf16[3,64,2,64,64]{4,3,2,1,0:T(8,128)(2,1)} %param.8, bf16[3,2,2,64,64]{4,3,2,1,0:T(8,128)(2,1)S(1)} %maximum_bitcast_fusion), kind=kOutput, calls=%fused_computation.11 | convolution fusion | flops 6307840 | bytes 3276800 | tf_op jit(solution)/shard_map/dkjco,djblkc->jblko/dot_general | solution.py:155
  47.7 1.9 %fusion.7 = bf16[32,2,2,1,16,64]{5,0,4,2,1,3:T(8,128)(2,1)S(1)} fusion(s32[64]{0:T(128)S(1)} %iota_add_fusion, s32[32,16]{0,1:T(8,128)S(1)} %multiply_add_fusion, bf16[2,2,64,64,1]{3,1,2,0,4:T(2,128)(2,1)S(1)} %fusion.15), kind=kOutput, calls=%fused_computation.6 | convolution fusion | flops 101318656 | bytes 297216 | tf_op jit(solution)/shard_map/rnk,jblko->rjblno/dot_general | solution.py:159
  49.6 0.2 copy.73
  49.8 1.1 %reshape.87 = bf16[32,2,2048]{2,1,0:T(2,128)(2,1)} reshape(bf16[32,1,2,2,16,64]{5,4,3,2,1,0:T(8,128)(2,1)S(1)} %bitcast.87) | data formatting | bytes 524288
  50.9 5.7 %all-to-all-start.1 = ((bf16[32,2,2048]{2,1,0:T(2,128)(2,1)}), bf16[32,2,2048]{2,1,0:T(2,128)(2,1)S(1)}, u32[]{:S(2)}, u32[]{:S(2)}) async-start(bf16[32,2,2048]{2,1,0:T(2,128)(2,1)} %reshape.87), calls=%async_computation.1 | async-start | bytes 524288 | tf_op jit(solution)/shard_map/all_to_all | solution.py:162
  56.6 0.0 copy-done.2
  56.6 0.7 copy.42
  57.3 0.0 copy-done.3
  57.3 0.7 copy.46.bias_ref
  58.0 0.0 copy-done
  58.0 0.7 copy.43
  58.7 0.0 copy-done.1
  58.7 0.7 copy.44
  59.5 1.8 %multiply_convert_fusion.lon_ref = bf16[64,1024]{1,0:T(8,128)(2,1)} fusion(s32[64]{0:T(128)S(1)} %iota_add_fusion), kind=kLoop, calls=%fused_computation.36 | loop fusion | flops 1114112 | bytes 131328 | tf_op jit(solution)/shard_map/convert_element_type | solution.py:138
  61.3 8.3 %all-to-all-done.1 = bf16[32,2,2048]{2,1,0:T(2,128)(2,1)S(1)} async-done(((bf16[32,2,2048]{2,1,0:T(2,128)(2,1)}), bf16[32,2,2048]{2,1,0:T(2,128)(2,1)S(1)}, u32[]{:S(2)}, u32[]{:S(2)}) %all-to-all-start.1) | async-done | bytes 262176 | tf_op jit(solution)/shard_map/all_to_all | solution.py:162
  69.6 0.4 reshape.88
  69.9 1.4 %copy.45.back_ref = bf16[32,64,64]{2,1,0:T(8,128)(2,1)} copy(bf16[32,64,64]{1,0,2:T(8,128)(2,1)S(1)} %bitcast.88) | data formatting | bytes 524288 | tf_op jit(solution)/shard_map/reshape;reshape | solution.py:169
  71.3 20.6 %shard_map.74 = bf16[32,64,1024]{2,1,0:T(8,128)(2,1)} custom-call(bf16[32,64,1024]{2,1,0:T(8,128)(2,1)} %bitcast.97, bf16[32,64,64]{2,1,0:T(8,128)(2,1)} %copy.45.back_ref, bf16[64,1024]{1,0:T(8,128)(2,1)} %multiply_convert_fusion.lon_ref, bf16[64,64]{1,0:T(8,128)(2,1)} %bitcast.95, f32[64,1]{1,0:T(8,128)} %copy.46.bias_ref, bf16[256,64]{1,0:T(8,128)(2,1)} %bitcast.93, ...), custom_call_target="tpu_custom_call" | custom-call | flops 3758096384 | bytes 8650752 | tf_op jit(solution)/shard_map/pallas_call | solution.py:99
  (2 shorter events, 0.0 us)
Async XLA Ops:
  7.0 25.5 %all-to-all-start = ((bf16[32,2,2048]{2,1,0:T(2,128)(2,1)}), bf16[32,2,2048]{2,1,0:T(2,128)(2,1)S(1)}, u32[]{:S(2)}, u32[]{:S(2)}) async-start(bf16[32,2,2048]{2,1,0:T(2,128)(2,1)} %reshape.85), calls=%async_computation | async-start | bytes 524288 | tf_op jit(solution)/shard_map/all_to_all | solution.py:147
  35.2 21.4 %copy-start.2 = (bf16[64,64]{1,0:T(8,128)(2,1)S(1)}, bf16[64,64]{1,0:T(8,128)(2,1)}, u32[]{:S(2)}) copy-start(bf16[64,64]{1,0:T(8,128)(2,1)} %param.9) | copy-start | bytes 24580
  35.2 22.1 %copy-start.3 = (f32[64]{0:T(128)S(1)}, f32[64]{0:T(128)}, u32[]{:S(2)}) copy-start(f32[64]{0:T(128)} %param.10) | copy-start | bytes 772
  35.2 22.8 %copy-start = (bf16[64,256]{1,0:T(8,128)(2,1)S(1)}, bf16[64,256]{1,0:T(8,128)(2,1)}, u32[]{:S(2)}) copy-start(bf16[64,256]{1,0:T(8,128)(2,1)} %param.11) | copy-start | bytes 98308
  35.2 23.5 %copy-start.1 = (bf16[64,256]{1,0:T(8,128)(2,1)S(1)}, bf16[64,256]{1,0:T(8,128)(2,1)}, u32[]{:S(2)}) copy-start(bf16[64,256]{1,0:T(8,128)(2,1)} %param.12) | copy-start | bytes 98308
  50.9 18.6 %all-to-all-start.1 = ((bf16[32,2,2048]{2,1,0:T(2,128)(2,1)}), bf16[32,2,2048]{2,1,0:T(2,128)(2,1)S(1)}, u32[]{:S(2)}, u32[]{:S(2)}) async-start(bf16[32,2,2048]{2,1,0:T(2,128)(2,1)} %reshape.87), calls=%async_computation.1 | async-start | bytes 524288 | tf_op jit(solution)/shard_map/all_to_all | solution.py:162

commit v10 on v8

--- a/solution.py
+++ b/solution.py
@@ -42,9 +42,9 @@
         value = jnp.dot(lhs, rhs, preferred_element_type=jnp.float32) + bias_ref[...]
         acts.append((0.5 * value * (1.0 + lax.erf(value * sqrt_half))).astype(jnp.bfloat16))
     act = jnp.concatenate(acts, axis=1)
-    gate = jnp.dot(gate_ref[...], act, preferred_element_type=jnp.float32)
+    half = jnp.dot(gate_ref[...], act, preferred_element_type=jnp.float32)
     upper = jnp.dot(up_ref[...], act, preferred_element_type=jnp.float32)
-    hidden = (0.5 * gate * (1.0 + jnp.tanh(0.5 * gate)) * upper).astype(jnp.bfloat16)
+    hidden = ((half + half * jnp.tanh(half)) * upper).astype(jnp.bfloat16)
     down = jnp.dot(down_ref[...], hidden, preferred_element_type=jnp.float32)
     for r in range(rows):
         grid = field_ref[r].astype(jnp.float32)
@@ -82,7 +82,7 @@
         lon_table.T,
         local_weight.T,
         local_bias.reshape(chans, 1),
-        gate_weight.T,
+        (gate_weight * 0.5).astype(gate_weight.dtype).T,
         up_weight.T,
         down_weight.T,
     )
@@ -104,8 +104,18 @@
     per = lon_modes // ranks
     along = jnp.einsum("xm,blncx->mblnc", lon_table, field, preferred_element_type=jnp.float32)
     along = along.astype(jnp.bfloat16).reshape((ranks, per) + along.shape[1:])
-    along = lax.all_to_all(along, "rows", 0, 0, tiled=True).astype(jnp.float32)
-    modes = jnp.einsum("sjblnc,snk->jblkc", along, lat_table, precision=high)
+    along = lax.all_to_all(along, "rows", 0, 0, tiled=True)
+    lat_high = lat_table.astype(jnp.bfloat16)
+    lat_low = (lat_table - lat_high.astype(jnp.float32)).astype(jnp.bfloat16)
+
+    def by_lat(spec, data, first):
+        pair = [(lat_high, data), (data, lat_high)][first]
+        rest = [(lat_low, data), (data, lat_low)][first]
+        return jnp.einsum(spec, *pair, preferred_element_type=jnp.float32) + jnp.einsum(
+            spec, *rest, preferred_element_type=jnp.float32
+        )
+
+    modes = by_lat("sjblnc,snk->jblkc", along, 1)
     modes = modes.astype(jnp.bfloat16)
     padded = extended(modes, (("lev", 2),), 1)
     mixed = jnp.einsum(
@@ -127,9 +137,7 @@
         preferred_element_type=jnp.float32,
     )
     mixed_b = mixed.astype(jnp.bfloat16)
-    values = jnp.einsum(
-        "rnk,jblko->rjblno", lat_table, mixed_b.astype(jnp.float32), precision=high
-    )
+    values = by_lat("rnk,jblko->rjblno", mixed_b, 0)
     values = lax.all_to_all(values.astype(jnp.bfloat16), "rows", 0, 0, tiled=True)
     back_b = jnp.transpose(values, (2, 3, 4, 5, 0, 1)).reshape(
         batch, levels, lat_rows, chans, lon_modes

time: 87.8 us -> 87.5 us (level)
  Pallas kernels: 20.6 us -> 18 us
  waiting for transfers between devices: 13.9 us -> 15.3 us
    pallas_call x1, Pallas kernels: 20.6 us -> 18 us  [finish(): pl.pallas_call(finish_kernel, out_shape=jax.ShapeDtypeStruct(field.shape,...]
    dot_general x2 -> x4, matrix products: 3.6 us -> 5.87 us  [the longest x2 3.07 us: by_lat(): jnp.einsum(spec, *rest, preferred_element_type=jnp.float32)]
    dot_general x1, matrix products: 2.23 us -> 0.65 us  [body(): jnp.einsum('kjco,jblkc->jblko', spectral_weight[1], padded[:, :, 1:levels...]
    ppermute x1, waiting for transfers between devices: 0.11 us -> 1.52 us  [extended(): lax.ppermute(tail, axis, [(i, (i + 1) % count) for i in range(ends)])]
    unnamed x17 -> x19, local copies, waits for them, and re-layouts: 5.08 us -> 4.46 us
  transfers between devices with their start and end apart: 4 -> 4, of which waited for: 3 -> 3; matrix products, arithmetic and copies ran while one was open for 17% -> 15% of each run, Pallas kernels for 0% -> 0%
where the time goes in v10:
time: 87.5 us; the launch traced here: 87.1 us
  starting transfers between devices  23.4 us (27%)
  Pallas kernels  18 us (21%)
  waiting for transfers between devices  15.3 us (17%)
  local copies, waits for them, and re-layouts  14.7 us (17%)
  matrix products  13.1 us (15%)
  other arithmetic  2.49 us (3%)
    pallas_call x1, Pallas kernels, finish(): pl.pallas_call(finish_kernel, out_shape=jax.ShapeDtypeStruct(field.shape,...  18 us
    all_to_all x1, starting transfers between devices, body(): along = lax.all_to_all(along, 'rows', 0, 0, tiled=True)  11.8 us
    all_to_all x1, waiting for transfers between devices, body(): lax.all_to_all(values.astype(jnp.bfloat16), 'rows', 0, 0, tiled=True)  8.18 us
    slice x1, local copies, waits for them, and re-layouts, body(): spectral_weight[0]  7.34 us
    all_to_all x1, starting transfers between devices, body(): lax.all_to_all(values.astype(jnp.bfloat16), 'rows', 0, 0, tiled=True)  6.23 us
    all_to_all x1, waiting for transfers between devices, body(): along = lax.all_to_all(along, 'rows', 0, 0, tiled=True)  5.58 us
    dot_general x1, matrix products, body(): jnp.einsum('xm,blncx->mblnc', lon_table, field, preferred_element_type=jn...  5.24 us
    unnamed x19, local copies, waits for them, and re-layouts  4.46 us
  transfers between devices with their start and end apart: 4, of which 3 were waited for; matrix products, arithmetic and copies ran while one was open for 15% of the time, Pallas kernels for 0%

profile of v10, /device:TPU:25, one launch (start us, length us, event | category | flops | bytes accessed | tf_op | source)
XLA Modules:
  0.0 87.1 jit_solution(2116710865201001143)
XLA Ops:
  0.0 5.2 %fusion.6 = bf16[64,2,16,64]{3,0,2,1:T(8,128)(2,1)S(1)} fusion(bf16[2,1,16,64,1024]{4,3,2,1,0:T(8,128)(2,1)} %param.7, s32[64]{0:T(128)S(1)} %iota_add_fusion), kind=kOutput, calls=%fused_computation.10 | convolution fusion | flops 269680640 | bytes 4456704 | tf_op jit(solution)/shard_map/xm,blncx->mblnc/dot_general | solution.py:105
  5.2 0.6 copy.125
  5.9 1.1 %reshape.110 = bf16[32,2,2048]{2,1,0:T(2,128)(2,1)} reshape(bf16[32,1,2,2,16,64]{5,4,3,2,1,0:T(8,128)(2,1)S(1)} %bitcast.99) | data formatting | bytes 524288
  6.9 11.8 %all-to-all-start = ((bf16[32,2,2048]{2,1,0:T(2,128)(2,1)}), bf16[32,2,2048]{2,1,0:T(2,128)(2,1)S(1)}, u32[]{:S(2)}, u32[]{:S(2)}) async-start(bf16[32,2,2048]{2,1,0:T(2,128)(2,1)} %reshape.110), calls=%async_computation | async-start | bytes 524288 | tf_op jit(solution)/shard_map/all_to_all | solution.py:107
  18.7 7.3 %fusion.81 = (bf16[1,64,2,64,64]{4,3,2,1,0:T(8,128)(2,1)S(1)}, bf16[1,64,2,64,64]{4,3,2,1,0:T(8,128)(2,1)}, bf16[1,64,2,64,64]{4,3,2,1,0:T(8,128)(2,1)}) fusion(bf16[3,64,2,64,64]{4,3,2,1,0:T(8,128)(2,1)} %param.8), kind=kLoop, calls=%fused_computation.100 | loop fusion | bytes 6291456 | tf_op jit(solution)/shard_map/slice | solution.py:123
  26.1 5.6 %all-to-all-done = bf16[32,2,2048]{2,1,0:T(2,128)(2,1)S(1)} async-done(((bf16[32,2,2048]{2,1,0:T(2,128)(2,1)}), bf16[32,2,2048]{2,1,0:T(2,128)(2,1)S(1)}, u32[]{:S(2)}, u32[]{:S(2)}) %all-to-all-start) | async-done | bytes 262176 | tf_op jit(solution)/shard_map/all_to_all | solution.py:107
  31.6 0.4 reshape.111
  32.0 0.0 copy-start.1
  32.0 1.6 %convolution_bitcast_fusion = f32[64,2,2,64]{3,0,2,1:T(8,128)S(1)} fusion(bf16[32,2,2,1,16,64]{5,4,2,1,3,0:T(8,128)(2,1)S(1)} %bitcast.102, s32[64]{0:T(128)S(1)} %iota_add_fusion, s32[32,16]{0,1:T(8,128)S(1)} %multiply_add_fusion), kind=kOutput, calls=%fused_computation.12 | convolution fusion | flops 17432576 | bytes 329984 | tf_op jit(solution)/shard_map/sjblnc,snk->jblkc/dot_general | solution.py:114
  33.6 1.6 %fusion.14 = bf16[64,2,2,64]{3,0,2,1:T(8,128)(2,1)S(1)} fusion(f32[64,2,2,64]{3,0,2,1:T(8,128)S(1)} %convolution_bitcast_fusion, bf16[32,2,2,1,16,64]{5,4,2,1,3,0:T(8,128)(2,1)S(1)} %bitcast.103, s32[64]{0:T(128)S(1)} %iota_add_fusion, s32[32,16]{0,1:T(8,128)S(1)} %multiply_add_fusion), kind=kOutput, calls=%fused_computation.18 | convolution fusion | flops 17367040 | bytes 362752 | tf_op jit(solution)/shard_map/sjblnc,snk->jblkc/dot_general | solution.py:114
  35.1 2.4 %collective-permute-start.1 = (bf16[2,2,1,64,64]{4,3,1,0,2:T(8,128)(2,1)S(1)}, bf16[2,2,1,64,64]{4,3,1,0,2:T(8,128)(2,1)S(1)}, u32[]{:S(2)}, u32[]{:S(2)}) collective-permute-start(bf16[2,2,1,64,64]{4,3,1,0,2:T(8,128)(2,1)S(1)} %bitcast.109), channel_id=1, source_target_pairs={{1,0},{2,1},{3,2},{4,3},{5,4},{6,5},{7,6},{9,8},{10,9},{11,10},{12... | collective-permute-start | bytes 98312 | tf_op jit(solution)/shard_map/ppermute | solution.py:21
  37.5 3.1 %collective-permute-start = (bf16[2,2,1,64,64]{4,3,1,0,2:T(8,128)(2,1)S(1)}, bf16[2,2,1,64,64]{4,3,1,0,2:T(8,128)(2,1)S(1)}, u32[]{:S(2)}, u32[]{:S(2)}) collective-permute-start(bf16[2,2,1,64,64]{4,3,1,0,2:T(8,128)(2,1)S(1)} %bitcast.110), channel_id=1, source_target_pairs={{0,1},{1,2},{2,3},{3,4},{4,5},{5,6},{6,7},{8,9},{9,10},{10,11},{11... | collective-permute-start | bytes 98312 | tf_op jit(solution)/shard_map/ppermute | solution.py:19
  40.6 0.7 fusion.3
  41.3 0.0 collective-permute-done.1
  41.3 0.7 fusion.2
  41.9 1.5 %collective-permute-done = bf16[2,2,1,64,64]{4,3,1,0,2:T(8,128)(2,1)S(1)} collective-permute-done((bf16[2,2,1,64,64]{4,3,1,0,2:T(8,128)(2,1)S(1)}, bf16[2,2,1,64,64]{4,3,1,0,2:T(8,128)(2,1)S(1)}, u32[]{:S(2)}, u32[]{:S(2)}) %collective-permute-start) | collective-permute-done | bytes 32800 | tf_op jit(solution)/shard_map/ppermute | solution.py:19
  43.5 0.7 fusion.15
  44.1 1.2 %fusion.38 = f32[2,2,64,32,16]{2,3,4,1,0:T(8,128)S(1)} fusion(s32[64]{0:T(128)S(1)} %iota_add_fusion, s32[32,16]{0,1:T(8,128)S(1)} %multiply_add_fusion, bf16[2,2,64,64,1]{3,1,2,0,4:T(2,128)(2,1)S(1)} %fusion.15), kind=kOutput, calls=%fused_computation.56 | convolution fusion | flops 17334272 | bytes 559360 | tf_op jit(solution)/shard_map/rnk,jblko->rjblno/dot_general | solution.py:114
  45.4 1.5 %fusion.9 = bf16[32,2,2,1,16,64]{5,0,4,2,1,3:T(8,128)(2,1)S(1)} fusion(f32[2,2,64,32,16]{2,3,4,1,0:T(8,128)S(1)} %fusion.38, s32[64]{0:T(128)S(1)} %iota_add_fusion, s32[32,16]{0,1:T(8,128)S(1)} %multiply_add_fusion, bf16[2,2,64,64,1]{3,1,2,0,4:T(2,128)(2,1)S(1)} %fusion.15), kind=kOutput, calls=%fused_computation.11 | convolution fusion | flops 17694720 | bytes 821504 | tf_op jit(solution)/shard_map/rnk,jblko->rjblno/dot_general | solution.py:114
  46.9 0.2 copy.124
  47.1 1.1 %reshape.112 = bf16[32,2,2048]{2,1,0:T(2,128)(2,1)} reshape(bf16[32,1,2,2,16,64]{5,4,3,2,1,0:T(8,128)(2,1)S(1)} %bitcast.100) | data formatting | bytes 524288
  48.2 6.2 %all-to-all-start.1 = ((bf16[32,2,2048]{2,1,0:T(2,128)(2,1)}), bf16[32,2,2048]{2,1,0:T(2,128)(2,1)S(1)}, u32[]{:S(2)}, u32[]{:S(2)}) async-start(bf16[32,2,2048]{2,1,0:T(2,128)(2,1)} %reshape.112), calls=%async_computation.1 | async-start | bytes 524288 | tf_op jit(solution)/shard_map/all_to_all | solution.py:141
  54.5 0.1 copy.70
  54.6 0.7 copy.72
  55.3 0.7 copy.74.bias_ref
  56.0 0.7 copy.69
  56.7 0.6 multiply_bitcast_fusion.gate_ref
  57.4 1.8 %multiply_convert_fusion.lon_ref = bf16[64,1024]{1,0:T(8,128)(2,1)} fusion(s32[64]{0:T(128)S(1)} %iota_add_fusion), kind=kLoop, calls=%fused_computation.44 | loop fusion | flops 1114112 | bytes 131328 | tf_op jit(solution)/shard_map/convert_element_type | solution.py:98
  59.2 8.2 %all-to-all-done.1 = bf16[32,2,2048]{2,1,0:T(2,128)(2,1)S(1)} async-done(((bf16[32,2,2048]{2,1,0:T(2,128)(2,1)}), bf16[32,2,2048]{2,1,0:T(2,128)(2,1)S(1)}, u32[]{:S(2)}, u32[]{:S(2)}) %all-to-all-start.1) | async-done | bytes 262176 | tf_op jit(solution)/shard_map/all_to_all | solution.py:141
  67.4 0.4 reshape.113
  67.7 1.4 %copy.73.back_ref = bf16[32,64,64]{2,1,0:T(8,128)(2,1)} copy(bf16[32,64,64]{1,0,2:T(8,128)(2,1)S(1)} %bitcast.101) | data formatting | bytes 524288 | tf_op jit(solution)/shard_map/reshape;reshape | solution.py:148
  69.1 18.0 %shard_map.73 = bf16[32,64,1024]{2,1,0:T(8,128)(2,1)} custom-call(bf16[32,64,1024]{2,1,0:T(8,128)(2,1)} %bitcast.108, bf16[32,64,64]{2,1,0:T(8,128)(2,1)} %copy.73.back_ref, bf16[64,1024]{1,0:T(8,128)(2,1)} %multiply_convert_fusion.lon_ref, bf16[64,64]{1,0:T(8,128)(2,1)} %bitcast.106, f32[64,1]{1,0:T(8,128)} %copy.74.bias_ref, ...), custom_call_target="tpu_custom_call" | custom-call | flops 3758096384 | bytes 8650752 | tf_op jit(solution)/shard_map/pallas_call | solution.py:59
  (13 shorter events, 0.0 us)
Async XLA Ops:
  6.9 24.7 %all-to-all-start = ((bf16[32,2,2048]{2,1,0:T(2,128)(2,1)}), bf16[32,2,2048]{2,1,0:T(2,128)(2,1)S(1)}, u32[]{:S(2)}, u32[]{:S(2)}) async-start(bf16[32,2,2048]{2,1,0:T(2,128)(2,1)} %reshape.110), calls=%async_computation | async-start | bytes 524288 | tf_op jit(solution)/shard_map/all_to_all | solution.py:107
  32.0 8.6 %copy-start.1 = (bf16[1,64,2,64,64]{4,3,2,1,0:T(8,128)(2,1)S(1)}, bf16[1,64,2,64,64]{4,3,2,1,0:T(8,128)(2,1)}, u32[]{:S(2)}) copy-start(bf16[1,64,2,64,64]{4,3,2,1,0:T(8,128)(2,1)} %get-tuple-element.6) | copy-start | bytes 3145732
  33.6 7.7 %copy-start = (bf16[1,64,2,64,64]{4,3,2,1,0:T(8,128)(2,1)S(1)}, bf16[1,64,2,64,64]{4,3,2,1,0:T(8,128)(2,1)}, u32[]{:S(2)}) copy-start(bf16[1,64,2,64,64]{4,3,2,1,0:T(8,128)(2,1)} %get-tuple-element.7) | copy-start | bytes 3145732
  35.1 6.1 %collective-permute-start.1 = (bf16[2,2,1,64,64]{4,3,1,0,2:T(8,128)(2,1)S(1)}, bf16[2,2,1,64,64]{4,3,1,0,2:T(8,128)(2,1)S(1)}, u32[]{:S(2)}, u32[]{:S(2)}) collective-permute-start(bf16[2,2,1,64,64]{4,3,1,0,2:T(8,128)(2,1)S(1)} %bitcast.109), channel_id=1, source_target_pairs={{1,0},{2,1},{3,2},{4,3},{5,4},{6,5},{7,6},{9,8},{10,9},{11,10},{12... | collective-permute-start | bytes 98312 | tf_op jit(solution)/shard_map/ppermute | solution.py:21
  37.5 5.9 %collective-permute-start = (bf16[2,2,1,64,64]{4,3,1,0,2:T(8,128)(2,1)S(1)}, bf16[2,2,1,64,64]{4,3,1,0,2:T(8,128)(2,1)S(1)}, u32[]{:S(2)}, u32[]{:S(2)}) collective-permute-start(bf16[2,2,1,64,64]{4,3,1,0,2:T(8,128)(2,1)S(1)} %bitcast.110), channel_id=1, source_target_pairs={{0,1},{1,2},{2,3},{3,4},{4,5},{5,6},{6,7},{8,9},{9,10},{10,11},{11... | collective-permute-start | bytes 98312 | tf_op jit(solution)/shard_map/ppermute | solution.py:19
  45.3 9.1 %copy-start.2 = (bf16[64,256]{1,0:T(8,128)(2,1)S(1)}, bf16[64,256]{1,0:T(8,128)(2,1)}, u32[]{:S(2)}) copy-start(bf16[64,256]{1,0:T(8,128)(2,1)} %param.11) | copy-start | bytes 98308
  45.4 9.2 %copy-start.3 = (bf16[64,256]{1,0:T(8,128)(2,1)S(1)}, bf16[64,256]{1,0:T(8,128)(2,1)}, u32[]{:S(2)}) copy-start(bf16[64,256]{1,0:T(8,128)(2,1)} %param.12) | copy-start | bytes 98308
  45.4 10.0 %copy-start.5 = (f32[64]{0:T(128)S(1)}, f32[64]{0:T(128)}, u32[]{:S(2)}) copy-start(f32[64]{0:T(128)} %param.10) | copy-start | bytes 772
  45.4 10.7 %copy-start.4 = (bf16[64,64]{1,0:T(8,128)(2,1)S(1)}, bf16[64,64]{1,0:T(8,128)(2,1)}, u32[]{:S(2)}) copy-start(bf16[64,64]{1,0:T(8,128)(2,1)} %param.9) | copy-start | bytes 24580
  48.2 19.2 %all-to-all-start.1 = ((bf16[32,2,2048]{2,1,0:T(2,128)(2,1)}), bf16[32,2,2048]{2,1,0:T(2,128)(2,1)S(1)}, u32[]{:S(2)}, u32[]{:S(2)}) async-start(bf16[32,2,2048]{2,1,0:T(2,128)(2,1)} %reshape.112), calls=%async_computation.1 | async-start | bytes 524288 | tf_op jit(solution)/shard_map/all_to_all | solution.py:141

commit v11 on v8

--- a/solution.py
+++ b/solution.py
@@ -42,9 +42,9 @@
         value = jnp.dot(lhs, rhs, preferred_element_type=jnp.float32) + bias_ref[...]
         acts.append((0.5 * value * (1.0 + lax.erf(value * sqrt_half))).astype(jnp.bfloat16))
     act = jnp.concatenate(acts, axis=1)
-    gate = jnp.dot(gate_ref[...], act, preferred_element_type=jnp.float32)
+    half = jnp.dot(gate_ref[...], act, preferred_element_type=jnp.float32)
     upper = jnp.dot(up_ref[...], act, preferred_element_type=jnp.float32)
-    hidden = (0.5 * gate * (1.0 + jnp.tanh(0.5 * gate)) * upper).astype(jnp.bfloat16)
+    hidden = ((half + half * jnp.tanh(half)) * upper).astype(jnp.bfloat16)
     down = jnp.dot(down_ref[...], hidden, preferred_element_type=jnp.float32)
     for r in range(rows):
         grid = field_ref[r].astype(jnp.float32)
@@ -82,7 +82,7 @@
         lon_table.T,
         local_weight.T,
         local_bias.reshape(chans, 1),
-        gate_weight.T,
+        (gate_weight * 0.5).astype(gate_weight.dtype).T,
         up_weight.T,
         down_weight.T,
     )

time: 87.8 us -> 85.2 us (0.970)
  Pallas kernels: 20.6 us -> 18 us
    pallas_call x1, Pallas kernels: 20.6 us -> 18 us  [finish(): pl.pallas_call(finish_kernel, out_shape=jax.ShapeDtypeStruct(field.shape,...]
  transfers between devices with their start and end apart: 4 -> 4, of which waited for: 3 -> 3; matrix products, arithmetic and copies ran while one was open for 17% -> 18% of each run, Pallas kernels for 0% -> 0%
where the time goes in v11:
time: 85.2 us; the launch traced here: 84.9 us
  starting transfers between devices  23.3 us (27%)
  Pallas kernels  18 us (21%)
  local copies, waits for them, and re-layouts  14.7 us (17%)
  waiting for transfers between devices  13.9 us (16%)
  matrix products  12.4 us (15%)
  other arithmetic  2.46 us (3%)
    pallas_call x1, Pallas kernels, finish(): pl.pallas_call(finish_kernel, out_shape=jax.ShapeDtypeStruct(field.shape,...  18 us
    all_to_all x1, starting transfers between devices, body(): along = lax.all_to_all(along, 'rows', 0, 0, tiled=True).astype(jnp.float32)  11.8 us
    all_to_all x1, waiting for transfers between devices, body(): lax.all_to_all(values.astype(jnp.bfloat16), 'rows', 0, 0, tiled=True)  8.2 us
    slice x1, local copies, waits for them, and re-layouts, body(): spectral_weight[0]  7.34 us
    all_to_all x1, starting transfers between devices, body(): lax.all_to_all(values.astype(jnp.bfloat16), 'rows', 0, 0, tiled=True)  6.24 us
    all_to_all x1, waiting for transfers between devices, body(): along = lax.all_to_all(along, 'rows', 0, 0, tiled=True).astype(jnp.float32)  5.58 us
    dot_general x1, matrix products, body(): jnp.einsum('xm,blncx->mblnc', lon_table, field, preferred_element_type=jn...  5.24 us
    unnamed x17, local copies, waits for them, and re-layouts  4.47 us
  transfers between devices with their start and end apart: 4, of which 3 were waited for; matrix products, arithmetic and copies ran while one was open for 18% of the time, Pallas kernels for 0%

profile of v11, /device:TPU:25, one launch (start us, length us, event | category | flops | bytes accessed | tf_op | source)
XLA Modules:
  0.0 84.9 jit_solution(16049689487971586793)
XLA Ops:
  0.0 5.2 %fusion.5 = bf16[64,2,16,64]{3,0,2,1:T(8,128)(2,1)S(1)} fusion(bf16[2,1,16,64,1024]{4,3,2,1,0:T(8,128)(2,1)} %param.7, s32[64]{0:T(128)S(1)} %iota_add_fusion), kind=kOutput, calls=%fused_computation.8 | convolution fusion | flops 269680640 | bytes 4456704 | tf_op jit(solution)/shard_map/xm,blncx->mblnc/dot_general | solution.py:105
  5.2 0.6 copy.110
  5.9 1.1 %reshape.96 = bf16[32,2,2048]{2,1,0:T(2,128)(2,1)} reshape(bf16[32,1,2,2,16,64]{5,4,3,2,1,0:T(8,128)(2,1)S(1)} %bitcast.85) | data formatting | bytes 524288
  7.0 11.8 %all-to-all-start = ((bf16[32,2,2048]{2,1,0:T(2,128)(2,1)}), bf16[32,2,2048]{2,1,0:T(2,128)(2,1)S(1)}, u32[]{:S(2)}, u32[]{:S(2)}) async-start(bf16[32,2,2048]{2,1,0:T(2,128)(2,1)} %reshape.96), calls=%async_computation | async-start | bytes 524288 | tf_op jit(solution)/shard_map/all_to_all | solution.py:107
  18.7 7.3 %fusion.60 = (bf16[1,64,2,64,64]{4,3,2,1,0:T(8,128)(2,1)S(1)}, bf16[1,64,2,64,64]{4,3,2,1,0:T(8,128)(2,1)}, bf16[1,64,2,64,64]{4,3,2,1,0:T(8,128)(2,1)}) fusion(bf16[3,64,2,64,64]{4,3,2,1,0:T(8,128)(2,1)} %param.8), kind=kLoop, calls=%fused_computation.79 | loop fusion | bytes 6291456 | tf_op jit(solution)/shard_map/slice | solution.py:113
  26.1 5.6 %all-to-all-done = bf16[32,2,2048]{2,1,0:T(2,128)(2,1)S(1)} async-done(((bf16[32,2,2048]{2,1,0:T(2,128)(2,1)}), bf16[32,2,2048]{2,1,0:T(2,128)(2,1)S(1)}, u32[]{:S(2)}, u32[]{:S(2)}) %all-to-all-start) | async-done | bytes 262176 | tf_op jit(solution)/shard_map/all_to_all | solution.py:107
  31.7 0.4 reshape.97
  32.0 1.7 %fusion.12 = bf16[64,2,2,64]{3,0,2,1:T(8,128)(2,1)S(1)} fusion(bf16[32,2,2,1,16,64]{5,4,2,1,3,0:T(8,128)(2,1)S(1)} %bitcast.88, s32[64]{0:T(128)S(1)} %iota_add_fusion, s32[32,16]{0,1:T(8,128)S(1)} %multiply_add_fusion), kind=kOutput, calls=%fused_computation.15 | convolution fusion | flops 101203968 | bytes 297216 | tf_op jit(solution)/shard_map/sjblnc,snk->jblkc/dot_general | solution.py:108
  33.7 2.4 %collective-permute-start.1 = (bf16[2,2,1,64,64]{4,3,1,0,2:T(8,128)(2,1)S(1)}, bf16[2,2,1,64,64]{4,3,1,0,2:T(8,128)(2,1)S(1)}, u32[]{:S(2)}, u32[]{:S(2)}) collective-permute-start(bf16[2,2,1,64,64]{4,3,1,0,2:T(8,128)(2,1)S(1)} %bitcast.94), channel_id=1, source_target_pairs={{1,0},{2,1},{3,2},{4,3},{5,4},{6,5},{7,6},{9,8},{10,9},{11,10},{12... | collective-permute-start | bytes 98312 | tf_op jit(solution)/shard_map/ppermute | solution.py:21
  36.1 2.9 %collective-permute-start = (bf16[2,2,1,64,64]{4,3,1,0,2:T(8,128)(2,1)S(1)}, bf16[2,2,1,64,64]{4,3,1,0,2:T(8,128)(2,1)S(1)}, u32[]{:S(2)}, u32[]{:S(2)}) collective-permute-start(bf16[2,2,1,64,64]{4,3,1,0,2:T(8,128)(2,1)S(1)} %bitcast.95), channel_id=1, source_target_pairs={{0,1},{1,2},{2,3},{3,4},{4,5},{5,6},{6,7},{8,9},{9,10},{10,11},{11... | collective-permute-start | bytes 98312 | tf_op jit(solution)/shard_map/ppermute | solution.py:19
  39.0 2.2 %fusion.3 = f32[2,64,2,64]{3,2,1,0:T(2,128)S(1)} fusion(bf16[1,64,2,64,64]{4,3,2,1,0:T(8,128)(2,1)} %get-tuple-element.6, bf16[2,2,64,64]{3,2,1,0:T(8,128)(2,1)S(1)} %bitcast.96), kind=kOutput, calls=%fused_computation.5 | convolution fusion | flops 2097152 | bytes 1146880 | tf_op jit(solution)/shard_map/kjco,jblkc->jblko/dot_general | solution.py:117
  41.3 0.7 fusion.2
  41.9 0.1 collective-permute-done
  42.1 0.7 fusion.13
  42.7 0.0 copy-start.1
  42.7 0.0 copy-start.2
  42.7 0.0 copy-start.4
  42.7 0.0 copy-start.3
  42.8 1.9 %fusion.8 = bf16[32,2,2,1,16,64]{5,0,4,2,1,3:T(8,128)(2,1)S(1)} fusion(s32[64]{0:T(128)S(1)} %iota_add_fusion, s32[32,16]{0,1:T(8,128)S(1)} %multiply_add_fusion, bf16[2,2,64,64,1]{3,1,2,0,4:T(2,128)(2,1)S(1)} %fusion.13), kind=kOutput, calls=%fused_computation.10 | convolution fusion | flops 101318656 | bytes 297216 | tf_op jit(solution)/shard_map/rnk,jblko->rjblno/dot_general | solution.py:130
  44.6 0.2 copy.109
  44.9 1.1 %reshape.98 = bf16[32,2,2048]{2,1,0:T(2,128)(2,1)} reshape(bf16[32,1,2,2,16,64]{5,4,3,2,1,0:T(8,128)(2,1)S(1)} %bitcast.86) | data formatting | bytes 524288
  46.0 6.2 %all-to-all-start.1 = ((bf16[32,2,2048]{2,1,0:T(2,128)(2,1)}), bf16[32,2,2048]{2,1,0:T(2,128)(2,1)S(1)}, u32[]{:S(2)}, u32[]{:S(2)}) async-start(bf16[32,2,2048]{2,1,0:T(2,128)(2,1)} %reshape.98), calls=%async_computation.1 | async-start | bytes 524288 | tf_op jit(solution)/shard_map/all_to_all | solution.py:133
  52.2 0.1 copy.66
  52.4 0.7 copy.68
  53.1 0.7 copy.70.bias_ref
  53.8 0.7 copy.65
  54.5 0.6 multiply_bitcast_fusion.gate_ref
  55.1 1.8 %multiply_convert_fusion.lon_ref = bf16[64,1024]{1,0:T(8,128)(2,1)} fusion(s32[64]{0:T(128)S(1)} %iota_add_fusion), kind=kLoop, calls=%fused_computation.41 | loop fusion | flops 1114112 | bytes 131328 | tf_op jit(solution)/shard_map/convert_element_type | solution.py:98
  56.9 8.2 %all-to-all-done.1 = bf16[32,2,2048]{2,1,0:T(2,128)(2,1)S(1)} async-done(((bf16[32,2,2048]{2,1,0:T(2,128)(2,1)}), bf16[32,2,2048]{2,1,0:T(2,128)(2,1)S(1)}, u32[]{:S(2)}, u32[]{:S(2)}) %all-to-all-start.1) | async-done | bytes 262176 | tf_op jit(solution)/shard_map/all_to_all | solution.py:133
  65.1 0.4 reshape.99
  65.5 1.4 %copy.69.back_ref = bf16[32,64,64]{2,1,0:T(8,128)(2,1)} copy(bf16[32,64,64]{1,0,2:T(8,128)(2,1)S(1)} %bitcast.87) | data formatting | bytes 524288 | tf_op jit(solution)/shard_map/reshape;reshape | solution.py:140
  66.9 18.0 %shard_map.73 = bf16[32,64,1024]{2,1,0:T(8,128)(2,1)} custom-call(bf16[32,64,1024]{2,1,0:T(8,128)(2,1)} %bitcast.93, bf16[32,64,64]{2,1,0:T(8,128)(2,1)} %copy.69.back_ref, bf16[64,1024]{1,0:T(8,128)(2,1)} %multiply_convert_fusion.lon_ref, bf16[64,64]{1,0:T(8,128)(2,1)} %bitcast.91, f32[64,1]{1,0:T(8,128)} %copy.70.bias_ref, ...), custom_call_target="tpu_custom_call" | custom-call | flops 3758096384 | bytes 8650752 | tf_op jit(solution)/shard_map/pallas_call | solution.py:59
  (9 shorter events, 0.0 us)
Async XLA Ops:
  7.0 24.7 %all-to-all-start = ((bf16[32,2,2048]{2,1,0:T(2,128)(2,1)}), bf16[32,2,2048]{2,1,0:T(2,128)(2,1)S(1)}, u32[]{:S(2)}, u32[]{:S(2)}) async-start(bf16[32,2,2048]{2,1,0:T(2,128)(2,1)} %reshape.96), calls=%async_computation | async-start | bytes 524288 | tf_op jit(solution)/shard_map/all_to_all | solution.py:107
  32.0 9.3 %copy-start = (bf16[1,64,2,64,64]{4,3,2,1,0:T(8,128)(2,1)S(1)}, bf16[1,64,2,64,64]{4,3,2,1,0:T(8,128)(2,1)}, u32[]{:S(2)}) copy-start(bf16[1,64,2,64,64]{4,3,2,1,0:T(8,128)(2,1)} %get-tuple-element.7) | copy-start | bytes 3145732
  33.7 7.5 %collective-permute-start.1 = (bf16[2,2,1,64,64]{4,3,1,0,2:T(8,128)(2,1)S(1)}, bf16[2,2,1,64,64]{4,3,1,0,2:T(8,128)(2,1)S(1)}, u32[]{:S(2)}, u32[]{:S(2)}) collective-permute-start(bf16[2,2,1,64,64]{4,3,1,0,2:T(8,128)(2,1)S(1)} %bitcast.94), channel_id=1, source_target_pairs={{1,0},{2,1},{3,2},{4,3},{5,4},{6,5},{7,6},{9,8},{10,9},{11,10},{12... | collective-permute-start | bytes 98312 | tf_op jit(solution)/shard_map/ppermute | solution.py:21
  36.1 5.9 %collective-permute-start = (bf16[2,2,1,64,64]{4,3,1,0,2:T(8,128)(2,1)S(1)}, bf16[2,2,1,64,64]{4,3,1,0,2:T(8,128)(2,1)S(1)}, u32[]{:S(2)}, u32[]{:S(2)}) collective-permute-start(bf16[2,2,1,64,64]{4,3,1,0,2:T(8,128)(2,1)S(1)} %bitcast.95), channel_id=1, source_target_pairs={{0,1},{1,2},{2,3},{3,4},{4,5},{5,6},{6,7},{8,9},{9,10},{10,11},{11... | collective-permute-start | bytes 98312 | tf_op jit(solution)/shard_map/ppermute | solution.py:19
  42.7 9.5 %copy-start.1 = (bf16[64,256]{1,0:T(8,128)(2,1)S(1)}, bf16[64,256]{1,0:T(8,128)(2,1)}, u32[]{:S(2)}) copy-start(bf16[64,256]{1,0:T(8,128)(2,1)} %param.11) | copy-start | bytes 98308
  42.7 9.6 %copy-start.2 = (bf16[64,256]{1,0:T(8,128)(2,1)S(1)}, bf16[64,256]{1,0:T(8,128)(2,1)}, u32[]{:S(2)}) copy-start(bf16[64,256]{1,0:T(8,128)(2,1)} %param.12) | copy-start | bytes 98308
  42.7 10.3 %copy-start.4 = (f32[64]{0:T(128)S(1)}, f32[64]{0:T(128)}, u32[]{:S(2)}) copy-start(f32[64]{0:T(128)} %param.10) | copy-start | bytes 772
  42.7 11.0 %copy-start.3 = (bf16[64,64]{1,0:T(8,128)(2,1)S(1)}, bf16[64,64]{1,0:T(8,128)(2,1)}, u32[]{:S(2)}) copy-start(bf16[64,64]{1,0:T(8,128)(2,1)} %param.9) | copy-start | bytes 24580
  46.0 19.2 %all-to-all-start.1 = ((bf16[32,2,2048]{2,1,0:T(2,128)(2,1)}), bf16[32,2,2048]{2,1,0:T(2,128)(2,1)S(1)}, u32[]{:S(2)}, u32[]{:S(2)}) async-start(bf16[32,2,2048]{2,1,0:T(2,128)(2,1)} %reshape.98), calls=%async_computation.1 | async-start | bytes 524288 | tf_op jit(solution)/shard_map/all_to_all | solution.py:133

commit v12 on v11

--- a/solution.py
+++ b/solution.py
@@ -32,7 +32,7 @@
     return (jnp.cos(angle) + jnp.sin(angle)) / math.sqrt(count)
 
 
-def finish_kernel(field_ref, back_ref, lon_ref, local_ref, bias_ref, gate_ref, up_ref, down_ref, out_ref):
+def finish_kernel(field_ref, back_ref, lon_ref, local_ref, bias_ref, gate_up_ref, down_ref, out_ref):
     sqrt_half = math.sqrt(0.5)
     rows, _, lon_cells = field_ref.shape
     acts = []
@@ -42,8 +42,9 @@
         value = jnp.dot(lhs, rhs, preferred_element_type=jnp.float32) + bias_ref[...]
         acts.append((0.5 * value * (1.0 + lax.erf(value * sqrt_half))).astype(jnp.bfloat16))
     act = jnp.concatenate(acts, axis=1)
-    half = jnp.dot(gate_ref[...], act, preferred_element_type=jnp.float32)
-    upper = jnp.dot(up_ref[...], act, preferred_element_type=jnp.float32)
+    both = jnp.dot(gate_up_ref[...], act, preferred_element_type=jnp.float32)
+    hid = gate_up_ref.shape[0] // 2
+    half, upper = both[:hid], both[hid:]
     hidden = ((half + half * jnp.tanh(half)) * upper).astype(jnp.bfloat16)
     down = jnp.dot(down_ref[...], hidden, preferred_element_type=jnp.float32)
     for r in range(rows):
@@ -51,7 +52,7 @@
         out_ref[r] = (grid + down[:, r * lon_cells : (r + 1) * lon_cells]).astype(out_ref.dtype)
 
 
-def finish(field, back, lon_table, local_weight, local_bias, gate_weight, up_weight, down_weight, block=4):
+def finish(field, back, lon_table, local_weight, local_bias, gate_weight, up_weight, down_weight, block=8):
     rows, chans, lon_cells = field.shape
     modes = back.shape[2]
     hid = gate_weight.shape[1]
@@ -66,8 +67,7 @@
             pl.BlockSpec((modes, lon_cells), whole),
             pl.BlockSpec((chans, chans), whole),
             pl.BlockSpec((chans, 1), whole),
-            pl.BlockSpec((hid, chans), whole),
-            pl.BlockSpec((hid, chans), whole),
+            pl.BlockSpec((2 * hid, chans), whole),
             pl.BlockSpec((chans, hid), whole),
         ],
         out_specs=pl.BlockSpec((block, chans, lon_cells), lambda i: (i, 0, 0)),
@@ -82,8 +82,7 @@
         lon_table.T,
         local_weight.T,
         local_bias.reshape(chans, 1),
-        (gate_weight * 0.5).astype(gate_weight.dtype).T,
-        up_weight.T,
+        jnp.concatenate([(gate_weight * 0.5).astype(gate_weight.dtype), up_weight], axis=1).T,
         down_weight.T,
     )
 

time: 85.2 us -> 85.5 us (level)
  starting transfers between devices: 23.3 us -> 24.9 us
  Pallas kernels: 18 us -> 16.6 us
    all_to_all x1, waiting for transfers between devices: 8.2 us -> 10.4 us  [body(): lax.all_to_all(values.astype(jnp.bfloat16), 'rows', 0, 0, tiled=True)]
    all_to_all x1, starting transfers between devices: 6.24 us -> 7.89 us  [body(): lax.all_to_all(values.astype(jnp.bfloat16), 'rows', 0, 0, tiled=True)]
    all_to_all x1, waiting for transfers between devices: 5.58 us -> 3.93 us  [body(): along = lax.all_to_all(along, 'rows', 0, 0, tiled=True).astype(jnp.float32)]
    pallas_call x1, Pallas kernels: 18 us -> 16.6 us  [finish(): pl.pallas_call(finish_kernel, out_shape=jax.ShapeDtypeStruct(field.shape,...]
  transfers between devices with their start and end apart: 4 -> 4, of which waited for: 3 -> 3; matrix products, arithmetic and copies ran while one was open for 18% -> 17% of each run, Pallas kernels for 0% -> 0%
where the time goes in v12:
time: 85.5 us; the launch traced here: 85.1 us
  starting transfers between devices  24.9 us (29%)
  Pallas kernels  16.6 us (19%)
  waiting for transfers between devices  14.5 us (17%)
  local copies, waits for them, and re-layouts  14.1 us (16%)
  matrix products  12.4 us (15%)
  other arithmetic  2.52 us (3%)
    pallas_call x1, Pallas kernels, finish(): pl.pallas_call(finish_kernel, out_shape=jax.ShapeDtypeStruct(field.shape,...  16.6 us
    all_to_all x1, starting transfers between devices, body(): along = lax.all_to_all(along, 'rows', 0, 0, tiled=True).astype(jnp.float32)  11.8 us
    all_to_all x1, waiting for transfers between devices, body(): lax.all_to_all(values.astype(jnp.bfloat16), 'rows', 0, 0, tiled=True)  10.4 us
    all_to_all x1, starting transfers between devices, body(): lax.all_to_all(values.astype(jnp.bfloat16), 'rows', 0, 0, tiled=True)  7.89 us
    slice x1, local copies, waits for them, and re-layouts, body(): spectral_weight[0]  7.34 us
    dot_general x1, matrix products, body(): jnp.einsum('xm,blncx->mblnc', lon_table, field, preferred_element_type=jn...  5.24 us
    all_to_all x1, waiting for transfers between devices, body(): along = lax.all_to_all(along, 'rows', 0, 0, tiled=True).astype(jnp.float32)  3.93 us
    unnamed x17, local copies, waits for them, and re-layouts  3.85 us
  transfers between devices with their start and end apart: 4, of which 3 were waited for; matrix products, arithmetic and copies ran while one was open for 17% of the time, Pallas kernels for 0%

profile of v12, /device:TPU:25, one launch (start us, length us, event | category | flops | bytes accessed | tf_op | source)
XLA Modules:
  0.0 85.1 jit_solution(16114557421609629766)
XLA Ops:
  0.0 5.2 %fusion.5 = bf16[64,2,16,64]{3,0,2,1:T(8,128)(2,1)S(1)} fusion(bf16[2,1,16,64,1024]{4,3,2,1,0:T(8,128)(2,1)} %param.7, s32[64]{0:T(128)S(1)} %iota_add_fusion), kind=kOutput, calls=%fused_computation.8 | convolution fusion | flops 269680640 | bytes 4456704 | tf_op jit(solution)/shard_map/xm,blncx->mblnc/dot_general | solution.py:104
  5.2 0.0 copy-start.2
  5.3 0.0 copy-start.4
  5.3 0.0 copy-start.3
  5.3 0.6 copy.110
  5.9 1.1 %reshape.96 = bf16[32,2,2048]{2,1,0:T(2,128)(2,1)} reshape(bf16[32,1,2,2,16,64]{5,4,3,2,1,0:T(8,128)(2,1)S(1)} %bitcast.84) | data formatting | bytes 524288
  7.0 11.8 %all-to-all-start = ((bf16[32,2,2048]{2,1,0:T(2,128)(2,1)}), bf16[32,2,2048]{2,1,0:T(2,128)(2,1)S(1)}, u32[]{:S(2)}, u32[]{:S(2)}) async-start(bf16[32,2,2048]{2,1,0:T(2,128)(2,1)} %reshape.96), calls=%async_computation | async-start | bytes 524288 | tf_op jit(solution)/shard_map/all_to_all | solution.py:106
  18.8 0.1 copy.66
  18.9 0.1 copy.68
  19.0 0.7 copy.70.bias_ref
  19.7 0.7 copy.65
  20.4 7.3 %fusion.60 = (bf16[1,64,2,64,64]{4,3,2,1,0:T(8,128)(2,1)S(1)}, bf16[1,64,2,64,64]{4,3,2,1,0:T(8,128)(2,1)}, bf16[1,64,2,64,64]{4,3,2,1,0:T(8,128)(2,1)}) fusion(bf16[3,64,2,64,64]{4,3,2,1,0:T(8,128)(2,1)} %param.8), kind=kLoop, calls=%fused_computation.80 | loop fusion | bytes 6291456 | tf_op jit(solution)/shard_map/slice | solution.py:112
  27.8 3.9 %all-to-all-done = bf16[32,2,2048]{2,1,0:T(2,128)(2,1)S(1)} async-done(((bf16[32,2,2048]{2,1,0:T(2,128)(2,1)}), bf16[32,2,2048]{2,1,0:T(2,128)(2,1)S(1)}, u32[]{:S(2)}, u32[]{:S(2)}) %all-to-all-start) | async-done | bytes 262176 | tf_op jit(solution)/shard_map/all_to_all | solution.py:106
  31.7 0.4 reshape.97
  32.1 1.7 %fusion.12 = bf16[64,2,2,64]{3,0,2,1:T(8,128)(2,1)S(1)} fusion(bf16[32,2,2,1,16,64]{5,4,2,1,3,0:T(8,128)(2,1)S(1)} %bitcast.87, s32[64]{0:T(128)S(1)} %iota_add_fusion, s32[32,16]{0,1:T(8,128)S(1)} %multiply_add_fusion), kind=kOutput, calls=%fused_computation.15 | convolution fusion | flops 101203968 | bytes 297216 | tf_op jit(solution)/shard_map/sjblnc,snk->jblkc/dot_general | solution.py:107
  33.8 2.4 %collective-permute-start.1 = (bf16[2,2,1,64,64]{4,3,1,0,2:T(8,128)(2,1)S(1)}, bf16[2,2,1,64,64]{4,3,1,0,2:T(8,128)(2,1)S(1)}, u32[]{:S(2)}, u32[]{:S(2)}) collective-permute-start(bf16[2,2,1,64,64]{4,3,1,0,2:T(8,128)(2,1)S(1)} %bitcast.92), channel_id=1, source_target_pairs={{1,0},{2,1},{3,2},{4,3},{5,4},{6,5},{7,6},{9,8},{10,9},{11,10},{12... | collective-permute-start | bytes 98312 | tf_op jit(solution)/shard_map/ppermute | solution.py:21
  36.2 2.9 %collective-permute-start = (bf16[2,2,1,64,64]{4,3,1,0,2:T(8,128)(2,1)S(1)}, bf16[2,2,1,64,64]{4,3,1,0,2:T(8,128)(2,1)S(1)}, u32[]{:S(2)}, u32[]{:S(2)}) collective-permute-start(bf16[2,2,1,64,64]{4,3,1,0,2:T(8,128)(2,1)S(1)} %bitcast.93), channel_id=1, source_target_pairs={{0,1},{1,2},{2,3},{3,4},{4,5},{5,6},{6,7},{8,9},{9,10},{10,11},{11... | collective-permute-start | bytes 98312 | tf_op jit(solution)/shard_map/ppermute | solution.py:19
  39.1 2.2 %fusion.3 = f32[2,64,2,64]{3,2,1,0:T(2,128)S(1)} fusion(bf16[1,64,2,64,64]{4,3,2,1,0:T(8,128)(2,1)} %get-tuple-element.6, bf16[2,2,64,64]{3,2,1,0:T(8,128)(2,1)S(1)} %bitcast.94), kind=kOutput, calls=%fused_computation.5 | convolution fusion | flops 2097152 | bytes 1146880 | tf_op jit(solution)/shard_map/kjco,jblkc->jblko/dot_general | solution.py:116
  41.3 0.0 collective-permute-done.1
  41.3 0.7 fusion.2
  42.0 0.1 collective-permute-done
  42.1 0.7 fusion.13
  42.8 1.9 %fusion.8 = bf16[32,2,2,1,16,64]{5,0,4,2,1,3:T(8,128)(2,1)S(1)} fusion(s32[64]{0:T(128)S(1)} %iota_add_fusion, s32[32,16]{0,1:T(8,128)S(1)} %multiply_add_fusion, bf16[2,2,64,64,1]{3,1,2,0,4:T(2,128)(2,1)S(1)} %fusion.13), kind=kOutput, calls=%fused_computation.10 | convolution fusion | flops 101318656 | bytes 297216 | tf_op jit(solution)/shard_map/rnk,jblko->rjblno/dot_general | solution.py:129
  44.6 0.2 copy.109
  44.9 1.1 %reshape.98 = bf16[32,2,2048]{2,1,0:T(2,128)(2,1)} reshape(bf16[32,1,2,2,16,64]{5,4,3,2,1,0:T(8,128)(2,1)S(1)} %bitcast.85) | data formatting | bytes 524288
  46.0 7.9 %all-to-all-start.1 = ((bf16[32,2,2048]{2,1,0:T(2,128)(2,1)}), bf16[32,2,2048]{2,1,0:T(2,128)(2,1)S(1)}, u32[]{:S(2)}, u32[]{:S(2)}) async-start(bf16[32,2,2048]{2,1,0:T(2,128)(2,1)} %reshape.98), calls=%async_computation.1 | async-start | bytes 524288 | tf_op jit(solution)/shard_map/all_to_all | solution.py:132
  53.9 0.7 maximum_bitcast_fusion.gate_up_ref
  54.6 1.8 %multiply_convert_fusion.lon_ref = bf16[64,1024]{1,0:T(8,128)(2,1)} fusion(s32[64]{0:T(128)S(1)} %iota_add_fusion), kind=kLoop, calls=%fused_computation.41 | loop fusion | flops 1114112 | bytes 131328 | tf_op jit(solution)/shard_map/convert_element_type | solution.py:97
  56.4 10.4 %all-to-all-done.1 = bf16[32,2,2048]{2,1,0:T(2,128)(2,1)S(1)} async-done(((bf16[32,2,2048]{2,1,0:T(2,128)(2,1)}), bf16[32,2,2048]{2,1,0:T(2,128)(2,1)S(1)}, u32[]{:S(2)}, u32[]{:S(2)}) %all-to-all-start.1) | async-done | bytes 262176 | tf_op jit(solution)/shard_map/all_to_all | solution.py:132
  66.8 0.4 reshape.99
  67.2 1.4 %copy.69.back_ref = bf16[32,64,64]{2,1,0:T(8,128)(2,1)} copy(bf16[32,64,64]{1,0,2:T(8,128)(2,1)S(1)} %bitcast.86) | data formatting | bytes 524288 | tf_op jit(solution)/shard_map/reshape;reshape | solution.py:139
  68.5 16.6 %shard_map.73 = bf16[32,64,1024]{2,1,0:T(8,128)(2,1)} custom-call(bf16[32,64,1024]{2,1,0:T(8,128)(2,1)} %bitcast.91, bf16[32,64,64]{2,1,0:T(8,128)(2,1)} %copy.69.back_ref, bf16[64,1024]{1,0:T(8,128)(2,1)} %multiply_convert_fusion.lon_ref, bf16[64,64]{1,0:T(8,128)(2,1)} %bitcast.89, f32[64,1]{1,0:T(8,128)} %copy.70.bias_ref, ...), custom_call_target="tpu_custom_call" | custom-call | flops 3758096384 | bytes 8650752 | tf_op jit(solution)/shard_map/pallas_call | solution.py:60
  (10 shorter events, 0.0 us)
Async XLA Ops:
  5.2 13.5 %copy-start.1 = (bf16[64,256]{1,0:T(8,128)(2,1)S(1)}, bf16[64,256]{1,0:T(8,128)(2,1)}, u32[]{:S(2)}) copy-start(bf16[64,256]{1,0:T(8,128)(2,1)} %param.11) | copy-start | bytes 98308
  5.2 13.6 %copy-start.2 = (bf16[64,256]{1,0:T(8,128)(2,1)S(1)}, bf16[64,256]{1,0:T(8,128)(2,1)}, u32[]{:S(2)}) copy-start(bf16[64,256]{1,0:T(8,128)(2,1)} %param.12) | copy-start | bytes 98308
  5.3 13.8 %copy-start.4 = (f32[64]{0:T(128)S(1)}, f32[64]{0:T(128)}, u32[]{:S(2)}) copy-start(f32[64]{0:T(128)} %param.10) | copy-start | bytes 772
  5.3 14.5 %copy-start.3 = (bf16[64,64]{1,0:T(8,128)(2,1)S(1)}, bf16[64,64]{1,0:T(8,128)(2,1)}, u32[]{:S(2)}) copy-start(bf16[64,64]{1,0:T(8,128)(2,1)} %param.9) | copy-start | bytes 24580
  7.0 24.7 %all-to-all-start = ((bf16[32,2,2048]{2,1,0:T(2,128)(2,1)}), bf16[32,2,2048]{2,1,0:T(2,128)(2,1)S(1)}, u32[]{:S(2)}, u32[]{:S(2)}) async-start(bf16[32,2,2048]{2,1,0:T(2,128)(2,1)} %reshape.96), calls=%async_computation | async-start | bytes 524288 | tf_op jit(solution)/shard_map/all_to_all | solution.py:106
  32.1 9.3 %copy-start = (bf16[1,64,2,64,64]{4,3,2,1,0:T(8,128)(2,1)S(1)}, bf16[1,64,2,64,64]{4,3,2,1,0:T(8,128)(2,1)}, u32[]{:S(2)}) copy-start(bf16[1,64,2,64,64]{4,3,2,1,0:T(8,128)(2,1)} %get-tuple-element.7) | copy-start | bytes 3145732
  33.8 7.5 %collective-permute-start.1 = (bf16[2,2,1,64,64]{4,3,1,0,2:T(8,128)(2,1)S(1)}, bf16[2,2,1,64,64]{4,3,1,0,2:T(8,128)(2,1)S(1)}, u32[]{:S(2)}, u32[]{:S(2)}) collective-permute-start(bf16[2,2,1,64,64]{4,3,1,0,2:T(8,128)(2,1)S(1)} %bitcast.92), channel_id=1, source_target_pairs={{1,0},{2,1},{3,2},{4,3},{5,4},{6,5},{7,6},{9,8},{10,9},{11,10},{12... | collective-permute-start | bytes 98312 | tf_op jit(solution)/shard_map/ppermute | solution.py:21
  36.2 5.9 %collective-permute-start = (bf16[2,2,1,64,64]{4,3,1,0,2:T(8,128)(2,1)S(1)}, bf16[2,2,1,64,64]{4,3,1,0,2:T(8,128)(2,1)S(1)}, u32[]{:S(2)}, u32[]{:S(2)}) collective-permute-start(bf16[2,2,1,64,64]{4,3,1,0,2:T(8,128)(2,1)S(1)} %bitcast.93), channel_id=1, source_target_pairs={{0,1},{1,2},{2,3},{3,4},{4,5},{5,6},{6,7},{8,9},{9,10},{10,11},{11... | collective-permute-start | bytes 98312 | tf_op jit(solution)/shard_map/ppermute | solution.py:19
  46.0 20.8 %all-to-all-start.1 = ((bf16[32,2,2048]{2,1,0:T(2,128)(2,1)}), bf16[32,2,2048]{2,1,0:T(2,128)(2,1)S(1)}, u32[]{:S(2)}, u32[]{:S(2)}) async-start(bf16[32,2,2048]{2,1,0:T(2,128)(2,1)} %reshape.98), calls=%async_computation.1 | async-start | bytes 524288 | tf_op jit(solution)/shard_map/all_to_all | solution.py:132

commit v13 on v12

--- a/solution.py
+++ b/solution.py
@@ -107,23 +107,9 @@
     modes = jnp.einsum("sjblnc,snk->jblkc", along, lat_table, precision=high)
     modes = modes.astype(jnp.bfloat16)
     padded = extended(modes, (("lev", 2),), 1)
+    stacked = jnp.stack([padded[:, :, shift : shift + levels] for shift in range(3)])
     mixed = jnp.einsum(
-        "kjco,jblkc->jblko",
-        spectral_weight[0],
-        padded[:, :, 0:levels],
-        preferred_element_type=jnp.float32,
-    )
-    mixed = mixed + jnp.einsum(
-        "kjco,jblkc->jblko",
-        spectral_weight[1],
-        padded[:, :, 1 : levels + 1],
-        preferred_element_type=jnp.float32,
-    )
-    mixed = mixed + jnp.einsum(
-        "kjco,jblkc->jblko",
-        spectral_weight[2],
-        padded[:, :, 2 : levels + 2],
-        preferred_element_type=jnp.float32,
+        "dkjco,djblkc->jblko", spectral_weight, stacked, preferred_element_type=jnp.float32
     )
     mixed_b = mixed.astype(jnp.bfloat16)
     values = jnp.einsum(

time: 85.5 us -> 87.9 us (1.028)
  waiting for transfers between devices: 14.5 us -> 24.7 us
  local copies, waits for them, and re-layouts: 14.1 us -> 6.74 us
  starting transfers between devices: 24.9 us -> 23.2 us
  matrix products: 12.4 us -> 13.5 us
    all_to_all x1, waiting for transfers between devices: 3.93 us -> 12.9 us  [body(): along = lax.all_to_all(along, 'rows', 0, 0, tiled=True).astype(jnp.float32)]
    slice x1 -> x0, local copies, waits for them, and re-layouts: 7.34 us -> none  [body(): spectral_weight[0]]
    all_to_all x1, starting transfers between devices: 7.89 us -> 6.18 us  [body(): lax.all_to_all(values.astype(jnp.bfloat16), 'rows', 0, 0, tiled=True)]
    ppermute x1, waiting for transfers between devices: 0.11 us -> 1.36 us  [extended(): lax.ppermute(tail, axis, [(i, (i + 1) % count) for i in range(ends)])]
    dot_general x3 -> x1, matrix products: 3.55 us -> 4.65 us  [body(): jnp.einsum('dkjco,djblkc->jblko', spectral_weight, stacked, preferred_ele...]
    unnamed x17 -> x15, local copies, waits for them, and re-layouts: 3.85 us -> 3.84 us
  transfers between devices with their start and end apart: 4 -> 4, of which waited for: 3 -> 3; matrix products, arithmetic and copies ran while one was open for 17% -> 5% of each run, Pallas kernels for 0% -> 0%
where the time goes in v13:
time: 87.9 us; the launch traced here: 87.5 us
  waiting for transfers between devices  24.7 us (28%)
  starting transfers between devices  23.2 us (26%)
  Pallas kernels  16.6 us (19%)
  matrix products  13.5 us (15%)
  local copies, waits for them, and re-layouts  6.74 us (8%)
  other arithmetic  2.57 us (3%)
    pallas_call x1, Pallas kernels, finish(): pl.pallas_call(finish_kernel, out_shape=jax.ShapeDtypeStruct(field.shape,...  16.6 us
    all_to_all x1, waiting for transfers between devices, body(): along = lax.all_to_all(along, 'rows', 0, 0, tiled=True).astype(jnp.float32)  12.9 us
    all_to_all x1, starting transfers between devices, body(): along = lax.all_to_all(along, 'rows', 0, 0, tiled=True).astype(jnp.float32)  11.8 us
    all_to_all x1, waiting for transfers between devices, body(): lax.all_to_all(values.astype(jnp.bfloat16), 'rows', 0, 0, tiled=True)  10.4 us
    all_to_all x1, starting transfers between devices, body(): lax.all_to_all(values.astype(jnp.bfloat16), 'rows', 0, 0, tiled=True)  6.18 us
    dot_general x1, matrix products, body(): jnp.einsum('xm,blncx->mblnc', lon_table, field, preferred_element_type=jn...  5.27 us
    dot_general x1, matrix products, body(): jnp.einsum('dkjco,djblkc->jblko', spectral_weight, stacked, preferred_ele...  4.65 us
    unnamed x15, local copies, waits for them, and re-layouts  3.84 us
  transfers between devices with their start and end apart: 4, of which 3 were waited for; matrix products, arithmetic and copies ran while one was open for 5% of the time, Pallas kernels for 0%

profile of v13, /device:TPU:25, one launch (start us, length us, event | category | flops | bytes accessed | tf_op | source)
XLA Modules:
  0.0 87.5 jit_solution(7995307703571784594)
XLA Ops:
  0.0 0.0 copy-start.2
  0.0 0.0 copy-start.1
  0.0 5.3 %fusion.4 = bf16[64,2,16,64]{3,0,2,1:T(8,128)(2,1)S(1)} fusion(bf16[2,1,16,64,1024]{4,3,2,1,0:T(8,128)(2,1)} %param.7, s32[64]{0:T(128)S(1)} %iota_add_fusion), kind=kOutput, calls=%fused_computation.4 | convolution fusion | flops 269680640 | bytes 4456704 | tf_op jit(solution)/shard_map/xm,blncx->mblnc/dot_general | solution.py:104
  5.3 0.6 copy.82
  5.9 1.1 %reshape.85 = bf16[32,2,2048]{2,1,0:T(2,128)(2,1)} reshape(bf16[32,1,2,2,16,64]{5,4,3,2,1,0:T(8,128)(2,1)S(1)} %bitcast.76) | data formatting | bytes 524288
  7.0 11.8 %all-to-all-start = ((bf16[32,2,2048]{2,1,0:T(2,128)(2,1)}), bf16[32,2,2048]{2,1,0:T(2,128)(2,1)S(1)}, u32[]{:S(2)}, u32[]{:S(2)}) async-start(bf16[32,2,2048]{2,1,0:T(2,128)(2,1)} %reshape.85), calls=%async_computation | async-start | bytes 524288 | tf_op jit(solution)/shard_map/all_to_all | solution.py:106
  18.8 12.9 %all-to-all-done = bf16[32,2,2048]{2,1,0:T(2,128)(2,1)S(1)} async-done(((bf16[32,2,2048]{2,1,0:T(2,128)(2,1)}), bf16[32,2,2048]{2,1,0:T(2,128)(2,1)S(1)}, u32[]{:S(2)}, u32[]{:S(2)}) %all-to-all-start) | async-done | bytes 262176 | tf_op jit(solution)/shard_map/all_to_all | solution.py:106
  31.7 0.3 reshape.86
  32.1 1.7 %fusion.14 = bf16[64,2,2,64]{3,0,2,1:T(8,128)(2,1)S(1)} fusion(bf16[32,2,2,1,16,64]{5,4,2,1,3,0:T(8,128)(2,1)S(1)} %bitcast.79, s32[64]{0:T(128)S(1)} %iota_add_fusion, s32[32,16]{0,1:T(8,128)S(1)} %multiply_add_fusion), kind=kOutput, calls=%fused_computation.10 | convolution fusion | flops 101203968 | bytes 297216 | tf_op jit(solution)/shard_map/sjblnc,snk->jblkc/dot_general | solution.py:107
  33.8 2.4 %collective-permute-start.1 = (bf16[2,2,1,64,64]{4,3,1,0,2:T(8,128)(2,1)S(1)}, bf16[2,2,1,64,64]{4,3,1,0,2:T(8,128)(2,1)S(1)}, u32[]{:S(2)}, u32[]{:S(2)}) collective-permute-start(bf16[2,2,1,64,64]{4,3,1,0,2:T(8,128)(2,1)S(1)} %bitcast.81), channel_id=1, source_target_pairs={{1,0},{2,1},{3,2},{4,3},{5,4},{6,5},{7,6},{9,8},{10,9},{11,10},{12... | collective-permute-start | bytes 98312 | tf_op jit(solution)/shard_map/ppermute | solution.py:21
  36.2 2.9 %collective-permute-start = (bf16[2,2,1,64,64]{4,3,1,0,2:T(8,128)(2,1)S(1)}, bf16[2,2,1,64,64]{4,3,1,0,2:T(8,128)(2,1)S(1)}, u32[]{:S(2)}, u32[]{:S(2)}) collective-permute-start(bf16[2,2,1,64,64]{4,3,1,0,2:T(8,128)(2,1)S(1)} %bitcast.82), channel_id=1, source_target_pairs={{0,1},{1,2},{2,3},{3,4},{4,5},{5,6},{6,7},{8,9},{9,10},{10,11},{11... | collective-permute-start | bytes 98312 | tf_op jit(solution)/shard_map/ppermute | solution.py:19
  39.1 0.0 copy-done.2
  39.1 0.7 copy.49
  39.8 0.0 copy-done.3
  39.8 0.7 copy.54.bias_ref
  40.5 0.0 copy-done
  40.5 0.1 copy.50
  40.6 0.0 copy-done.1
  40.6 0.1 copy.52
  40.8 0.0 collective-permute-done.1
  40.8 1.4 %collective-permute-done = bf16[2,2,1,64,64]{4,3,1,0,2:T(8,128)(2,1)S(1)} collective-permute-done((bf16[2,2,1,64,64]{4,3,1,0,2:T(8,128)(2,1)S(1)}, bf16[2,2,1,64,64]{4,3,1,0,2:T(8,128)(2,1)S(1)}, u32[]{:S(2)}, u32[]{:S(2)}) %collective-permute-start) | collective-permute-done | bytes 32800 | tf_op jit(solution)/shard_map/ppermute | solution.py:19
  42.2 4.6 %fusion.15 = bf16[2,2,64,64,1]{3,1,2,0,4:T(2,128)(2,1)S(1)} fusion(bf16[3,64,2,64,64]{4,3,2,1,0:T(8,128)(2,1)} %param.8, bf16[3,2,2,64,64]{4,3,2,1,0:T(8,128)(2,1)S(1)} %maximum_bitcast_fusion), kind=kOutput, calls=%fused_computation.11 | convolution fusion | flops 6307840 | bytes 3276800 | tf_op jit(solution)/shard_map/dkjco,djblkc->jblko/dot_general | solution.py:111
  46.8 1.9 %fusion.7 = bf16[32,2,2,1,16,64]{5,0,4,2,1,3:T(8,128)(2,1)S(1)} fusion(s32[64]{0:T(128)S(1)} %iota_add_fusion, s32[32,16]{0,1:T(8,128)S(1)} %multiply_add_fusion, bf16[2,2,64,64,1]{3,1,2,0,4:T(2,128)(2,1)S(1)} %fusion.15), kind=kOutput, calls=%fused_computation.6 | convolution fusion | flops 101318656 | bytes 297216 | tf_op jit(solution)/shard_map/rnk,jblko->rjblno/dot_general | solution.py:115
  48.7 0.2 copy.81
  48.9 1.1 %reshape.87 = bf16[32,2,2048]{2,1,0:T(2,128)(2,1)} reshape(bf16[32,1,2,2,16,64]{5,4,3,2,1,0:T(8,128)(2,1)S(1)} %bitcast.77) | data formatting | bytes 524288
  50.0 6.2 %all-to-all-start.1 = ((bf16[32,2,2048]{2,1,0:T(2,128)(2,1)}), bf16[32,2,2048]{2,1,0:T(2,128)(2,1)S(1)}, u32[]{:S(2)}, u32[]{:S(2)}) async-start(bf16[32,2,2048]{2,1,0:T(2,128)(2,1)} %reshape.87), calls=%async_computation.1 | async-start | bytes 524288 | tf_op jit(solution)/shard_map/all_to_all | solution.py:118
  56.2 0.7 maximum_bitcast_fusion.1.gate_up_ref
  56.9 1.8 %multiply_convert_fusion.lon_ref = bf16[64,1024]{1,0:T(8,128)(2,1)} fusion(s32[64]{0:T(128)S(1)} %iota_add_fusion), kind=kLoop, calls=%fused_computation.36 | loop fusion | flops 1114112 | bytes 131328 | tf_op jit(solution)/shard_map/convert_element_type | solution.py:97
  58.7 10.4 %all-to-all-done.1 = bf16[32,2,2048]{2,1,0:T(2,128)(2,1)S(1)} async-done(((bf16[32,2,2048]{2,1,0:T(2,128)(2,1)}), bf16[32,2,2048]{2,1,0:T(2,128)(2,1)S(1)}, u32[]{:S(2)}, u32[]{:S(2)}) %all-to-all-start.1) | async-done | bytes 262176 | tf_op jit(solution)/shard_map/all_to_all | solution.py:118
  69.1 0.3 reshape.88
  69.5 1.4 %copy.53.back_ref = bf16[32,64,64]{2,1,0:T(8,128)(2,1)} copy(bf16[32,64,64]{1,0,2:T(8,128)(2,1)S(1)} %bitcast.78) | data formatting | bytes 524288 | tf_op jit(solution)/shard_map/reshape;reshape | solution.py:125
  70.9 16.6 %shard_map.73 = bf16[32,64,1024]{2,1,0:T(8,128)(2,1)} custom-call(bf16[32,64,1024]{2,1,0:T(8,128)(2,1)} %bitcast.88, bf16[32,64,64]{2,1,0:T(8,128)(2,1)} %copy.53.back_ref, bf16[64,1024]{1,0:T(8,128)(2,1)} %multiply_convert_fusion.lon_ref, bf16[64,64]{1,0:T(8,128)(2,1)} %bitcast.86, f32[64,1]{1,0:T(8,128)} %copy.54.bias_ref, ...), custom_call_target="tpu_custom_call" | custom-call | flops 3758096384 | bytes 8650752 | tf_op jit(solution)/shard_map/pallas_call | solution.py:60
  (6 shorter events, 0.1 us)
Async XLA Ops:
  0.0 39.1 %copy-start.2 = (bf16[64,64]{1,0:T(8,128)(2,1)S(1)}, bf16[64,64]{1,0:T(8,128)(2,1)}, u32[]{:S(2)}) copy-start(bf16[64,64]{1,0:T(8,128)(2,1)} %param.9) | copy-start | bytes 24580
  0.0 39.8 %copy-start.3 = (f32[64]{0:T(128)S(1)}, f32[64]{0:T(128)}, u32[]{:S(2)}) copy-start(f32[64]{0:T(128)} %param.10) | copy-start | bytes 772
  0.0 40.5 %copy-start = (bf16[64,256]{1,0:T(8,128)(2,1)S(1)}, bf16[64,256]{1,0:T(8,128)(2,1)}, u32[]{:S(2)}) copy-start(bf16[64,256]{1,0:T(8,128)(2,1)} %param.11) | copy-start | bytes 98308
  0.0 40.6 %copy-start.1 = (bf16[64,256]{1,0:T(8,128)(2,1)S(1)}, bf16[64,256]{1,0:T(8,128)(2,1)}, u32[]{:S(2)}) copy-start(bf16[64,256]{1,0:T(8,128)(2,1)} %param.12) | copy-start | bytes 98308
  7.0 24.7 %all-to-all-start = ((bf16[32,2,2048]{2,1,0:T(2,128)(2,1)}), bf16[32,2,2048]{2,1,0:T(2,128)(2,1)S(1)}, u32[]{:S(2)}, u32[]{:S(2)}) async-start(bf16[32,2,2048]{2,1,0:T(2,128)(2,1)} %reshape.85), calls=%async_computation | async-start | bytes 524288 | tf_op jit(solution)/shard_map/all_to_all | solution.py:106
  33.8 6.9 %collective-permute-start.1 = (bf16[2,2,1,64,64]{4,3,1,0,2:T(8,128)(2,1)S(1)}, bf16[2,2,1,64,64]{4,3,1,0,2:T(8,128)(2,1)S(1)}, u32[]{:S(2)}, u32[]{:S(2)}) collective-permute-start(bf16[2,2,1,64,64]{4,3,1,0,2:T(8,128)(2,1)S(1)} %bitcast.81), channel_id=1, source_target_pairs={{1,0},{2,1},{3,2},{4,3},{5,4},{6,5},{7,6},{9,8},{10,9},{11,10},{12... | collective-permute-start | bytes 98312 | tf_op jit(solution)/shard_map/ppermute | solution.py:21
  36.2 5.9 %collective-permute-start = (bf16[2,2,1,64,64]{4,3,1,0,2:T(8,128)(2,1)S(1)}, bf16[2,2,1,64,64]{4,3,1,0,2:T(8,128)(2,1)S(1)}, u32[]{:S(2)}, u32[]{:S(2)}) collective-permute-start(bf16[2,2,1,64,64]{4,3,1,0,2:T(8,128)(2,1)S(1)} %bitcast.82), channel_id=1, source_target_pairs={{0,1},{1,2},{2,3},{3,4},{4,5},{5,6},{6,7},{8,9},{9,10},{10,11},{11... | collective-permute-start | bytes 98312 | tf_op jit(solution)/shard_map/ppermute | solution.py:19
  50.0 19.1 %all-to-all-start.1 = ((bf16[32,2,2048]{2,1,0:T(2,128)(2,1)}), bf16[32,2,2048]{2,1,0:T(2,128)(2,1)S(1)}, u32[]{:S(2)}, u32[]{:S(2)}) async-start(bf16[32,2,2048]{2,1,0:T(2,128)(2,1)} %reshape.87), calls=%async_computation.1 | async-start | bytes 524288 | tf_op jit(solution)/shard_map/all_to_all | solution.py:118

commit v14 on v12

--- a/solution.py
+++ b/solution.py
@@ -30,6 +30,34 @@
     turns = positions[:, None] * freq[None, :] % count
     angle = 2.0 * math.pi / count * turns.astype(jnp.float32)
     return (jnp.cos(angle) + jnp.sin(angle)) / math.sqrt(count)
+
+
+def along_kernel(lon_ref, field_ref, out_ref):
+    rows, chans, lon_cells = field_ref.shape
+    grid = field_ref[...].reshape(rows * chans, lon_cells)
+    out_ref[...] = lax.dot_general(
+        lon_ref[...], grid, (((1,), (1,)), ((), ())), preferred_element_type=jnp.float32
+    ).astype(out_ref.dtype)
+
+
+def along_modes(field, lon_table, block=8):
+    rows, chans, lon_cells = field.shape
+    modes = lon_table.shape[1]
+    return pl.pallas_call(
+        along_kernel,
+        out_shape=jax.ShapeDtypeStruct((modes, rows * chans), jnp.bfloat16),
+        grid=(rows // block,),
+        in_specs=[
+            pl.BlockSpec((modes, lon_cells), lambda i: (0, 0)),
+            pl.BlockSpec((block, chans, lon_cells), lambda i: (i, 0, 0)),
+        ],
+        out_specs=pl.BlockSpec((modes, block * chans), lambda i: (0, i)),
+        cost_estimate=pl.CostEstimate(
+            flops=2 * modes * rows * chans * lon_cells,
+            transcendentals=0,
+            bytes_accessed=2 * field.size + 2 * modes * rows * chans,
+        ),
+    )(lon_table.T, field)
 
 
 def finish_kernel(field_ref, back_ref, lon_ref, local_ref, bias_ref, gate_up_ref, down_ref, out_ref):
@@ -101,8 +129,8 @@
         ranks, lat_rows, lat_modes
     )
     per = lon_modes // ranks
-    along = jnp.einsum("xm,blncx->mblnc", lon_table, field, preferred_element_type=jnp.float32)
-    along = along.astype(jnp.bfloat16).reshape((ranks, per) + along.shape[1:])
+    along = along_modes(field.reshape(-1, chans, lon_cells), lon_table)
+    along = along.reshape((ranks, per, batch, levels, lat_rows, chans))
     along = lax.all_to_all(along, "rows", 0, 0, tiled=True).astype(jnp.float32)
     modes = jnp.einsum("sjblnc,snk->jblkc", along, lat_table, precision=high)
     modes = modes.astype(jnp.bfloat16)

time: 85.5 us -> 86.1 us (level)
  matrix products: 12.4 us -> 7.16 us
  Pallas kernels: 16.6 us -> 21.3 us
  waiting for transfers between devices: 14.5 us -> 16.3 us
  starting transfers between devices: 24.9 us -> 23.3 us
  local copies, waits for them, and re-layouts: 14.1 us -> 15 us
    dot_general x1 -> x0, matrix products: 5.24 us -> none  [body(): jnp.einsum('xm,blncx->mblnc', lon_table, field, preferred_element_type=jn...]
    pallas_call x0 -> x1, Pallas kernels: none -> 4.67 us  [along_modes(): pl.pallas_call(along_kernel, out_shape=jax.ShapeDtypeStruct((modes, rows...]
    all_to_all x1, starting transfers between devices: 7.89 us -> 6.24 us  [body(): lax.all_to_all(values.astype(jnp.bfloat16), 'rows', 0, 0, tiled=True)]
    all_to_all x1, waiting for transfers between devices: 3.93 us -> 5.58 us  [body(): along = lax.all_to_all(along, 'rows', 0, 0, tiled=True).astype(jnp.float32)]
    unnamed x17 -> x18, local copies, waits for them, and re-layouts: 3.85 us -> 3.89 us
  transfers between devices with their start and end apart: 4 -> 4, of which waited for: 3 -> 3; matrix products, arithmetic and copies ran while one was open for 17% -> 15% of each run, Pallas kernels for 0% -> 0%
where the time goes in v14:
time: 86.1 us; the launch traced here: 85.6 us
  starting transfers between devices  23.3 us (27%)
  Pallas kernels  21.3 us (25%)
  waiting for transfers between devices  16.3 us (19%)
  local copies, waits for them, and re-layouts  15 us (17%)
  matrix products  7.16 us (8%)
  other arithmetic  2.51 us (3%)
    pallas_call x1, Pallas kernels, finish(): pl.pallas_call(finish_kernel, out_shape=jax.ShapeDtypeStruct(field.shape,...  16.6 us
    all_to_all x1, starting transfers between devices, body(): along = lax.all_to_all(along, 'rows', 0, 0, tiled=True).astype(jnp.float32)  11.8 us
    all_to_all x1, waiting for transfers between devices, body(): lax.all_to_all(values.astype(jnp.bfloat16), 'rows', 0, 0, tiled=True)  10.6 us
    slice x1, local copies, waits for them, and re-layouts, body(): spectral_weight[0]  7.34 us
    all_to_all x1, starting transfers between devices, body(): lax.all_to_all(values.astype(jnp.bfloat16), 'rows', 0, 0, tiled=True)  6.24 us
    all_to_all x1, waiting for transfers between devices, body(): along = lax.all_to_all(along, 'rows', 0, 0, tiled=True).astype(jnp.float32)  5.58 us
    pallas_call x1, Pallas kernels, along_modes(): pl.pallas_call(along_kernel, out_shape=jax.ShapeDtypeStruct((modes, rows...  4.67 us
    unnamed x18, local copies, waits for them, and re-layouts  3.89 us
  transfers between devices with their start and end apart: 4, of which 3 were waited for; matrix products, arithmetic and copies ran while one was open for 15% of the time, Pallas kernels for 0%

profile of v14, /device:TPU:25, one launch (start us, length us, event | category | flops | bytes accessed | tf_op | source)
XLA Modules:
  0.0 85.6 jit_solution(12544952208724601200)
XLA Ops:
  0.0 1.8 %multiply_convert_fusion.lon_ref = bf16[64,1024]{1,0:T(8,128)(2,1)} fusion(s32[64]{0:T(128)S(1)} %iota_add_fusion), kind=kLoop, calls=%fused_computation.32 | loop fusion | flops 1114112 | bytes 131328 | tf_op jit(solution)/shard_map/convert_element_type | solution.py:125
  1.8 4.7 %shard_map.73 = bf16[64,2048]{1,0:T(8,128)(2,1)} custom-call(bf16[64,1024]{1,0:T(8,128)(2,1)} %multiply_convert_fusion.lon_ref, bf16[32,64,1024]{2,1,0:T(8,128)(2,1)} %bitcast.74), custom_call_target="tpu_custom_call" | custom-call | flops 268435456 | bytes 4456448 | tf_op jit(solution)/shard_map/pallas_call | solution.py:46
  6.5 1.5 %reshape.78 = bf16[32,2,2,1,16,64]{5,4,2,1,0,3:T(8,128)(2,1)S(1)} reshape(bf16[64,2048]{1,0:T(8,128)(2,1)} %shard_map.73) | data formatting | bytes 524288 | tf_op jit(solution)/shard_map/reshape | solution.py:133
  8.0 1.1 %reshape.89 = bf16[32,2,2048]{2,1,0:T(2,128)(2,1)} reshape(bf16[32,1,2,2,16,64]{5,4,3,2,1,0:T(8,128)(2,1)S(1)} %bitcast_bitcast_fusion) | data formatting | bytes 524288
  9.1 11.8 %all-to-all-start = ((bf16[32,2,2048]{2,1,0:T(2,128)(2,1)}), bf16[32,2,2048]{2,1,0:T(2,128)(2,1)S(1)}, u32[]{:S(2)}, u32[]{:S(2)}) async-start(bf16[32,2,2048]{2,1,0:T(2,128)(2,1)} %reshape.89), calls=%async_computation | async-start | bytes 524288 | tf_op jit(solution)/shard_map/all_to_all | solution.py:134
  20.9 7.3 %fusion.36 = (bf16[1,64,2,64,64]{4,3,2,1,0:T(8,128)(2,1)S(1)}, bf16[1,64,2,64,64]{4,3,2,1,0:T(8,128)(2,1)}, bf16[1,64,2,64,64]{4,3,2,1,0:T(8,128)(2,1)}) fusion(bf16[3,64,2,64,64]{4,3,2,1,0:T(8,128)(2,1)} %param.8), kind=kLoop, calls=%fused_computation.55 | loop fusion | bytes 6291456 | tf_op jit(solution)/shard_map/slice | solution.py:140
  28.2 5.6 %all-to-all-done = bf16[32,2,2048]{2,1,0:T(2,128)(2,1)S(1)} async-done(((bf16[32,2,2048]{2,1,0:T(2,128)(2,1)}), bf16[32,2,2048]{2,1,0:T(2,128)(2,1)S(1)}, u32[]{:S(2)}, u32[]{:S(2)}) %all-to-all-start) | async-done | bytes 262176 | tf_op jit(solution)/shard_map/all_to_all | solution.py:134
  33.8 0.4 reshape.90
  34.2 1.7 %fusion.7 = bf16[64,2,2,64]{3,0,2,1:T(8,128)(2,1)S(1)} fusion(bf16[32,2,2,1,16,64]{5,4,2,1,3,0:T(8,128)(2,1)S(1)} %bitcast.78, s32[64]{0:T(128)S(1)} %iota_add_fusion, s32[32,16]{0,1:T(8,128)S(1)} %multiply_add_fusion), kind=kOutput, calls=%fused_computation.12 | convolution fusion | flops 101203968 | bytes 297216 | tf_op jit(solution)/shard_map/sjblnc,snk->jblkc/dot_general | solution.py:135
  35.9 2.4 %collective-permute-start.1 = (bf16[2,2,1,64,64]{4,3,1,0,2:T(8,128)(2,1)S(1)}, bf16[2,2,1,64,64]{4,3,1,0,2:T(8,128)(2,1)S(1)}, u32[]{:S(2)}, u32[]{:S(2)}) collective-permute-start(bf16[2,2,1,64,64]{4,3,1,0,2:T(8,128)(2,1)S(1)} %bitcast.81), channel_id=1, source_target_pairs={{1,0},{2,1},{3,2},{4,3},{5,4},{6,5},{7,6},{9,8},{10,9},{11,10},{12... | collective-permute-start | bytes 98312 | tf_op jit(solution)/shard_map/ppermute | solution.py:21
  38.3 2.9 %collective-permute-start = (bf16[2,2,1,64,64]{4,3,1,0,2:T(8,128)(2,1)S(1)}, bf16[2,2,1,64,64]{4,3,1,0,2:T(8,128)(2,1)S(1)}, u32[]{:S(2)}, u32[]{:S(2)}) collective-permute-start(bf16[2,2,1,64,64]{4,3,1,0,2:T(8,128)(2,1)S(1)} %bitcast.82), channel_id=1, source_target_pairs={{0,1},{1,2},{2,3},{3,4},{4,5},{5,6},{6,7},{8,9},{9,10},{10,11},{11... | collective-permute-start | bytes 98312 | tf_op jit(solution)/shard_map/ppermute | solution.py:19
  41.2 2.2 %fusion.1 = f32[2,64,2,64]{3,2,1,0:T(2,128)S(1)} fusion(bf16[1,64,2,64,64]{4,3,2,1,0:T(8,128)(2,1)} %get-tuple-element.6, bf16[2,2,64,64]{3,2,1,0:T(8,128)(2,1)S(1)} %bitcast.83), kind=kOutput, calls=%fused_computation.3 | convolution fusion | flops 2097152 | bytes 1146880 | tf_op jit(solution)/shard_map/kjco,jblkc->jblko/dot_general | solution.py:144
  43.4 0.7 fusion
  44.1 0.1 collective-permute-done
  44.2 0.7 fusion.8
  44.9 0.0 copy-start.1
  44.9 0.0 copy-start.2
  44.9 0.0 copy-start.4
  44.9 0.0 copy-start.3
  44.9 1.9 %fusion.3 = bf16[32,2,2,1,16,64]{5,0,4,2,1,3:T(8,128)(2,1)S(1)} fusion(s32[64]{0:T(128)S(1)} %iota_add_fusion, s32[32,16]{0,1:T(8,128)S(1)} %multiply_add_fusion, bf16[2,2,64,64,1]{3,1,2,0,4:T(2,128)(2,1)S(1)} %fusion.8), kind=kOutput, calls=%fused_computation.7 | convolution fusion | flops 101318656 | bytes 297216 | tf_op jit(solution)/shard_map/rnk,jblko->rjblno/dot_general | solution.py:157
  46.8 0.2 copy.107
  47.0 1.1 %reshape.91 = bf16[32,2,2048]{2,1,0:T(2,128)(2,1)} reshape(bf16[32,1,2,2,16,64]{5,4,3,2,1,0:T(8,128)(2,1)S(1)} %bitcast.76) | data formatting | bytes 524288
  48.1 6.2 %all-to-all-start.1 = ((bf16[32,2,2048]{2,1,0:T(2,128)(2,1)}), bf16[32,2,2048]{2,1,0:T(2,128)(2,1)S(1)}, u32[]{:S(2)}, u32[]{:S(2)}) async-start(bf16[32,2,2048]{2,1,0:T(2,128)(2,1)} %reshape.91), calls=%async_computation.1 | async-start | bytes 524288 | tf_op jit(solution)/shard_map/all_to_all | solution.py:160
  54.4 0.1 copy.66
  54.5 0.1 copy.68
  54.6 0.7 copy.70.bias_ref
  55.3 0.7 copy.65
  56.0 0.7 maximum_bitcast_fusion.gate_up_ref
  56.7 10.6 %all-to-all-done.1 = bf16[32,2,2048]{2,1,0:T(2,128)(2,1)S(1)} async-done(((bf16[32,2,2048]{2,1,0:T(2,128)(2,1)}), bf16[32,2,2048]{2,1,0:T(2,128)(2,1)S(1)}, u32[]{:S(2)}, u32[]{:S(2)}) %all-to-all-start.1) | async-done | bytes 262176 | tf_op jit(solution)/shard_map/all_to_all | solution.py:160
  67.3 0.4 reshape.92
  67.7 1.4 %copy.69.back_ref = bf16[32,64,64]{2,1,0:T(8,128)(2,1)} copy(bf16[32,64,64]{1,0,2:T(8,128)(2,1)S(1)} %bitcast.77) | data formatting | bytes 524288 | tf_op jit(solution)/shard_map/reshape;reshape | solution.py:167
  69.0 16.6 %shard_map.74 = bf16[32,64,1024]{2,1,0:T(8,128)(2,1)} custom-call(bf16[32,64,1024]{2,1,0:T(8,128)(2,1)} %bitcast.75, bf16[32,64,64]{2,1,0:T(8,128)(2,1)} %copy.69.back_ref, bf16[64,1024]{1,0:T(8,128)(2,1)} %multiply_convert_fusion.lon_ref, bf16[64,64]{1,0:T(8,128)(2,1)} %bitcast.79, f32[64,1]{1,0:T(8,128)} %copy.70.bias_ref, ...), custom_call_target="tpu_custom_call" | custom-call | flops 3758096384 | bytes 8650752 | tf_op jit(solution)/shard_map/pallas_call | solution.py:88
  (11 shorter events, 0.1 us)
Async XLA Ops:
  9.1 24.7 %all-to-all-start = ((bf16[32,2,2048]{2,1,0:T(2,128)(2,1)}), bf16[32,2,2048]{2,1,0:T(2,128)(2,1)S(1)}, u32[]{:S(2)}, u32[]{:S(2)}) async-start(bf16[32,2,2048]{2,1,0:T(2,128)(2,1)} %reshape.89), calls=%async_computation | async-start | bytes 524288 | tf_op jit(solution)/shard_map/all_to_all | solution.py:134
  34.2 9.3 %copy-start = (bf16[1,64,2,64,64]{4,3,2,1,0:T(8,128)(2,1)S(1)}, bf16[1,64,2,64,64]{4,3,2,1,0:T(8,128)(2,1)}, u32[]{:S(2)}) copy-start(bf16[1,64,2,64,64]{4,3,2,1,0:T(8,128)(2,1)} %get-tuple-element.7) | copy-start | bytes 3145732
  35.9 7.5 %collective-permute-start.1 = (bf16[2,2,1,64,64]{4,3,1,0,2:T(8,128)(2,1)S(1)}, bf16[2,2,1,64,64]{4,3,1,0,2:T(8,128)(2,1)S(1)}, u32[]{:S(2)}, u32[]{:S(2)}) collective-permute-start(bf16[2,2,1,64,64]{4,3,1,0,2:T(8,128)(2,1)S(1)} %bitcast.81), channel_id=1, source_target_pairs={{1,0},{2,1},{3,2},{4,3},{5,4},{6,5},{7,6},{9,8},{10,9},{11,10},{12... | collective-permute-start | bytes 98312 | tf_op jit(solution)/shard_map/ppermute | solution.py:21
  38.3 5.9 %collective-permute-start = (bf16[2,2,1,64,64]{4,3,1,0,2:T(8,128)(2,1)S(1)}, bf16[2,2,1,64,64]{4,3,1,0,2:T(8,128)(2,1)S(1)}, u32[]{:S(2)}, u32[]{:S(2)}) collective-permute-start(bf16[2,2,1,64,64]{4,3,1,0,2:T(8,128)(2,1)S(1)} %bitcast.82), channel_id=1, source_target_pairs={{0,1},{1,2},{2,3},{3,4},{4,5},{5,6},{6,7},{8,9},{9,10},{10,11},{11... | collective-permute-start | bytes 98312 | tf_op jit(solution)/shard_map/ppermute | solution.py:19
  44.9 9.5 %copy-start.1 = (bf16[64,256]{1,0:T(8,128)(2,1)S(1)}, bf16[64,256]{1,0:T(8,128)(2,1)}, u32[]{:S(2)}) copy-start(bf16[64,256]{1,0:T(8,128)(2,1)} %param.11) | copy-start | bytes 98308
  44.9 9.6 %copy-start.2 = (bf16[64,256]{1,0:T(8,128)(2,1)S(1)}, bf16[64,256]{1,0:T(8,128)(2,1)}, u32[]{:S(2)}) copy-start(bf16[64,256]{1,0:T(8,128)(2,1)} %param.12) | copy-start | bytes 98308
  44.9 9.7 %copy-start.4 = (f32[64]{0:T(128)S(1)}, f32[64]{0:T(128)}, u32[]{:S(2)}) copy-start(f32[64]{0:T(128)} %param.10) | copy-start | bytes 772
  44.9 10.4 %copy-start.3 = (bf16[64,64]{1,0:T(8,128)(2,1)S(1)}, bf16[64,64]{1,0:T(8,128)(2,1)}, u32[]{:S(2)}) copy-start(bf16[64,64]{1,0:T(8,128)(2,1)} %param.9) | copy-start | bytes 24580
  48.1 19.2 %all-to-all-start.1 = ((bf16[32,2,2048]{2,1,0:T(2,128)(2,1)}), bf16[32,2,2048]{2,1,0:T(2,128)(2,1)S(1)}, u32[]{:S(2)}, u32[]{:S(2)}) async-start(bf16[32,2,2048]{2,1,0:T(2,128)(2,1)} %reshape.91), calls=%async_computation.1 | async-start | bytes 524288 | tf_op jit(solution)/shard_map/all_to_all | solution.py:160

commit v15 on v12

--- a/solution.py
+++ b/solution.py
@@ -37,9 +37,11 @@
     rows, _, lon_cells = field_ref.shape
     acts = []
     for r in range(rows):
-        lhs = jnp.concatenate([back_ref[r], local_ref[...]], axis=1)
+        lhs = jnp.concatenate([back_ref[:, r, :], local_ref[...].T], axis=0)
         rhs = jnp.concatenate([lon_ref[...], field_ref[r]], axis=0)
-        value = jnp.dot(lhs, rhs, preferred_element_type=jnp.float32) + bias_ref[...]
+        value = lax.dot_general(
+            lhs, rhs, (((0,), (0,)), ((), ())), preferred_element_type=jnp.float32
+        ) + bias_ref[...]
         acts.append((0.5 * value * (1.0 + lax.erf(value * sqrt_half))).astype(jnp.bfloat16))
     act = jnp.concatenate(acts, axis=1)
     both = jnp.dot(gate_up_ref[...], act, preferred_element_type=jnp.float32)
@@ -54,7 +56,7 @@
 
 def finish(field, back, lon_table, local_weight, local_bias, gate_weight, up_weight, down_weight, block=8):
     rows, chans, lon_cells = field.shape
-    modes = back.shape[2]
+    modes = back.shape[0]
     hid = gate_weight.shape[1]
     whole = lambda i: (0, 0)
     return pl.pallas_call(
@@ -63,7 +65,7 @@
         grid=(rows // block,),
         in_specs=[
             pl.BlockSpec((block, chans, lon_cells), lambda i: (i, 0, 0)),
-            pl.BlockSpec((block, chans, modes), lambda i: (i, 0, 0)),
+            pl.BlockSpec((modes, block, chans), lambda i: (0, i, 0)),
             pl.BlockSpec((modes, lon_cells), whole),
             pl.BlockSpec((chans, chans), whole),
             pl.BlockSpec((chans, 1), whole),
@@ -130,13 +132,11 @@
         "rnk,jblko->rjblno", lat_table, mixed_b.astype(jnp.float32), precision=high
     )
     values = lax.all_to_all(values.astype(jnp.bfloat16), "rows", 0, 0, tiled=True)
-    back_b = jnp.transpose(values, (2, 3, 4, 5, 0, 1)).reshape(
-        batch, levels, lat_rows, chans, lon_modes
-    )
+    back_b = values.reshape(lon_modes, batch * levels * lat_rows, chans)
 
     result = finish(
         field.reshape(batch * levels * lat_rows, chans, lon_cells),
-        back_b.reshape(batch * levels * lat_rows, chans, lon_modes),
+        back_b,
         lon_table,
         local_weight,
         local_bias,

time: 85.5 us -> 85.5 us (level)
    another operation x1 -> x0, local copies, waits for them, and re-layouts: 1.38 us -> none  [body(): back_b.reshape(batch * levels * lat_rows, chans, lon_modes)]
where the time goes in v15:
time: 85.5 us; the launch traced here: 85.1 us
  starting transfers between devices  24.9 us (29%)
  Pallas kernels  17.2 us (20%)
  waiting for transfers between devices  14.5 us (17%)
  local copies, waits for them, and re-layouts  13.5 us (16%)
  matrix products  12.4 us (15%)
  other arithmetic  2.52 us (3%)
    pallas_call x1, Pallas kernels, finish(): pl.pallas_call(finish_kernel, out_shape=jax.ShapeDtypeStruct(field.shape,...  17.2 us
    all_to_all x1, starting transfers between devices, body(): along = lax.all_to_all(along, 'rows', 0, 0, tiled=True).astype(jnp.float32)  11.8 us
    all_to_all x1, waiting for transfers between devices, body(): lax.all_to_all(values.astype(jnp.bfloat16), 'rows', 0, 0, tiled=True)  10.4 us
    all_to_all x1, starting transfers between devices, body(): lax.all_to_all(values.astype(jnp.bfloat16), 'rows', 0, 0, tiled=True)  7.89 us
    slice x1, local copies, waits for them, and re-layouts, body(): spectral_weight[0]  7.34 us
    dot_general x1, matrix products, body(): jnp.einsum('xm,blncx->mblnc', lon_table, field, preferred_element_type=jn...  5.24 us
    unnamed x17, local copies, waits for them, and re-layouts  4.67 us
    all_to_all x1, waiting for transfers between devices, body(): along = lax.all_to_all(along, 'rows', 0, 0, tiled=True).astype(jnp.float32)  3.93 us
  transfers between devices with their start and end apart: 4, of which 3 were waited for; matrix products, arithmetic and copies ran while one was open for 17% of the time, Pallas kernels for 0%

profile of v15, /device:TPU:25, one launch (start us, length us, event | category | flops | bytes accessed | tf_op | source)
XLA Modules:
  0.0 85.1 jit_solution(13498268506202484009)
XLA Ops:
  0.0 5.2 %fusion.5 = bf16[64,2,16,64]{3,0,2,1:T(8,128)(2,1)S(1)} fusion(bf16[2,1,16,64,1024]{4,3,2,1,0:T(8,128)(2,1)} %param.7, s32[64]{0:T(128)S(1)} %iota_add_fusion), kind=kOutput, calls=%fused_computation.8 | convolution fusion | flops 269680640 | bytes 4456704 | tf_op jit(solution)/shard_map/xm,blncx->mblnc/dot_general | solution.py:106
  5.2 0.0 copy-start.2
  5.3 0.0 copy-start.4
  5.3 0.0 copy-start.3
  5.3 0.6 copy.91
  5.9 1.1 %reshape.100 = bf16[32,2,2048]{2,1,0:T(2,128)(2,1)} reshape(bf16[32,1,2,2,16,64]{5,4,3,2,1,0:T(8,128)(2,1)S(1)} %bitcast.80) | data formatting | bytes 524288
  7.0 11.8 %all-to-all-start = ((bf16[32,2,2048]{2,1,0:T(2,128)(2,1)}), bf16[32,2,2048]{2,1,0:T(2,128)(2,1)S(1)}, u32[]{:S(2)}, u32[]{:S(2)}) async-start(bf16[32,2,2048]{2,1,0:T(2,128)(2,1)} %reshape.100), calls=%async_computation | async-start | bytes 524288 | tf_op jit(solution)/shard_map/all_to_all | solution.py:108
  18.8 0.1 copy.48
  18.9 0.1 copy.50
  19.0 0.0 copy-done.4
  19.0 0.7 copy.51.bias_ref
  19.7 0.7 copy.47
  20.4 7.3 %fusion.60 = (bf16[1,64,2,64,64]{4,3,2,1,0:T(8,128)(2,1)S(1)}, bf16[1,64,2,64,64]{4,3,2,1,0:T(8,128)(2,1)}, bf16[1,64,2,64,64]{4,3,2,1,0:T(8,128)(2,1)}) fusion(bf16[3,64,2,64,64]{4,3,2,1,0:T(8,128)(2,1)} %param.8), kind=kLoop, calls=%fused_computation.80 | loop fusion | bytes 6291456 | tf_op jit(solution)/shard_map/slice | solution.py:114
  27.8 3.9 %all-to-all-done = bf16[32,2,2048]{2,1,0:T(2,128)(2,1)S(1)} async-done(((bf16[32,2,2048]{2,1,0:T(2,128)(2,1)}), bf16[32,2,2048]{2,1,0:T(2,128)(2,1)S(1)}, u32[]{:S(2)}, u32[]{:S(2)}) %all-to-all-start) | async-done | bytes 262176 | tf_op jit(solution)/shard_map/all_to_all | solution.py:108
  31.7 0.4 reshape.101
  32.1 1.7 %fusion.12 = bf16[64,2,2,64]{3,0,2,1:T(8,128)(2,1)S(1)} fusion(bf16[32,2,2,1,16,64]{5,4,2,1,3,0:T(8,128)(2,1)S(1)} %bitcast.83, s32[64]{0:T(128)S(1)} %iota_add_fusion, s32[32,16]{0,1:T(8,128)S(1)} %multiply_add_fusion), kind=kOutput, calls=%fused_computation.15 | convolution fusion | flops 101203968 | bytes 297216 | tf_op jit(solution)/shard_map/sjblnc,snk->jblkc/dot_general | solution.py:109
  33.8 2.4 %collective-permute-start.1 = (bf16[2,2,1,64,64]{4,3,1,0,2:T(8,128)(2,1)S(1)}, bf16[2,2,1,64,64]{4,3,1,0,2:T(8,128)(2,1)S(1)}, u32[]{:S(2)}, u32[]{:S(2)}) collective-permute-start(bf16[2,2,1,64,64]{4,3,1,0,2:T(8,128)(2,1)S(1)} %bitcast.88), channel_id=1, source_target_pairs={{1,0},{2,1},{3,2},{4,3},{5,4},{6,5},{7,6},{9,8},{10,9},{11,10},{12... | collective-permute-start | bytes 98312 | tf_op jit(solution)/shard_map/ppermute | solution.py:21
  36.2 2.9 %collective-permute-start = (bf16[2,2,1,64,64]{4,3,1,0,2:T(8,128)(2,1)S(1)}, bf16[2,2,1,64,64]{4,3,1,0,2:T(8,128)(2,1)S(1)}, u32[]{:S(2)}, u32[]{:S(2)}) collective-permute-start(bf16[2,2,1,64,64]{4,3,1,0,2:T(8,128)(2,1)S(1)} %bitcast.89), channel_id=1, source_target_pairs={{0,1},{1,2},{2,3},{3,4},{4,5},{5,6},{6,7},{8,9},{9,10},{10,11},{11... | collective-permute-start | bytes 98312 | tf_op jit(solution)/shard_map/ppermute | solution.py:19
  39.1 2.2 %fusion.3 = f32[2,64,2,64]{3,2,1,0:T(2,128)S(1)} fusion(bf16[1,64,2,64,64]{4,3,2,1,0:T(8,128)(2,1)} %get-tuple-element.6, bf16[2,2,64,64]{3,2,1,0:T(8,128)(2,1)S(1)} %bitcast.90), kind=kOutput, calls=%fused_computation.5 | convolution fusion | flops 2097152 | bytes 1146880 | tf_op jit(solution)/shard_map/kjco,jblkc->jblko/dot_general | solution.py:118
  41.3 0.0 collective-permute-done.1
  41.3 0.7 fusion.2
  42.0 0.1 collective-permute-done
  42.1 0.7 fusion.13
  42.8 1.9 %fusion.8 = bf16[32,2,2,1,16,64]{5,0,4,2,1,3:T(8,128)(2,1)S(1)} fusion(s32[64]{0:T(128)S(1)} %iota_add_fusion, s32[32,16]{0,1:T(8,128)S(1)} %multiply_add_fusion, bf16[2,2,64,64,1]{3,1,2,0,4:T(2,128)(2,1)S(1)} %fusion.13), kind=kOutput, calls=%fused_computation.10 | convolution fusion | flops 101318656 | bytes 297216 | tf_op jit(solution)/shard_map/rnk,jblko->rjblno/dot_general | solution.py:131
  44.6 0.2 copy.90
  44.9 1.1 %reshape.102 = bf16[32,2,2048]{2,1,0:T(2,128)(2,1)} reshape(bf16[32,1,2,2,16,64]{5,4,3,2,1,0:T(8,128)(2,1)S(1)} %bitcast.81) | data formatting | bytes 524288
  46.0 7.9 %all-to-all-start.1 = ((bf16[32,2,2048]{2,1,0:T(2,128)(2,1)}), bf16[32,2,2048]{2,1,0:T(2,128)(2,1)S(1)}, u32[]{:S(2)}, u32[]{:S(2)}) async-start(bf16[32,2,2048]{2,1,0:T(2,128)(2,1)} %reshape.102), calls=%async_computation.1 | async-start | bytes 524288 | tf_op jit(solution)/shard_map/all_to_all | solution.py:134
  53.9 0.7 maximum_bitcast_fusion.gate_up_ref
  54.6 1.8 %multiply_convert_fusion.lon_ref = bf16[64,1024]{1,0:T(8,128)(2,1)} fusion(s32[64]{0:T(128)S(1)} %iota_add_fusion), kind=kLoop, calls=%fused_computation.41 | loop fusion | flops 1114112 | bytes 131328 | tf_op jit(solution)/shard_map/convert_element_type | solution.py:99
  56.4 10.4 %all-to-all-done.1 = bf16[32,2,2048]{2,1,0:T(2,128)(2,1)S(1)} async-done(((bf16[32,2,2048]{2,1,0:T(2,128)(2,1)}), bf16[32,2,2048]{2,1,0:T(2,128)(2,1)S(1)}, u32[]{:S(2)}, u32[]{:S(2)}) %all-to-all-start.1) | async-done | bytes 262176 | tf_op jit(solution)/shard_map/all_to_all | solution.py:134
  66.8 1.2 %reshape.103 = bf16[32,1,2,2,16,64]{5,4,3,2,1,0:T(8,128)(2,1)} reshape(bf16[32,2,2048]{2,1,0:T(2,128)(2,1)S(1)} %all-to-all-done.1) | data formatting | bytes 524288
  68.0 17.2 %shard_map.73 = bf16[32,64,1024]{2,1,0:T(8,128)(2,1)} custom-call(bf16[32,64,1024]{2,1,0:T(8,128)(2,1)} %bitcast.87, bf16[64,32,64]{2,1,0:T(8,128)(2,1)} %bitcast.82, bf16[64,1024]{1,0:T(8,128)(2,1)} %multiply_convert_fusion.lon_ref, bf16[64,64]{1,0:T(8,128)(2,1)} %bitcast.85, f32[64,1]{1,0:T(8,128)} %copy.51.bias_ref, ...), custom_call_target="tpu_custom_call" | custom-call | flops 3758096384 | bytes 8650752 | tf_op jit(solution)/shard_map/pallas_call | solution.py:62
  (9 shorter events, 0.0 us)
Async XLA Ops:
  5.2 13.5 %copy-start.1 = (bf16[64,256]{1,0:T(8,128)(2,1)S(1)}, bf16[64,256]{1,0:T(8,128)(2,1)}, u32[]{:S(2)}) copy-start(bf16[64,256]{1,0:T(8,128)(2,1)} %param.11) | copy-start | bytes 98308
  5.2 13.6 %copy-start.2 = (bf16[64,256]{1,0:T(8,128)(2,1)S(1)}, bf16[64,256]{1,0:T(8,128)(2,1)}, u32[]{:S(2)}) copy-start(bf16[64,256]{1,0:T(8,128)(2,1)} %param.12) | copy-start | bytes 98308
  5.3 13.8 %copy-start.4 = (f32[64]{0:T(128)S(1)}, f32[64]{0:T(128)}, u32[]{:S(2)}) copy-start(f32[64]{0:T(128)} %param.10) | copy-start | bytes 772
  5.3 14.5 %copy-start.3 = (bf16[64,64]{1,0:T(8,128)(2,1)S(1)}, bf16[64,64]{1,0:T(8,128)(2,1)}, u32[]{:S(2)}) copy-start(bf16[64,64]{1,0:T(8,128)(2,1)} %param.9) | copy-start | bytes 24580
  7.0 24.7 %all-to-all-start = ((bf16[32,2,2048]{2,1,0:T(2,128)(2,1)}), bf16[32,2,2048]{2,1,0:T(2,128)(2,1)S(1)}, u32[]{:S(2)}, u32[]{:S(2)}) async-start(bf16[32,2,2048]{2,1,0:T(2,128)(2,1)} %reshape.100), calls=%async_computation | async-start | bytes 524288 | tf_op jit(solution)/shard_map/all_to_all | solution.py:108
  32.1 9.3 %copy-start = (bf16[1,64,2,64,64]{4,3,2,1,0:T(8,128)(2,1)S(1)}, bf16[1,64,2,64,64]{4,3,2,1,0:T(8,128)(2,1)}, u32[]{:S(2)}) copy-start(bf16[1,64,2,64,64]{4,3,2,1,0:T(8,128)(2,1)} %get-tuple-element.7) | copy-start | bytes 3145732
  33.8 7.5 %collective-permute-start.1 = (bf16[2,2,1,64,64]{4,3,1,0,2:T(8,128)(2,1)S(1)}, bf16[2,2,1,64,64]{4,3,1,0,2:T(8,128)(2,1)S(1)}, u32[]{:S(2)}, u32[]{:S(2)}) collective-permute-start(bf16[2,2,1,64,64]{4,3,1,0,2:T(8,128)(2,1)S(1)} %bitcast.88), channel_id=1, source_target_pairs={{1,0},{2,1},{3,2},{4,3},{5,4},{6,5},{7,6},{9,8},{10,9},{11,10},{12... | collective-permute-start | bytes 98312 | tf_op jit(solution)/shard_map/ppermute | solution.py:21
  36.2 5.9 %collective-permute-start = (bf16[2,2,1,64,64]{4,3,1,0,2:T(8,128)(2,1)S(1)}, bf16[2,2,1,64,64]{4,3,1,0,2:T(8,128)(2,1)S(1)}, u32[]{:S(2)}, u32[]{:S(2)}) collective-permute-start(bf16[2,2,1,64,64]{4,3,1,0,2:T(8,128)(2,1)S(1)} %bitcast.89), channel_id=1, source_target_pairs={{0,1},{1,2},{2,3},{3,4},{4,5},{5,6},{6,7},{8,9},{9,10},{10,11},{11... | collective-permute-start | bytes 98312 | tf_op jit(solution)/shard_map/ppermute | solution.py:19
  46.0 20.8 %all-to-all-start.1 = ((bf16[32,2,2048]{2,1,0:T(2,128)(2,1)}), bf16[32,2,2048]{2,1,0:T(2,128)(2,1)S(1)}, u32[]{:S(2)}, u32[]{:S(2)}) async-start(bf16[32,2,2048]{2,1,0:T(2,128)(2,1)} %reshape.102), calls=%async_computation.1 | async-start | bytes 524288 | tf_op jit(solution)/shard_map/all_to_all | solution.py:134

commit v16 on v12

--- a/solution.py
+++ b/solution.py
@@ -88,7 +88,6 @@
 
 
 def body(field, spectral_weight, local_weight, local_bias, gate_weight, up_weight, down_weight):
-    high = lax.Precision.HIGHEST
     batch, levels, lat_rows, chans, lon_cells = field.shape
     ranks = lax.axis_size("rows")
     lat_total = lat_rows * ranks
@@ -103,8 +102,9 @@
     per = lon_modes // ranks
     along = jnp.einsum("xm,blncx->mblnc", lon_table, field, preferred_element_type=jnp.float32)
     along = along.astype(jnp.bfloat16).reshape((ranks, per) + along.shape[1:])
-    along = lax.all_to_all(along, "rows", 0, 0, tiled=True).astype(jnp.float32)
-    modes = jnp.einsum("sjblnc,snk->jblkc", along, lat_table, precision=high)
+    along = lax.all_to_all(along, "rows", 0, 0, tiled=True)
+    lat_b = lat_table.astype(jnp.bfloat16)
+    modes = jnp.einsum("sjblnc,snk->jblkc", along, lat_b, preferred_element_type=jnp.float32)
     modes = modes.astype(jnp.bfloat16)
     padded = extended(modes, (("lev", 2),), 1)
     mixed = jnp.einsum(
@@ -126,9 +126,7 @@
         preferred_element_type=jnp.float32,
     )
     mixed_b = mixed.astype(jnp.bfloat16)
-    values = jnp.einsum(
-        "rnk,jblko->rjblno", lat_table, mixed_b.astype(jnp.float32), precision=high
-    )
+    values = jnp.einsum("rnk,jblko->rjblno", lat_b, mixed_b, preferred_element_type=jnp.float32)
     values = lax.all_to_all(values.astype(jnp.bfloat16), "rows", 0, 0, tiled=True)
     back_b = jnp.transpose(values, (2, 3, 4, 5, 0, 1)).reshape(
         batch, levels, lat_rows, chans, lon_modes

time: 85.5 us -> 84.9 us (level)
  no operation moved by 1% of the time
where the time goes in v16:
time: 84.9 us; the launch traced here: 84.6 us
  starting transfers between devices  24.9 us (29%)
  Pallas kernels  16.6 us (20%)
  waiting for transfers between devices  14.5 us (17%)
  local copies, waits for them, and re-layouts  14.1 us (17%)
  matrix products  11.8 us (14%)
  other arithmetic  2.52 us (3%)
    pallas_call x1, Pallas kernels, finish(): pl.pallas_call(finish_kernel, out_shape=jax.ShapeDtypeStruct(field.shape,...  16.6 us
    all_to_all x1, starting transfers between devices, body(): along = lax.all_to_all(along, 'rows', 0, 0, tiled=True)  11.8 us
    all_to_all x1, waiting for transfers between devices, body(): lax.all_to_all(values.astype(jnp.bfloat16), 'rows', 0, 0, tiled=True)  10.4 us
    all_to_all x1, starting transfers between devices, body(): lax.all_to_all(values.astype(jnp.bfloat16), 'rows', 0, 0, tiled=True)  7.89 us
    slice x1, local copies, waits for them, and re-layouts, body(): spectral_weight[0]  7.34 us
    dot_general x1, matrix products, body(): jnp.einsum('xm,blncx->mblnc', lon_table, field, preferred_element_type=jn...  5.24 us
    all_to_all x1, waiting for transfers between devices, body(): along = lax.all_to_all(along, 'rows', 0, 0, tiled=True)  3.93 us
    unnamed x17, local copies, waits for them, and re-layouts  3.85 us
  transfers between devices with their start and end apart: 4, of which 3 were waited for; matrix products, arithmetic and copies ran while one was open for 17% of the time, Pallas kernels for 0%

profile of v16, /device:TPU:25, one launch (start us, length us, event | category | flops | bytes accessed | tf_op | source)
XLA Modules:
  0.0 84.6 jit_solution(219876406173336974)
XLA Ops:
  0.0 5.2 %fusion.5 = bf16[64,2,16,64]{3,0,2,1:T(8,128)(2,1)S(1)} fusion(bf16[2,1,16,64,1024]{4,3,2,1,0:T(8,128)(2,1)} %param.7, s32[64]{0:T(128)S(1)} %iota_add_fusion), kind=kOutput, calls=%fused_computation.8 | convolution fusion | flops 269680640 | bytes 4456704 | tf_op jit(solution)/shard_map/xm,blncx->mblnc/dot_general | solution.py:103
  5.2 0.0 copy-start.2
  5.3 0.0 copy-start.4
  5.3 0.0 copy-start.3
  5.3 0.6 copy.110
  5.9 1.1 %reshape.97 = bf16[32,2,2048]{2,1,0:T(2,128)(2,1)} reshape(bf16[32,1,2,2,16,64]{5,4,3,2,1,0:T(8,128)(2,1)S(1)} %bitcast.83) | data formatting | bytes 524288
  7.0 11.8 %all-to-all-start = ((bf16[32,2,2048]{2,1,0:T(2,128)(2,1)}), bf16[32,2,2048]{2,1,0:T(2,128)(2,1)S(1)}, u32[]{:S(2)}, u32[]{:S(2)}) async-start(bf16[32,2,2048]{2,1,0:T(2,128)(2,1)} %reshape.97), calls=%async_computation | async-start | bytes 524288 | tf_op jit(solution)/shard_map/all_to_all | solution.py:105
  18.8 0.1 copy.66
  18.9 0.1 copy.68
  19.0 0.7 copy.70.bias_ref
  19.7 0.7 copy.65
  20.4 7.3 %fusion.67 = (bf16[1,64,2,64,64]{4,3,2,1,0:T(8,128)(2,1)S(1)}, bf16[1,64,2,64,64]{4,3,2,1,0:T(8,128)(2,1)}, bf16[1,64,2,64,64]{4,3,2,1,0:T(8,128)(2,1)}) fusion(bf16[3,64,2,64,64]{4,3,2,1,0:T(8,128)(2,1)} %param.8), kind=kLoop, calls=%fused_computation.85 | loop fusion | bytes 6291456 | tf_op jit(solution)/shard_map/slice | solution.py:112
  27.8 3.9 %all-to-all-done = bf16[32,2,2048]{2,1,0:T(2,128)(2,1)S(1)} async-done(((bf16[32,2,2048]{2,1,0:T(2,128)(2,1)}), bf16[32,2,2048]{2,1,0:T(2,128)(2,1)S(1)}, u32[]{:S(2)}, u32[]{:S(2)}) %all-to-all-start) | async-done | bytes 262176 | tf_op jit(solution)/shard_map/all_to_all | solution.py:105
  31.7 0.4 reshape.98
  32.1 1.6 %fusion.12 = bf16[64,2,2,64]{3,0,2,1:T(8,128)(2,1)S(1)} fusion(bf16[32,2,2,1,16,64]{5,4,2,1,3,0:T(8,128)(2,1)S(1)} %bitcast.86, s32[64]{0:T(128)S(1)} %iota_add_fusion, s32[32,16]{0,1:T(8,128)S(1)} %multiply_add_fusion), kind=kOutput, calls=%fused_computation.15 | convolution fusion | flops 17350656 | bytes 297216 | tf_op jit(solution)/shard_map/sjblnc,snk->jblkc/dot_general | solution.py:107
  33.6 2.4 %collective-permute-start.1 = (bf16[2,2,1,64,64]{4,3,1,0,2:T(8,128)(2,1)S(1)}, bf16[2,2,1,64,64]{4,3,1,0,2:T(8,128)(2,1)S(1)}, u32[]{:S(2)}, u32[]{:S(2)}) collective-permute-start(bf16[2,2,1,64,64]{4,3,1,0,2:T(8,128)(2,1)S(1)} %bitcast.91), channel_id=1, source_target_pairs={{1,0},{2,1},{3,2},{4,3},{5,4},{6,5},{7,6},{9,8},{10,9},{11,10},{12... | collective-permute-start | bytes 98312 | tf_op jit(solution)/shard_map/ppermute | solution.py:21
  36.0 2.9 %collective-permute-start = (bf16[2,2,1,64,64]{4,3,1,0,2:T(8,128)(2,1)S(1)}, bf16[2,2,1,64,64]{4,3,1,0,2:T(8,128)(2,1)S(1)}, u32[]{:S(2)}, u32[]{:S(2)}) collective-permute-start(bf16[2,2,1,64,64]{4,3,1,0,2:T(8,128)(2,1)S(1)} %bitcast.92), channel_id=1, source_target_pairs={{0,1},{1,2},{2,3},{3,4},{4,5},{5,6},{6,7},{8,9},{9,10},{10,11},{11... | collective-permute-start | bytes 98312 | tf_op jit(solution)/shard_map/ppermute | solution.py:19
  38.9 2.2 %fusion.3 = f32[2,64,2,64]{3,2,1,0:T(2,128)S(1)} fusion(bf16[1,64,2,64,64]{4,3,2,1,0:T(8,128)(2,1)} %get-tuple-element.6, bf16[2,2,64,64]{3,2,1,0:T(8,128)(2,1)S(1)} %bitcast.93), kind=kOutput, calls=%fused_computation.5 | convolution fusion | flops 2097152 | bytes 1146880 | tf_op jit(solution)/shard_map/kjco,jblkc->jblko/dot_general | solution.py:116
  41.2 0.0 collective-permute-done.1
  41.2 0.7 fusion.2
  41.8 0.1 collective-permute-done
  41.9 0.7 fusion.13
  42.6 1.5 %fusion.8 = bf16[32,2,2,1,16,64]{5,0,4,2,1,3:T(8,128)(2,1)S(1)} fusion(s32[64]{0:T(128)S(1)} %iota_add_fusion, s32[32,16]{0,1:T(8,128)S(1)} %multiply_add_fusion, bf16[2,2,64,64,1]{3,1,2,0,4:T(2,128)(2,1)S(1)} %fusion.13), kind=kOutput, calls=%fused_computation.10 | convolution fusion | flops 17465344 | bytes 297216 | tf_op jit(solution)/shard_map/rnk,jblko->rjblno/dot_general | solution.py:129
  44.1 0.2 copy.109
  44.3 1.1 %reshape.99 = bf16[32,2,2048]{2,1,0:T(2,128)(2,1)} reshape(bf16[32,1,2,2,16,64]{5,4,3,2,1,0:T(8,128)(2,1)S(1)} %bitcast.84) | data formatting | bytes 524288
  45.4 7.9 %all-to-all-start.1 = ((bf16[32,2,2048]{2,1,0:T(2,128)(2,1)}), bf16[32,2,2048]{2,1,0:T(2,128)(2,1)S(1)}, u32[]{:S(2)}, u32[]{:S(2)}) async-start(bf16[32,2,2048]{2,1,0:T(2,128)(2,1)} %reshape.99), calls=%async_computation.1 | async-start | bytes 524288 | tf_op jit(solution)/shard_map/all_to_all | solution.py:130
  53.3 0.7 maximum_bitcast_fusion.gate_up_ref
  54.0 1.8 %multiply_convert_fusion.lon_ref = bf16[64,1024]{1,0:T(8,128)(2,1)} fusion(s32[64]{0:T(128)S(1)} %iota_add_fusion), kind=kLoop, calls=%fused_computation.39 | loop fusion | flops 1114112 | bytes 131328 | tf_op jit(solution)/shard_map/convert_element_type | solution.py:96
  55.8 10.4 %all-to-all-done.1 = bf16[32,2,2048]{2,1,0:T(2,128)(2,1)S(1)} async-done(((bf16[32,2,2048]{2,1,0:T(2,128)(2,1)}), bf16[32,2,2048]{2,1,0:T(2,128)(2,1)S(1)}, u32[]{:S(2)}, u32[]{:S(2)}) %all-to-all-start.1) | async-done | bytes 262176 | tf_op jit(solution)/shard_map/all_to_all | solution.py:130
  66.2 0.4 reshape.100
  66.6 1.4 %copy.69.back_ref = bf16[32,64,64]{2,1,0:T(8,128)(2,1)} copy(bf16[32,64,64]{1,0,2:T(8,128)(2,1)S(1)} %bitcast.85) | data formatting | bytes 524288 | tf_op jit(solution)/shard_map/reshape;reshape | solution.py:137
  68.0 16.6 %shard_map.73 = bf16[32,64,1024]{2,1,0:T(8,128)(2,1)} custom-call(bf16[32,64,1024]{2,1,0:T(8,128)(2,1)} %bitcast.90, bf16[32,64,64]{2,1,0:T(8,128)(2,1)} %copy.69.back_ref, bf16[64,1024]{1,0:T(8,128)(2,1)} %multiply_convert_fusion.lon_ref, bf16[64,64]{1,0:T(8,128)(2,1)} %bitcast.88, f32[64,1]{1,0:T(8,128)} %copy.70.bias_ref, ...), custom_call_target="tpu_custom_call" | custom-call | flops 3758096384 | bytes 8650752 | tf_op jit(solution)/shard_map/pallas_call | solution.py:60
  (10 shorter events, 0.0 us)
Async XLA Ops:
  5.2 13.5 %copy-start.1 = (bf16[64,256]{1,0:T(8,128)(2,1)S(1)}, bf16[64,256]{1,0:T(8,128)(2,1)}, u32[]{:S(2)}) copy-start(bf16[64,256]{1,0:T(8,128)(2,1)} %param.11) | copy-start | bytes 98308
  5.2 13.6 %copy-start.2 = (bf16[64,256]{1,0:T(8,128)(2,1)S(1)}, bf16[64,256]{1,0:T(8,128)(2,1)}, u32[]{:S(2)}) copy-start(bf16[64,256]{1,0:T(8,128)(2,1)} %param.12) | copy-start | bytes 98308
  5.3 13.8 %copy-start.4 = (f32[64]{0:T(128)S(1)}, f32[64]{0:T(128)}, u32[]{:S(2)}) copy-start(f32[64]{0:T(128)} %param.10) | copy-start | bytes 772
  5.3 14.5 %copy-start.3 = (bf16[64,64]{1,0:T(8,128)(2,1)S(1)}, bf16[64,64]{1,0:T(8,128)(2,1)}, u32[]{:S(2)}) copy-start(bf16[64,64]{1,0:T(8,128)(2,1)} %param.9) | copy-start | bytes 24580
  7.0 24.7 %all-to-all-start = ((bf16[32,2,2048]{2,1,0:T(2,128)(2,1)}), bf16[32,2,2048]{2,1,0:T(2,128)(2,1)S(1)}, u32[]{:S(2)}, u32[]{:S(2)}) async-start(bf16[32,2,2048]{2,1,0:T(2,128)(2,1)} %reshape.97), calls=%async_computation | async-start | bytes 524288 | tf_op jit(solution)/shard_map/all_to_all | solution.py:105
  32.1 9.1 %copy-start = (bf16[1,64,2,64,64]{4,3,2,1,0:T(8,128)(2,1)S(1)}, bf16[1,64,2,64,64]{4,3,2,1,0:T(8,128)(2,1)}, u32[]{:S(2)}) copy-start(bf16[1,64,2,64,64]{4,3,2,1,0:T(8,128)(2,1)} %get-tuple-element.7) | copy-start | bytes 3145732
  33.6 7.5 %collective-permute-start.1 = (bf16[2,2,1,64,64]{4,3,1,0,2:T(8,128)(2,1)S(1)}, bf16[2,2,1,64,64]{4,3,1,0,2:T(8,128)(2,1)S(1)}, u32[]{:S(2)}, u32[]{:S(2)}) collective-permute-start(bf16[2,2,1,64,64]{4,3,1,0,2:T(8,128)(2,1)S(1)} %bitcast.91), channel_id=1, source_target_pairs={{1,0},{2,1},{3,2},{4,3},{5,4},{6,5},{7,6},{9,8},{10,9},{11,10},{12... | collective-permute-start | bytes 98312 | tf_op jit(solution)/shard_map/ppermute | solution.py:21
  36.0 5.9 %collective-permute-start = (bf16[2,2,1,64,64]{4,3,1,0,2:T(8,128)(2,1)S(1)}, bf16[2,2,1,64,64]{4,3,1,0,2:T(8,128)(2,1)S(1)}, u32[]{:S(2)}, u32[]{:S(2)}) collective-permute-start(bf16[2,2,1,64,64]{4,3,1,0,2:T(8,128)(2,1)S(1)} %bitcast.92), channel_id=1, source_target_pairs={{0,1},{1,2},{2,3},{3,4},{4,5},{5,6},{6,7},{8,9},{9,10},{10,11},{11... | collective-permute-start | bytes 98312 | tf_op jit(solution)/shard_map/ppermute | solution.py:19
  45.4 20.8 %all-to-all-start.1 = ((bf16[32,2,2048]{2,1,0:T(2,128)(2,1)}), bf16[32,2,2048]{2,1,0:T(2,128)(2,1)S(1)}, u32[]{:S(2)}, u32[]{:S(2)}) async-start(bf16[32,2,2048]{2,1,0:T(2,128)(2,1)} %reshape.99), calls=%async_computation.1 | async-start | bytes 524288 | tf_op jit(solution)/shard_map/all_to_all | solution.py:130

commit v17 on v15

--- a/solution.py
+++ b/solution.py
@@ -90,7 +90,6 @@
 
 
 def body(field, spectral_weight, local_weight, local_bias, gate_weight, up_weight, down_weight):
-    high = lax.Precision.HIGHEST
     batch, levels, lat_rows, chans, lon_cells = field.shape
     ranks = lax.axis_size("rows")
     lat_total = lat_rows * ranks
@@ -105,8 +104,9 @@
     per = lon_modes // ranks
     along = jnp.einsum("xm,blncx->mblnc", lon_table, field, preferred_element_type=jnp.float32)
     along = along.astype(jnp.bfloat16).reshape((ranks, per) + along.shape[1:])
-    along = lax.all_to_all(along, "rows", 0, 0, tiled=True).astype(jnp.float32)
-    modes = jnp.einsum("sjblnc,snk->jblkc", along, lat_table, precision=high)
+    along = lax.all_to_all(along, "rows", 0, 0, tiled=True)
+    lat_b = lat_table.astype(jnp.bfloat16)
+    modes = jnp.einsum("sjblnc,snk->jblkc", along, lat_b, preferred_element_type=jnp.float32)
     modes = modes.astype(jnp.bfloat16)
     padded = extended(modes, (("lev", 2),), 1)
     mixed = jnp.einsum(
@@ -128,9 +128,7 @@
         preferred_element_type=jnp.float32,
     )
     mixed_b = mixed.astype(jnp.bfloat16)
-    values = jnp.einsum(
-        "rnk,jblko->rjblno", lat_table, mixed_b.astype(jnp.float32), precision=high
-    )
+    values = jnp.einsum("rnk,jblko->rjblno", lat_b, mixed_b, preferred_element_type=jnp.float32)
     values = lax.all_to_all(values.astype(jnp.bfloat16), "rows", 0, 0, tiled=True)
     back_b = values.reshape(lon_modes, batch * levels * lat_rows, chans)
 

time: 85.5 us -> 84.9 us (level)
  no operation moved by 1% of the time
where the time goes in v17:
time: 84.9 us; the launch traced here: 84.5 us
  starting transfers between devices  24.9 us (29%)
  Pallas kernels  17.2 us (20%)
  waiting for transfers between devices  14.5 us (17%)
  local copies, waits for them, and re-layouts  13.5 us (16%)
  matrix products  11.8 us (14%)
  other arithmetic  2.52 us (3%)
    pallas_call x1, Pallas kernels, finish(): pl.pallas_call(finish_kernel, out_shape=jax.ShapeDtypeStruct(field.shape,...  17.2 us
    all_to_all x1, starting transfers between devices, body(): along = lax.all_to_all(along, 'rows', 0, 0, tiled=True)  11.8 us
    all_to_all x1, waiting for transfers between devices, body(): lax.all_to_all(values.astype(jnp.bfloat16), 'rows', 0, 0, tiled=True)  10.4 us
    all_to_all x1, starting transfers between devices, body(): lax.all_to_all(values.astype(jnp.bfloat16), 'rows', 0, 0, tiled=True)  7.89 us
    slice x1, local copies, waits for them, and re-layouts, body(): spectral_weight[0]  7.34 us
    dot_general x1, matrix products, body(): jnp.einsum('xm,blncx->mblnc', lon_table, field, preferred_element_type=jn...  5.24 us
    unnamed x17, local copies, waits for them, and re-layouts  4.67 us
    all_to_all x1, waiting for transfers between devices, body(): along = lax.all_to_all(along, 'rows', 0, 0, tiled=True)  3.93 us
  transfers between devices with their start and end apart: 4, of which 3 were waited for; matrix products, arithmetic and copies ran while one was open for 17% of the time, Pallas kernels for 0%

profile of v17, /device:TPU:25, one launch (start us, length us, event | category | flops | bytes accessed | tf_op | source)
XLA Modules:
  0.0 84.5 jit_solution(4125175114824815895)
XLA Ops:
  0.0 5.2 %fusion.5 = bf16[64,2,16,64]{3,0,2,1:T(8,128)(2,1)S(1)} fusion(bf16[2,1,16,64,1024]{4,3,2,1,0:T(8,128)(2,1)} %param.7, s32[64]{0:T(128)S(1)} %iota_add_fusion), kind=kOutput, calls=%fused_computation.8 | convolution fusion | flops 269680640 | bytes 4456704 | tf_op jit(solution)/shard_map/xm,blncx->mblnc/dot_general | solution.py:105
  5.2 0.0 copy-start.2
  5.3 0.0 copy-start.4
  5.3 0.0 copy-start.3
  5.3 0.6 copy.91
  5.9 1.1 %reshape.101 = bf16[32,2,2048]{2,1,0:T(2,128)(2,1)} reshape(bf16[32,1,2,2,16,64]{5,4,3,2,1,0:T(8,128)(2,1)S(1)} %bitcast.79) | data formatting | bytes 524288
  7.0 11.8 %all-to-all-start = ((bf16[32,2,2048]{2,1,0:T(2,128)(2,1)}), bf16[32,2,2048]{2,1,0:T(2,128)(2,1)S(1)}, u32[]{:S(2)}, u32[]{:S(2)}) async-start(bf16[32,2,2048]{2,1,0:T(2,128)(2,1)} %reshape.101), calls=%async_computation | async-start | bytes 524288 | tf_op jit(solution)/shard_map/all_to_all | solution.py:107
  18.8 0.1 copy.48
  18.9 0.1 copy.50
  19.0 0.0 copy-done.4
  19.0 0.7 copy.51.bias_ref
  19.7 0.7 copy.47
  20.4 7.3 %fusion.67 = (bf16[1,64,2,64,64]{4,3,2,1,0:T(8,128)(2,1)S(1)}, bf16[1,64,2,64,64]{4,3,2,1,0:T(8,128)(2,1)}, bf16[1,64,2,64,64]{4,3,2,1,0:T(8,128)(2,1)}) fusion(bf16[3,64,2,64,64]{4,3,2,1,0:T(8,128)(2,1)} %param.8), kind=kLoop, calls=%fused_computation.85 | loop fusion | bytes 6291456 | tf_op jit(solution)/shard_map/slice | solution.py:114
  27.8 3.9 %all-to-all-done = bf16[32,2,2048]{2,1,0:T(2,128)(2,1)S(1)} async-done(((bf16[32,2,2048]{2,1,0:T(2,128)(2,1)}), bf16[32,2,2048]{2,1,0:T(2,128)(2,1)S(1)}, u32[]{:S(2)}, u32[]{:S(2)}) %all-to-all-start) | async-done | bytes 262176 | tf_op jit(solution)/shard_map/all_to_all | solution.py:107
  31.7 0.4 reshape.102
  32.1 1.6 %fusion.12 = bf16[64,2,2,64]{3,0,2,1:T(8,128)(2,1)S(1)} fusion(bf16[32,2,2,1,16,64]{5,4,2,1,3,0:T(8,128)(2,1)S(1)} %bitcast.82, s32[64]{0:T(128)S(1)} %iota_add_fusion, s32[32,16]{0,1:T(8,128)S(1)} %multiply_add_fusion), kind=kOutput, calls=%fused_computation.15 | convolution fusion | flops 17350656 | bytes 297216 | tf_op jit(solution)/shard_map/sjblnc,snk->jblkc/dot_general | solution.py:109
  33.6 2.4 %collective-permute-start.1 = (bf16[2,2,1,64,64]{4,3,1,0,2:T(8,128)(2,1)S(1)}, bf16[2,2,1,64,64]{4,3,1,0,2:T(8,128)(2,1)S(1)}, u32[]{:S(2)}, u32[]{:S(2)}) collective-permute-start(bf16[2,2,1,64,64]{4,3,1,0,2:T(8,128)(2,1)S(1)} %bitcast.87), channel_id=1, source_target_pairs={{1,0},{2,1},{3,2},{4,3},{5,4},{6,5},{7,6},{9,8},{10,9},{11,10},{12... | collective-permute-start | bytes 98312 | tf_op jit(solution)/shard_map/ppermute | solution.py:21
  36.0 2.9 %collective-permute-start = (bf16[2,2,1,64,64]{4,3,1,0,2:T(8,128)(2,1)S(1)}, bf16[2,2,1,64,64]{4,3,1,0,2:T(8,128)(2,1)S(1)}, u32[]{:S(2)}, u32[]{:S(2)}) collective-permute-start(bf16[2,2,1,64,64]{4,3,1,0,2:T(8,128)(2,1)S(1)} %bitcast.88), channel_id=1, source_target_pairs={{0,1},{1,2},{2,3},{3,4},{4,5},{5,6},{6,7},{8,9},{9,10},{10,11},{11... | collective-permute-start | bytes 98312 | tf_op jit(solution)/shard_map/ppermute | solution.py:19
  38.9 2.2 %fusion.3 = f32[2,64,2,64]{3,2,1,0:T(2,128)S(1)} fusion(bf16[1,64,2,64,64]{4,3,2,1,0:T(8,128)(2,1)} %get-tuple-element.6, bf16[2,2,64,64]{3,2,1,0:T(8,128)(2,1)S(1)} %bitcast.89), kind=kOutput, calls=%fused_computation.5 | convolution fusion | flops 2097152 | bytes 1146880 | tf_op jit(solution)/shard_map/kjco,jblkc->jblko/dot_general | solution.py:118
  41.2 0.0 collective-permute-done.1
  41.2 0.7 fusion.2
  41.8 0.1 collective-permute-done
  41.9 0.7 fusion.13
  42.6 1.5 %fusion.8 = bf16[32,2,2,1,16,64]{5,0,4,2,1,3:T(8,128)(2,1)S(1)} fusion(s32[64]{0:T(128)S(1)} %iota_add_fusion, s32[32,16]{0,1:T(8,128)S(1)} %multiply_add_fusion, bf16[2,2,64,64,1]{3,1,2,0,4:T(2,128)(2,1)S(1)} %fusion.13), kind=kOutput, calls=%fused_computation.10 | convolution fusion | flops 17465344 | bytes 297216 | tf_op jit(solution)/shard_map/rnk,jblko->rjblno/dot_general | solution.py:131
  44.1 0.2 copy.90
  44.3 1.1 %reshape.103 = bf16[32,2,2048]{2,1,0:T(2,128)(2,1)} reshape(bf16[32,1,2,2,16,64]{5,4,3,2,1,0:T(8,128)(2,1)S(1)} %bitcast.80) | data formatting | bytes 524288
  45.4 7.9 %all-to-all-start.1 = ((bf16[32,2,2048]{2,1,0:T(2,128)(2,1)}), bf16[32,2,2048]{2,1,0:T(2,128)(2,1)S(1)}, u32[]{:S(2)}, u32[]{:S(2)}) async-start(bf16[32,2,2048]{2,1,0:T(2,128)(2,1)} %reshape.103), calls=%async_computation.1 | async-start | bytes 524288 | tf_op jit(solution)/shard_map/all_to_all | solution.py:132
  53.3 0.7 maximum_bitcast_fusion.gate_up_ref
  54.0 1.8 %multiply_convert_fusion.lon_ref = bf16[64,1024]{1,0:T(8,128)(2,1)} fusion(s32[64]{0:T(128)S(1)} %iota_add_fusion), kind=kLoop, calls=%fused_computation.39 | loop fusion | flops 1114112 | bytes 131328 | tf_op jit(solution)/shard_map/convert_element_type | solution.py:98
  55.8 10.4 %all-to-all-done.1 = bf16[32,2,2048]{2,1,0:T(2,128)(2,1)S(1)} async-done(((bf16[32,2,2048]{2,1,0:T(2,128)(2,1)}), bf16[32,2,2048]{2,1,0:T(2,128)(2,1)S(1)}, u32[]{:S(2)}, u32[]{:S(2)}) %all-to-all-start.1) | async-done | bytes 262176 | tf_op jit(solution)/shard_map/all_to_all | solution.py:132
  66.2 1.2 %reshape.104 = bf16[32,1,2,2,16,64]{5,4,3,2,1,0:T(8,128)(2,1)} reshape(bf16[32,2,2048]{2,1,0:T(2,128)(2,1)S(1)} %all-to-all-done.1) | data formatting | bytes 524288
  67.4 17.2 %shard_map.73 = bf16[32,64,1024]{2,1,0:T(8,128)(2,1)} custom-call(bf16[32,64,1024]{2,1,0:T(8,128)(2,1)} %bitcast.86, bf16[64,32,64]{2,1,0:T(8,128)(2,1)} %bitcast.81, bf16[64,1024]{1,0:T(8,128)(2,1)} %multiply_convert_fusion.lon_ref, bf16[64,64]{1,0:T(8,128)(2,1)} %bitcast.84, f32[64,1]{1,0:T(8,128)} %copy.51.bias_ref, ...), custom_call_target="tpu_custom_call" | custom-call | flops 3758096384 | bytes 8650752 | tf_op jit(solution)/shard_map/pallas_call | solution.py:62
  (9 shorter events, 0.0 us)
Async XLA Ops:
  5.2 13.5 %copy-start.1 = (bf16[64,256]{1,0:T(8,128)(2,1)S(1)}, bf16[64,256]{1,0:T(8,128)(2,1)}, u32[]{:S(2)}) copy-start(bf16[64,256]{1,0:T(8,128)(2,1)} %param.11) | copy-start | bytes 98308
  5.2 13.6 %copy-start.2 = (bf16[64,256]{1,0:T(8,128)(2,1)S(1)}, bf16[64,256]{1,0:T(8,128)(2,1)}, u32[]{:S(2)}) copy-start(bf16[64,256]{1,0:T(8,128)(2,1)} %param.12) | copy-start | bytes 98308
  5.3 13.8 %copy-start.4 = (f32[64]{0:T(128)S(1)}, f32[64]{0:T(128)}, u32[]{:S(2)}) copy-start(f32[64]{0:T(128)} %param.10) | copy-start | bytes 772
  5.3 14.5 %copy-start.3 = (bf16[64,64]{1,0:T(8,128)(2,1)S(1)}, bf16[64,64]{1,0:T(8,128)(2,1)}, u32[]{:S(2)}) copy-start(bf16[64,64]{1,0:T(8,128)(2,1)} %param.9) | copy-start | bytes 24580
  7.0 24.7 %all-to-all-start = ((bf16[32,2,2048]{2,1,0:T(2,128)(2,1)}), bf16[32,2,2048]{2,1,0:T(2,128)(2,1)S(1)}, u32[]{:S(2)}, u32[]{:S(2)}) async-start(bf16[32,2,2048]{2,1,0:T(2,128)(2,1)} %reshape.101), calls=%async_computation | async-start | bytes 524288 | tf_op jit(solution)/shard_map/all_to_all | solution.py:107
  32.1 9.1 %copy-start = (bf16[1,64,2,64,64]{4,3,2,1,0:T(8,128)(2,1)S(1)}, bf16[1,64,2,64,64]{4,3,2,1,0:T(8,128)(2,1)}, u32[]{:S(2)}) copy-start(bf16[1,64,2,64,64]{4,3,2,1,0:T(8,128)(2,1)} %get-tuple-element.7) | copy-start | bytes 3145732
  33.6 7.5 %collective-permute-start.1 = (bf16[2,2,1,64,64]{4,3,1,0,2:T(8,128)(2,1)S(1)}, bf16[2,2,1,64,64]{4,3,1,0,2:T(8,128)(2,1)S(1)}, u32[]{:S(2)}, u32[]{:S(2)}) collective-permute-start(bf16[2,2,1,64,64]{4,3,1,0,2:T(8,128)(2,1)S(1)} %bitcast.87), channel_id=1, source_target_pairs={{1,0},{2,1},{3,2},{4,3},{5,4},{6,5},{7,6},{9,8},{10,9},{11,10},{12... | collective-permute-start | bytes 98312 | tf_op jit(solution)/shard_map/ppermute | solution.py:21
  36.0 5.9 %collective-permute-start = (bf16[2,2,1,64,64]{4,3,1,0,2:T(8,128)(2,1)S(1)}, bf16[2,2,1,64,64]{4,3,1,0,2:T(8,128)(2,1)S(1)}, u32[]{:S(2)}, u32[]{:S(2)}) collective-permute-start(bf16[2,2,1,64,64]{4,3,1,0,2:T(8,128)(2,1)S(1)} %bitcast.88), channel_id=1, source_target_pairs={{0,1},{1,2},{2,3},{3,4},{4,5},{5,6},{6,7},{8,9},{9,10},{10,11},{11... | collective-permute-start | bytes 98312 | tf_op jit(solution)/shard_map/ppermute | solution.py:19
  45.4 20.8 %all-to-all-start.1 = ((bf16[32,2,2048]{2,1,0:T(2,128)(2,1)}), bf16[32,2,2048]{2,1,0:T(2,128)(2,1)S(1)}, u32[]{:S(2)}, u32[]{:S(2)}) async-start(bf16[32,2,2048]{2,1,0:T(2,128)(2,1)} %reshape.103), calls=%async_computation.1 | async-start | bytes 524288 | tf_op jit(solution)/shard_map/all_to_all | solution.py:132

commit v18 on v17

--- a/solution.py
+++ b/solution.py
@@ -47,7 +47,8 @@
     both = jnp.dot(gate_up_ref[...], act, preferred_element_type=jnp.float32)
     hid = gate_up_ref.shape[0] // 2
     half, upper = both[:hid], both[hid:]
-    hidden = ((half + half * jnp.tanh(half)) * upper).astype(jnp.bfloat16)
+    half = half.astype(jnp.bfloat16)
+    hidden = (half + half * jnp.tanh(half)) * upper.astype(jnp.bfloat16)
     down = jnp.dot(down_ref[...], hidden, preferred_element_type=jnp.float32)
     for r in range(rows):
         grid = field_ref[r].astype(jnp.float32)

time: 84.9 us -> 84.8 us (level)
  no operation moved by 1% of the time
where the time goes in v18:
time: 84.8 us; the launch traced here: 84.4 us
  starting transfers between devices  24.9 us (29%)
  Pallas kernels  17 us (20%)
  waiting for transfers between devices  14.5 us (17%)
  local copies, waits for them, and re-layouts  13.5 us (16%)
  matrix products  11.8 us (14%)
  other arithmetic  2.52 us (3%)
    pallas_call x1, Pallas kernels, finish(): pl.pallas_call(finish_kernel, out_shape=jax.ShapeDtypeStruct(field.shape,...  17 us
    all_to_all x1, starting transfers between devices, body(): along = lax.all_to_all(along, 'rows', 0, 0, tiled=True)  11.8 us
    all_to_all x1, waiting for transfers between devices, body(): lax.all_to_all(values.astype(jnp.bfloat16), 'rows', 0, 0, tiled=True)  10.4 us
    all_to_all x1, starting transfers between devices, body(): lax.all_to_all(values.astype(jnp.bfloat16), 'rows', 0, 0, tiled=True)  7.89 us
    slice x1, local copies, waits for them, and re-layouts, body(): spectral_weight[0]  7.34 us
    dot_general x1, matrix products, body(): jnp.einsum('xm,blncx->mblnc', lon_table, field, preferred_element_type=jn...  5.24 us
    unnamed x17, local copies, waits for them, and re-layouts  4.67 us
    all_to_all x1, waiting for transfers between devices, body(): along = lax.all_to_all(along, 'rows', 0, 0, tiled=True)  3.93 us
  transfers between devices with their start and end apart: 4, of which 3 were waited for; matrix products, arithmetic and copies ran while one was open for 17% of the time, Pallas kernels for 0%

profile of v18, /device:TPU:25, one launch (start us, length us, event | category | flops | bytes accessed | tf_op | source)
XLA Modules:
  0.0 84.4 jit_solution(1625167848778611850)
XLA Ops:
  0.0 5.2 %fusion.5 = bf16[64,2,16,64]{3,0,2,1:T(8,128)(2,1)S(1)} fusion(bf16[2,1,16,64,1024]{4,3,2,1,0:T(8,128)(2,1)} %param.7, s32[64]{0:T(128)S(1)} %iota_add_fusion), kind=kOutput, calls=%fused_computation.8 | convolution fusion | flops 269680640 | bytes 4456704 | tf_op jit(solution)/shard_map/xm,blncx->mblnc/dot_general | solution.py:106
  5.2 0.0 copy-start.2
  5.3 0.0 copy-start.4
  5.3 0.0 copy-start.3
  5.3 0.6 copy.91
  5.9 1.1 %reshape.101 = bf16[32,2,2048]{2,1,0:T(2,128)(2,1)} reshape(bf16[32,1,2,2,16,64]{5,4,3,2,1,0:T(8,128)(2,1)S(1)} %bitcast.79) | data formatting | bytes 524288
  7.0 11.8 %all-to-all-start = ((bf16[32,2,2048]{2,1,0:T(2,128)(2,1)}), bf16[32,2,2048]{2,1,0:T(2,128)(2,1)S(1)}, u32[]{:S(2)}, u32[]{:S(2)}) async-start(bf16[32,2,2048]{2,1,0:T(2,128)(2,1)} %reshape.101), calls=%async_computation | async-start | bytes 524288 | tf_op jit(solution)/shard_map/all_to_all | solution.py:108
  18.8 0.1 copy.48
  18.9 0.1 copy.50
  19.0 0.0 copy-done.4
  19.0 0.7 copy.51.bias_ref
  19.7 0.7 copy.47
  20.4 7.3 %fusion.67 = (bf16[1,64,2,64,64]{4,3,2,1,0:T(8,128)(2,1)S(1)}, bf16[1,64,2,64,64]{4,3,2,1,0:T(8,128)(2,1)}, bf16[1,64,2,64,64]{4,3,2,1,0:T(8,128)(2,1)}) fusion(bf16[3,64,2,64,64]{4,3,2,1,0:T(8,128)(2,1)} %param.8), kind=kLoop, calls=%fused_computation.85 | loop fusion | bytes 6291456 | tf_op jit(solution)/shard_map/slice | solution.py:115
  27.8 3.9 %all-to-all-done = bf16[32,2,2048]{2,1,0:T(2,128)(2,1)S(1)} async-done(((bf16[32,2,2048]{2,1,0:T(2,128)(2,1)}), bf16[32,2,2048]{2,1,0:T(2,128)(2,1)S(1)}, u32[]{:S(2)}, u32[]{:S(2)}) %all-to-all-start) | async-done | bytes 262176 | tf_op jit(solution)/shard_map/all_to_all | solution.py:108
  31.7 0.4 reshape.102
  32.1 1.6 %fusion.12 = bf16[64,2,2,64]{3,0,2,1:T(8,128)(2,1)S(1)} fusion(bf16[32,2,2,1,16,64]{5,4,2,1,3,0:T(8,128)(2,1)S(1)} %bitcast.82, s32[64]{0:T(128)S(1)} %iota_add_fusion, s32[32,16]{0,1:T(8,128)S(1)} %multiply_add_fusion), kind=kOutput, calls=%fused_computation.15 | convolution fusion | flops 17350656 | bytes 297216 | tf_op jit(solution)/shard_map/sjblnc,snk->jblkc/dot_general | solution.py:110
  33.6 2.4 %collective-permute-start.1 = (bf16[2,2,1,64,64]{4,3,1,0,2:T(8,128)(2,1)S(1)}, bf16[2,2,1,64,64]{4,3,1,0,2:T(8,128)(2,1)S(1)}, u32[]{:S(2)}, u32[]{:S(2)}) collective-permute-start(bf16[2,2,1,64,64]{4,3,1,0,2:T(8,128)(2,1)S(1)} %bitcast.87), channel_id=1, source_target_pairs={{1,0},{2,1},{3,2},{4,3},{5,4},{6,5},{7,6},{9,8},{10,9},{11,10},{12... | collective-permute-start | bytes 98312 | tf_op jit(solution)/shard_map/ppermute | solution.py:21
  36.0 2.9 %collective-permute-start = (bf16[2,2,1,64,64]{4,3,1,0,2:T(8,128)(2,1)S(1)}, bf16[2,2,1,64,64]{4,3,1,0,2:T(8,128)(2,1)S(1)}, u32[]{:S(2)}, u32[]{:S(2)}) collective-permute-start(bf16[2,2,1,64,64]{4,3,1,0,2:T(8,128)(2,1)S(1)} %bitcast.88), channel_id=1, source_target_pairs={{0,1},{1,2},{2,3},{3,4},{4,5},{5,6},{6,7},{8,9},{9,10},{10,11},{11... | collective-permute-start | bytes 98312 | tf_op jit(solution)/shard_map/ppermute | solution.py:19
  38.9 2.2 %fusion.3 = f32[2,64,2,64]{3,2,1,0:T(2,128)S(1)} fusion(bf16[1,64,2,64,64]{4,3,2,1,0:T(8,128)(2,1)} %get-tuple-element.6, bf16[2,2,64,64]{3,2,1,0:T(8,128)(2,1)S(1)} %bitcast.89), kind=kOutput, calls=%fused_computation.5 | convolution fusion | flops 2097152 | bytes 1146880 | tf_op jit(solution)/shard_map/kjco,jblkc->jblko/dot_general | solution.py:119
  41.2 0.0 collective-permute-done.1
  41.2 0.7 fusion.2
  41.8 0.1 collective-permute-done
  41.9 0.7 fusion.13
  42.6 1.5 %fusion.8 = bf16[32,2,2,1,16,64]{5,0,4,2,1,3:T(8,128)(2,1)S(1)} fusion(s32[64]{0:T(128)S(1)} %iota_add_fusion, s32[32,16]{0,1:T(8,128)S(1)} %multiply_add_fusion, bf16[2,2,64,64,1]{3,1,2,0,4:T(2,128)(2,1)S(1)} %fusion.13), kind=kOutput, calls=%fused_computation.10 | convolution fusion | flops 17465344 | bytes 297216 | tf_op jit(solution)/shard_map/rnk,jblko->rjblno/dot_general | solution.py:132
  44.1 0.2 copy.90
  44.3 1.1 %reshape.103 = bf16[32,2,2048]{2,1,0:T(2,128)(2,1)} reshape(bf16[32,1,2,2,16,64]{5,4,3,2,1,0:T(8,128)(2,1)S(1)} %bitcast.80) | data formatting | bytes 524288
  45.4 7.9 %all-to-all-start.1 = ((bf16[32,2,2048]{2,1,0:T(2,128)(2,1)}), bf16[32,2,2048]{2,1,0:T(2,128)(2,1)S(1)}, u32[]{:S(2)}, u32[]{:S(2)}) async-start(bf16[32,2,2048]{2,1,0:T(2,128)(2,1)} %reshape.103), calls=%async_computation.1 | async-start | bytes 524288 | tf_op jit(solution)/shard_map/all_to_all | solution.py:133
  53.3 0.7 maximum_bitcast_fusion.gate_up_ref
  54.0 1.8 %multiply_convert_fusion.lon_ref = bf16[64,1024]{1,0:T(8,128)(2,1)} fusion(s32[64]{0:T(128)S(1)} %iota_add_fusion), kind=kLoop, calls=%fused_computation.39 | loop fusion | flops 1114112 | bytes 131328 | tf_op jit(solution)/shard_map/convert_element_type | solution.py:99
  55.8 10.4 %all-to-all-done.1 = bf16[32,2,2048]{2,1,0:T(2,128)(2,1)S(1)} async-done(((bf16[32,2,2048]{2,1,0:T(2,128)(2,1)}), bf16[32,2,2048]{2,1,0:T(2,128)(2,1)S(1)}, u32[]{:S(2)}, u32[]{:S(2)}) %all-to-all-start.1) | async-done | bytes 262176 | tf_op jit(solution)/shard_map/all_to_all | solution.py:133
  66.2 1.2 %reshape.104 = bf16[32,1,2,2,16,64]{5,4,3,2,1,0:T(8,128)(2,1)} reshape(bf16[32,2,2048]{2,1,0:T(2,128)(2,1)S(1)} %all-to-all-done.1) | data formatting | bytes 524288
  67.4 17.0 %shard_map.73 = bf16[32,64,1024]{2,1,0:T(8,128)(2,1)} custom-call(bf16[32,64,1024]{2,1,0:T(8,128)(2,1)} %bitcast.86, bf16[64,32,64]{2,1,0:T(8,128)(2,1)} %bitcast.81, bf16[64,1024]{1,0:T(8,128)(2,1)} %multiply_convert_fusion.lon_ref, bf16[64,64]{1,0:T(8,128)(2,1)} %bitcast.84, f32[64,1]{1,0:T(8,128)} %copy.51.bias_ref, ...), custom_call_target="tpu_custom_call" | custom-call | flops 3758096384 | bytes 8650752 | tf_op jit(solution)/shard_map/pallas_call | solution.py:63
  (9 shorter events, 0.0 us)
Async XLA Ops:
  5.2 13.5 %copy-start.1 = (bf16[64,256]{1,0:T(8,128)(2,1)S(1)}, bf16[64,256]{1,0:T(8,128)(2,1)}, u32[]{:S(2)}) copy-start(bf16[64,256]{1,0:T(8,128)(2,1)} %param.11) | copy-start | bytes 98308
  5.2 13.6 %copy-start.2 = (bf16[64,256]{1,0:T(8,128)(2,1)S(1)}, bf16[64,256]{1,0:T(8,128)(2,1)}, u32[]{:S(2)}) copy-start(bf16[64,256]{1,0:T(8,128)(2,1)} %param.12) | copy-start | bytes 98308
  5.3 13.8 %copy-start.4 = (f32[64]{0:T(128)S(1)}, f32[64]{0:T(128)}, u32[]{:S(2)}) copy-start(f32[64]{0:T(128)} %param.10) | copy-start | bytes 772
  5.3 14.5 %copy-start.3 = (bf16[64,64]{1,0:T(8,128)(2,1)S(1)}, bf16[64,64]{1,0:T(8,128)(2,1)}, u32[]{:S(2)}) copy-start(bf16[64,64]{1,0:T(8,128)(2,1)} %param.9) | copy-start | bytes 24580
  7.0 24.7 %all-to-all-start = ((bf16[32,2,2048]{2,1,0:T(2,128)(2,1)}), bf16[32,2,2048]{2,1,0:T(2,128)(2,1)S(1)}, u32[]{:S(2)}, u32[]{:S(2)}) async-start(bf16[32,2,2048]{2,1,0:T(2,128)(2,1)} %reshape.101), calls=%async_computation | async-start | bytes 524288 | tf_op jit(solution)/shard_map/all_to_all | solution.py:108
  32.1 9.1 %copy-start = (bf16[1,64,2,64,64]{4,3,2,1,0:T(8,128)(2,1)S(1)}, bf16[1,64,2,64,64]{4,3,2,1,0:T(8,128)(2,1)}, u32[]{:S(2)}) copy-start(bf16[1,64,2,64,64]{4,3,2,1,0:T(8,128)(2,1)} %get-tuple-element.7) | copy-start | bytes 3145732
  33.6 7.5 %collective-permute-start.1 = (bf16[2,2,1,64,64]{4,3,1,0,2:T(8,128)(2,1)S(1)}, bf16[2,2,1,64,64]{4,3,1,0,2:T(8,128)(2,1)S(1)}, u32[]{:S(2)}, u32[]{:S(2)}) collective-permute-start(bf16[2,2,1,64,64]{4,3,1,0,2:T(8,128)(2,1)S(1)} %bitcast.87), channel_id=1, source_target_pairs={{1,0},{2,1},{3,2},{4,3},{5,4},{6,5},{7,6},{9,8},{10,9},{11,10},{12... | collective-permute-start | bytes 98312 | tf_op jit(solution)/shard_map/ppermute | solution.py:21
  36.0 5.9 %collective-permute-start = (bf16[2,2,1,64,64]{4,3,1,0,2:T(8,128)(2,1)S(1)}, bf16[2,2,1,64,64]{4,3,1,0,2:T(8,128)(2,1)S(1)}, u32[]{:S(2)}, u32[]{:S(2)}) collective-permute-start(bf16[2,2,1,64,64]{4,3,1,0,2:T(8,128)(2,1)S(1)} %bitcast.88), channel_id=1, source_target_pairs={{0,1},{1,2},{2,3},{3,4},{4,5},{5,6},{6,7},{8,9},{9,10},{10,11},{11... | collective-permute-start | bytes 98312 | tf_op jit(solution)/shard_map/ppermute | solution.py:19
  45.4 20.8 %all-to-all-start.1 = ((bf16[32,2,2048]{2,1,0:T(2,128)(2,1)}), bf16[32,2,2048]{2,1,0:T(2,128)(2,1)S(1)}, u32[]{:S(2)}, u32[]{:S(2)}) async-start(bf16[32,2,2048]{2,1,0:T(2,128)(2,1)} %reshape.103), calls=%async_computation.1 | async-start | bytes 524288 | tf_op jit(solution)/shard_map/all_to_all | solution.py:133

commit v19 on v17

--- a/solution.py
+++ b/solution.py
@@ -37,7 +37,7 @@
     rows, _, lon_cells = field_ref.shape
     acts = []
     for r in range(rows):
-        lhs = jnp.concatenate([back_ref[:, r, :], local_ref[...].T], axis=0)
+        lhs = jnp.concatenate([back_ref[:, r, :], local_ref[...]], axis=0)
         rhs = jnp.concatenate([lon_ref[...], field_ref[r]], axis=0)
         value = lax.dot_general(
             lhs, rhs, (((0,), (0,)), ((), ())), preferred_element_type=jnp.float32
@@ -82,7 +82,7 @@
         field,
         back,
         lon_table.T,
-        local_weight.T,
+        local_weight,
         local_bias.reshape(chans, 1),
         jnp.concatenate([(gate_weight * 0.5).astype(gate_weight.dtype), up_weight], axis=1).T,
         down_weight.T,

time: 84.9 us -> 84.5 us (level)
    unnamed x17 -> x14, local copies, waits for them, and re-layouts: 4.67 us -> 3.97 us
  transfers between devices with their start and end apart: 4 -> 4, of which waited for: 3 -> 3; matrix products, arithmetic and copies ran while one was open for 17% -> 16% of each run, Pallas kernels for 0% -> 0%
where the time goes in v19:
time: 84.5 us; the launch traced here: 84.1 us
  starting transfers between devices  24.2 us (29%)
  Pallas kernels  17.4 us (21%)
  waiting for transfers between devices  15.1 us (18%)
  local copies, waits for them, and re-layouts  12.8 us (15%)
  matrix products  11.8 us (14%)
  other arithmetic  2.52 us (3%)
    pallas_call x1, Pallas kernels, finish(): pl.pallas_call(finish_kernel, out_shape=jax.ShapeDtypeStruct(field.shape,...  17.4 us
    all_to_all x1, starting transfers between devices, body(): along = lax.all_to_all(along, 'rows', 0, 0, tiled=True)  11.8 us
    all_to_all x1, waiting for transfers between devices, body(): lax.all_to_all(values.astype(jnp.bfloat16), 'rows', 0, 0, tiled=True)  10.4 us
    slice x1, local copies, waits for them, and re-layouts, body(): spectral_weight[0]  7.34 us
    all_to_all x1, starting transfers between devices, body(): lax.all_to_all(values.astype(jnp.bfloat16), 'rows', 0, 0, tiled=True)  7.21 us
    dot_general x1, matrix products, body(): jnp.einsum('xm,blncx->mblnc', lon_table, field, preferred_element_type=jn...  5.24 us
    all_to_all x1, waiting for transfers between devices, body(): along = lax.all_to_all(along, 'rows', 0, 0, tiled=True)  4.61 us
    unnamed x14, local copies, waits for them, and re-layouts  3.97 us
  transfers between devices with their start and end apart: 4, of which 3 were waited for; matrix products, arithmetic and copies ran while one was open for 16% of the time, Pallas kernels for 0%

profile of v19, /device:TPU:25, one launch (start us, length us, event | category | flops | bytes accessed | tf_op | source)
XLA Modules:
  0.0 84.1 jit_solution(12622904790711165012)
XLA Ops:
  0.0 5.2 %fusion.5 = bf16[64,2,16,64]{3,0,2,1:T(8,128)(2,1)S(1)} fusion(bf16[2,1,16,64,1024]{4,3,2,1,0:T(8,128)(2,1)} %param.7, s32[64]{0:T(128)S(1)} %iota_add_fusion), kind=kOutput, calls=%fused_computation.8 | convolution fusion | flops 269680640 | bytes 4456704 | tf_op jit(solution)/shard_map/xm,blncx->mblnc/dot_general | solution.py:105
  5.2 0.0 copy-start.2
  5.3 0.0 copy-start.3
  5.3 0.6 copy.88
  5.9 1.1 %reshape.101 = bf16[32,2,2048]{2,1,0:T(2,128)(2,1)} reshape(bf16[32,1,2,2,16,64]{5,4,3,2,1,0:T(8,128)(2,1)S(1)} %bitcast.78) | data formatting | bytes 524288
  7.0 11.8 %all-to-all-start = ((bf16[32,2,2048]{2,1,0:T(2,128)(2,1)}), bf16[32,2,2048]{2,1,0:T(2,128)(2,1)S(1)}, u32[]{:S(2)}, u32[]{:S(2)}) async-start(bf16[32,2,2048]{2,1,0:T(2,128)(2,1)} %reshape.101), calls=%async_computation | async-start | bytes 524288 | tf_op jit(solution)/shard_map/all_to_all | solution.py:107
  18.8 0.0 copy-done.1
  18.8 0.1 copy.45
  18.9 0.0 copy-done.2
  18.9 0.1 copy.47
  19.0 0.0 copy-done.3
  19.0 0.7 copy.48.bias_ref
  19.7 7.3 %fusion.67 = (bf16[1,64,2,64,64]{4,3,2,1,0:T(8,128)(2,1)S(1)}, bf16[1,64,2,64,64]{4,3,2,1,0:T(8,128)(2,1)}, bf16[1,64,2,64,64]{4,3,2,1,0:T(8,128)(2,1)}) fusion(bf16[3,64,2,64,64]{4,3,2,1,0:T(8,128)(2,1)} %param.8), kind=kLoop, calls=%fused_computation.85 | loop fusion | bytes 6291456 | tf_op jit(solution)/shard_map/slice | solution.py:114
  27.1 4.6 %all-to-all-done = bf16[32,2,2048]{2,1,0:T(2,128)(2,1)S(1)} async-done(((bf16[32,2,2048]{2,1,0:T(2,128)(2,1)}), bf16[32,2,2048]{2,1,0:T(2,128)(2,1)S(1)}, u32[]{:S(2)}, u32[]{:S(2)}) %all-to-all-start) | async-done | bytes 262176 | tf_op jit(solution)/shard_map/all_to_all | solution.py:107
  31.7 0.4 reshape.102
  32.1 1.6 %fusion.12 = bf16[64,2,2,64]{3,0,2,1:T(8,128)(2,1)S(1)} fusion(bf16[32,2,2,1,16,64]{5,4,2,1,3,0:T(8,128)(2,1)S(1)} %bitcast.81, s32[64]{0:T(128)S(1)} %iota_add_fusion, s32[32,16]{0,1:T(8,128)S(1)} %multiply_add_fusion), kind=kOutput, calls=%fused_computation.15 | convolution fusion | flops 17350656 | bytes 297216 | tf_op jit(solution)/shard_map/sjblnc,snk->jblkc/dot_general | solution.py:109
  33.6 2.4 %collective-permute-start.1 = (bf16[2,2,1,64,64]{4,3,1,0,2:T(8,128)(2,1)S(1)}, bf16[2,2,1,64,64]{4,3,1,0,2:T(8,128)(2,1)S(1)}, u32[]{:S(2)}, u32[]{:S(2)}) collective-permute-start(bf16[2,2,1,64,64]{4,3,1,0,2:T(8,128)(2,1)S(1)} %bitcast.85), channel_id=1, source_target_pairs={{1,0},{2,1},{3,2},{4,3},{5,4},{6,5},{7,6},{9,8},{10,9},{11,10},{12... | collective-permute-start | bytes 98312 | tf_op jit(solution)/shard_map/ppermute | solution.py:21
  36.0 2.9 %collective-permute-start = (bf16[2,2,1,64,64]{4,3,1,0,2:T(8,128)(2,1)S(1)}, bf16[2,2,1,64,64]{4,3,1,0,2:T(8,128)(2,1)S(1)}, u32[]{:S(2)}, u32[]{:S(2)}) collective-permute-start(bf16[2,2,1,64,64]{4,3,1,0,2:T(8,128)(2,1)S(1)} %bitcast.86), channel_id=1, source_target_pairs={{0,1},{1,2},{2,3},{3,4},{4,5},{5,6},{6,7},{8,9},{9,10},{10,11},{11... | collective-permute-start | bytes 98312 | tf_op jit(solution)/shard_map/ppermute | solution.py:19
  38.9 2.2 %fusion.3 = f32[2,64,2,64]{3,2,1,0:T(2,128)S(1)} fusion(bf16[1,64,2,64,64]{4,3,2,1,0:T(8,128)(2,1)} %get-tuple-element.6, bf16[2,2,64,64]{3,2,1,0:T(8,128)(2,1)S(1)} %bitcast.87), kind=kOutput, calls=%fused_computation.5 | convolution fusion | flops 2097152 | bytes 1146880 | tf_op jit(solution)/shard_map/kjco,jblkc->jblko/dot_general | solution.py:118
  41.1 0.0 collective-permute-done.1
  41.1 0.7 fusion.2
  41.8 0.1 collective-permute-done
  41.9 0.7 fusion.13
  42.6 1.5 %fusion.8 = bf16[32,2,2,1,16,64]{5,0,4,2,1,3:T(8,128)(2,1)S(1)} fusion(s32[64]{0:T(128)S(1)} %iota_add_fusion, s32[32,16]{0,1:T(8,128)S(1)} %multiply_add_fusion, bf16[2,2,64,64,1]{3,1,2,0,4:T(2,128)(2,1)S(1)} %fusion.13), kind=kOutput, calls=%fused_computation.10 | convolution fusion | flops 17465344 | bytes 297216 | tf_op jit(solution)/shard_map/rnk,jblko->rjblno/dot_general | solution.py:131
  44.1 0.2 copy.87
  44.3 1.1 %reshape.103 = bf16[32,2,2048]{2,1,0:T(2,128)(2,1)} reshape(bf16[32,1,2,2,16,64]{5,4,3,2,1,0:T(8,128)(2,1)S(1)} %bitcast.79) | data formatting | bytes 524288
  45.4 7.2 %all-to-all-start.1 = ((bf16[32,2,2048]{2,1,0:T(2,128)(2,1)}), bf16[32,2,2048]{2,1,0:T(2,128)(2,1)S(1)}, u32[]{:S(2)}, u32[]{:S(2)}) async-start(bf16[32,2,2048]{2,1,0:T(2,128)(2,1)} %reshape.103), calls=%async_computation.1 | async-start | bytes 524288 | tf_op jit(solution)/shard_map/all_to_all | solution.py:132
  52.6 0.7 maximum_bitcast_fusion.gate_up_ref
  53.3 1.8 %multiply_convert_fusion.lon_ref = bf16[64,1024]{1,0:T(8,128)(2,1)} fusion(s32[64]{0:T(128)S(1)} %iota_add_fusion), kind=kLoop, calls=%fused_computation.39 | loop fusion | flops 1114112 | bytes 131328 | tf_op jit(solution)/shard_map/convert_element_type | solution.py:98
  55.1 10.4 %all-to-all-done.1 = bf16[32,2,2048]{2,1,0:T(2,128)(2,1)S(1)} async-done(((bf16[32,2,2048]{2,1,0:T(2,128)(2,1)}), bf16[32,2,2048]{2,1,0:T(2,128)(2,1)S(1)}, u32[]{:S(2)}, u32[]{:S(2)}) %all-to-all-start.1) | async-done | bytes 262176 | tf_op jit(solution)/shard_map/all_to_all | solution.py:132
  65.5 1.2 %reshape.104 = bf16[32,1,2,2,16,64]{5,4,3,2,1,0:T(8,128)(2,1)} reshape(bf16[32,2,2048]{2,1,0:T(2,128)(2,1)S(1)} %all-to-all-done.1) | data formatting | bytes 524288
  66.7 17.4 %shard_map.73 = bf16[32,64,1024]{2,1,0:T(8,128)(2,1)} custom-call(bf16[32,64,1024]{2,1,0:T(8,128)(2,1)} %bitcast.84, bf16[64,32,64]{2,1,0:T(8,128)(2,1)} %bitcast.80, bf16[64,1024]{1,0:T(8,128)(2,1)} %multiply_convert_fusion.lon_ref, bf16[64,64]{1,0:T(8,128)(2,1)} %local_ref.1, f32[64,1]{1,0:T(8,128)} %copy.48.bias_ref, ...), custom_call_target="tpu_custom_call" | custom-call | flops 3758096384 | bytes 8650752 | tf_op jit(solution)/shard_map/pallas_call | solution.py:62
  (6 shorter events, 0.0 us)
Async XLA Ops:
  5.2 13.5 %copy-start.1 = (bf16[64,256]{1,0:T(8,128)(2,1)S(1)}, bf16[64,256]{1,0:T(8,128)(2,1)}, u32[]{:S(2)}) copy-start(bf16[64,256]{1,0:T(8,128)(2,1)} %param.11) | copy-start | bytes 98308
  5.2 13.6 %copy-start.2 = (bf16[64,256]{1,0:T(8,128)(2,1)S(1)}, bf16[64,256]{1,0:T(8,128)(2,1)}, u32[]{:S(2)}) copy-start(bf16[64,256]{1,0:T(8,128)(2,1)} %param.12) | copy-start | bytes 98308
  5.3 13.8 %copy-start.3 = (f32[64]{0:T(128)S(1)}, f32[64]{0:T(128)}, u32[]{:S(2)}) copy-start(f32[64]{0:T(128)} %param.10) | copy-start | bytes 772
  7.0 24.7 %all-to-all-start = ((bf16[32,2,2048]{2,1,0:T(2,128)(2,1)}), bf16[32,2,2048]{2,1,0:T(2,128)(2,1)S(1)}, u32[]{:S(2)}, u32[]{:S(2)}) async-start(bf16[32,2,2048]{2,1,0:T(2,128)(2,1)} %reshape.101), calls=%async_computation | async-start | bytes 524288 | tf_op jit(solution)/shard_map/all_to_all | solution.py:107
  32.1 9.1 %copy-start = (bf16[1,64,2,64,64]{4,3,2,1,0:T(8,128)(2,1)S(1)}, bf16[1,64,2,64,64]{4,3,2,1,0:T(8,128)(2,1)}, u32[]{:S(2)}) copy-start(bf16[1,64,2,64,64]{4,3,2,1,0:T(8,128)(2,1)} %get-tuple-element.7) | copy-start | bytes 3145732
  33.6 7.5 %collective-permute-start.1 = (bf16[2,2,1,64,64]{4,3,1,0,2:T(8,128)(2,1)S(1)}, bf16[2,2,1,64,64]{4,3,1,0,2:T(8,128)(2,1)S(1)}, u32[]{:S(2)}, u32[]{:S(2)}) collective-permute-start(bf16[2,2,1,64,64]{4,3,1,0,2:T(8,128)(2,1)S(1)} %bitcast.85), channel_id=1, source_target_pairs={{1,0},{2,1},{3,2},{4,3},{5,4},{6,5},{7,6},{9,8},{10,9},{11,10},{12... | collective-permute-start | bytes 98312 | tf_op jit(solution)/shard_map/ppermute | solution.py:21
  36.0 5.9 %collective-permute-start = (bf16[2,2,1,64,64]{4,3,1,0,2:T(8,128)(2,1)S(1)}, bf16[2,2,1,64,64]{4,3,1,0,2:T(8,128)(2,1)S(1)}, u32[]{:S(2)}, u32[]{:S(2)}) collective-permute-start(bf16[2,2,1,64,64]{4,3,1,0,2:T(8,128)(2,1)S(1)} %bitcast.86), channel_id=1, source_target_pairs={{0,1},{1,2},{2,3},{3,4},{4,5},{5,6},{6,7},{8,9},{9,10},{10,11},{11... | collective-permute-start | bytes 98312 | tf_op jit(solution)/shard_map/ppermute | solution.py:19
  45.4 20.1 %all-to-all-start.1 = ((bf16[32,2,2048]{2,1,0:T(2,128)(2,1)}), bf16[32,2,2048]{2,1,0:T(2,128)(2,1)S(1)}, u32[]{:S(2)}, u32[]{:S(2)}) async-start(bf16[32,2,2048]{2,1,0:T(2,128)(2,1)} %reshape.103), calls=%async_computation.1 | async-start | bytes 524288 | tf_op jit(solution)/shard_map/all_to_all | solution.py:132
